TPU v7x, 32 devices: a whole 2x2x4 slice. The times are simulated.
32 devices in a mesh: sec: 16 (over z, y, core), row: 2 (over x).
Axes of the slice: x: 2, y: 2, z: 4, core: 2. Of those that a mesh axis runs over, the one named last changes fastest.
Arguments:
- section_images: bfloat16 [16, 256, 512], P('sec', 'row'), may hold values from -6 to 6
- displacement: float32 [2, 16, 2, 4], P(None, 'sec', 'row'), may hold values from -2 to 2
- fold_mask: int32 [2, 16, 2, 4], P(None, 'sec', 'row'), may hold values 0 or 1
Outputs:
- relaxed_field: float32 [2, 16, 2, 4], P(None, 'sec', 'row')
- mean_offsets: float32 [2, 16, 2, 4], P(None, 'sec', 'row')
All inputs are finite; a program needn't handle non-finite values. No bound on the sum of `fold_mask` on one device may be relied on, other than what follows from the above.
Results may differ from a plain program's by a relative error of at most 0.0003.
Values may be sent and summed in bfloat16 or wider, within the bound.
No kernel may reach another device: no remote copies, remote signals or barrier semaphores. Data moves between devices by JAX's collectives and lax.ppermute only.
A program may use at most 64 MiB of HBM per device.

v0:
```python
import math

import jax
import jax.numpy as jnp
import numpy as np
from jax import lax
from jax.experimental import pallas as pl
from jax.experimental.pallas import tpu as pltpu
from jax.sharding import PartitionSpec as P

PATCH = 128
HALF = PATCH // 2
ITERS = 3
HALO = 3
WINDOW = 8
EXTRA = 16

step_size = 0.5
stiffness = 0.2
epsilon = 1e-06
sharpness = 0.5 * PATCH
bf16 = jnp.bfloat16
f32 = jnp.float32


def split_table(table):
    table = np.asarray(table, np.float32)
    high = table.astype(bf16)
    low = (table - high.astype(np.float32)).astype(bf16)
    return high, low


def tables():
    n = PATCH
    index = np.arange(n)
    angle = 2.0 * np.pi / n * ((index[:, None] * index[None, :]) % n)
    cosine, sine = np.cos(angle), np.sin(angle)
    sign = 1.0 - 2.0 * (index % 2)

    basis = np.zeros((n, n))
    basis[:, :HALF] = cosine[:, :HALF]
    basis[:, HALF] = sign
    basis[:, HALF + 1 :] = -sine[:, 1:HALF]

    back = np.zeros((n, n))
    back[0] = 1.0
    back[1:HALF] = 2.0 * cosine[1:HALF]
    back[HALF] = sign
    back[HALF + 1 :] = -2.0 * sine[1:HALF]
    back /= n * n

    kernel = np.zeros((n, n))
    kernel[:HALF] = cosine[:HALF]
    kernel[HALF] = sign
    kernel[HALF + 1 :] = -sine[1:HALF]
    kernel /= n

    def doubled(table):
        pair = np.concatenate(split_table(table), axis=1)
        return np.concatenate([pair, pair], axis=0)

    down = np.concatenate(split_table(np.concatenate([cosine, -sine], axis=0)), axis=1)
    up = np.concatenate(split_table(np.concatenate([cosine, -sine], axis=1)), axis=0)
    return doubled(basis), down, up, doubled(kernel), doubled(back)


def split(values):
    high = values.astype(bf16)
    low = (values - high.astype(f32)).astype(bf16)
    return high, low


def dot(left, right):
    return jnp.dot(left, right, preferred_element_type=f32)


def fold(wide):
    return wide[:, :PATCH] + wide[:, PATCH:]


def lanes(shape):
    return lax.broadcasted_iota(jnp.int32, shape, len(shape) - 1)


def alternating(shape, dim):
    return (1 - 2 * (lax.broadcasted_iota(jnp.int32, shape, dim) % 2)).astype(f32)


def pack_kernel(cols, shift_ref, mask_ref, image_ref, out_ref):
    core = lax.rem(lax.axis_index("sec"), 2)
    width = cols * PATCH
    for part in range(2):
        half = lax.rem(core + part, 2)

        @pl.when(half == 0)
        def _(part=part):
            out_ref[part, :PATCH, :] = image_ref[0, :, :width]

        @pl.when(half == 1)
        def _(part=part):
            out_ref[part, :PATCH, :] = image_ref[0, :, width:]

        for col in range(cols):
            place = half * cols + col
            row = lax.broadcasted_iota(jnp.int32, (EXTRA, PATCH), 0)
            values = jnp.zeros((EXTRA, PATCH), f32)
            for dim in range(2):
                shift = jnp.full((EXTRA, PATCH), shift_ref[dim, 0, 0, place], f32)
                high = shift.astype(bf16).astype(f32)
                middle = (shift - high).astype(bf16).astype(f32)
                low = (shift - high) - middle
                mask = jnp.full((EXTRA, PATCH), mask_ref[dim, 0, 0, place].astype(f32), f32)
                for at, part_value in enumerate((high, middle, low)):
                    values = jnp.where(row == 3 * dim + at, part_value, values)
                values = jnp.where(row == 6 + dim, mask, values)
            out_ref[part, PATCH:, col * PATCH : (col + 1) * PATCH] = values.astype(bf16)


def forward_patch(pixels, basis_ref, down_ref):
    values = pixels.astype(f32)
    total = jnp.sum(jnp.sum(values, axis=0, keepdims=True), axis=1, keepdims=True)
    values = values - total * (1.0 / (PATCH * PATCH))
    rows = fold(dot(jnp.concatenate(split(values), axis=1), basis_ref[...]))
    energy_row = jnp.sum(rows * rows, axis=0, keepdims=True)
    nyquist_row = jnp.sum(rows * alternating(rows.shape, 0), axis=0, keepdims=True)
    pair = jnp.concatenate(split(rows), axis=1)
    both = fold(dot(down_ref[...], jnp.concatenate([pair, pair], axis=0)))
    first, second = both[:PATCH], both[PATCH:]
    lane = lanes((1, PATCH))
    sigma = jnp.where(lane > HALF, 1.0, -1.0) * jnp.where(lane % HALF == 0, 0.0, 1.0)
    real = first + sigma * pltpu.roll(second, HALF, 1)
    imag = second - sigma * pltpu.roll(first, HALF, 1)
    return real, imag, energy_row, nyquist_row


def pre_kernel(cols, *refs):
    (own, own_x, near_a, near_ax, near_b, near_bx, far, far_x, basis_ref, down_ref, up_ref) = refs[:11]
    (base_ref, stats_ref) = refs[11:13]
    real_ref, imag_ref, energy_ref, nyquist_ref = refs[13:]
    sec = lax.axis_index("sec")
    core = lax.rem(sec, 2)
    odd = lax.rem(sec // 2, 2)
    after_a = 5 - 4 * odd
    after_b = 1 + 4 * odd
    blocks = (
        (own.at[0], HALO + core),
        (own_x, HALO + 1 - core),
        (near_a.at[0], after_a + core),
        (near_ax, after_a + 1 - core),
        (near_b.at[0], after_b + core),
        (near_bx, after_b + 1 - core),
        (far.at[0], (WINDOW - 1) * (1 - core)),
        (far_x, (WINDOW - 1) * core),
    )
    for block, slot in blocks:
        for col in range(cols):
            where = slice(col * PATCH, (col + 1) * PATCH)
            real, imag, energy_row, nyquist_row = forward_patch(block[:PATCH, where], basis_ref, down_ref)
            real_ref[slot, col] = real
            imag_ref[slot, col] = imag
            energy_ref[col, pl.ds(slot, 1), :] = energy_row
            nyquist_ref[col, pl.ds(slot, 1), :] = nyquist_row
            small = block[PATCH:, where].astype(f32)
            for dim in range(2):
                shift = small[3 * dim : 3 * dim + 1] + small[3 * dim + 1 : 3 * dim + 2] + small[3 * dim + 2 : 3 * dim + 3]
                stats_ref[col, 5 + dim, pl.ds(slot, 1), :] = shift
                stats_ref[col, 7 + dim, pl.ds(slot, 1), :] = small[6 + dim : 7 + dim]
    lane = lanes((WINDOW, PATCH))
    weight = jnp.where(lane % HALF == 0, 1.0, 2.0)
    at_nyquist = jnp.where(lane == HALF, 1.0, 0.0)
    area = float(PATCH * PATCH)

    def spread(values):
        return jnp.broadcast_to(jnp.sum(values, axis=1, keepdims=True), (WINDOW, PATCH))

    for col in range(cols):
        energy, nyquist = energy_ref[col], nyquist_ref[col]
        corner = spread(nyquist * at_nyquist)
        corner_energy = corner * corner / area
        row_energy = spread(weight * (1.0 - at_nyquist) * nyquist * nyquist) / area
        col_energy = jnp.maximum(spread(energy * at_nyquist) / PATCH - corner_energy, 0.0)
        whole = spread(weight * energy) / PATCH
        stats_ref[col, 0] = jnp.maximum(whole - row_energy - col_energy - corner_energy, 0.0)
        stats_ref[col, 1] = row_energy
        stats_ref[col, 2] = col_energy
        stats_ref[col, 3] = corner_energy
        stats_ref[col, 4] = corner
    low_lane = lanes((1, PATCH)) <= HALF
    for pair in range(WINDOW - 1):
        for col in range(cols):
            sr, si = real_ref[pair, col], imag_ref[pair, col]
            nr, ni = real_ref[pair + 1, col], imag_ref[pair + 1, col]
            same = sr * nr + si * ni
            cross = si * nr - sr * ni
            top = jnp.concatenate(split(jnp.where(low_lane, same, cross)), axis=1)
            bottom = jnp.concatenate(split(jnp.where(low_lane, cross, -same)), axis=1)
            wide = fold(dot(up_ref[...], jnp.concatenate([top, bottom], axis=0)))
            base = wide[:PATCH] + wide[PATCH:]
            base_ref[col, pair] = jnp.concatenate(split(base), axis=1)


def cos_sin_turns(turns):
    rest = turns - jnp.round(turns)
    z = rest * math.pi
    zz = z * z
    sine = jnp.full_like(z, 1.0 / 6227020800.0)
    for factor in (-1.0 / 39916800.0, 1.0 / 362880.0, -1.0 / 5040.0, 1.0 / 120.0, -1.0 / 6.0, 1.0):
        sine = sine * zz + factor
    sine = sine * z
    cosine = jnp.full_like(z, 1.0 / 479001600.0)
    for factor in (-1.0 / 3628800.0, 1.0 / 40320.0, -1.0 / 720.0, 1.0 / 24.0, -0.5, 1.0):
        cosine = cosine * zz + factor
    return 1.0 - 2.0 * sine * sine, 2.0 * sine * cosine


def next_section(values):
    return pltpu.roll(values, WINDOW - 1, 0)


def previous_section(values):
    return pltpu.roll(values, 1, 0)


def column(message, lane):
    return jnp.broadcast_to(message[:, lane : lane + 1], (WINDOW, PATCH))


def pack_columns(values):
    lane = lanes((WINDOW, PATCH))
    packed = jnp.zeros((WINDOW, PATCH), f32)
    for at, value in enumerate(values):
        packed = jnp.where(lane == at, value, packed)
    return packed


def smoothed(updated, vertical, beside, core, cols):
    result = []
    for dim in range(2):
        current = []
        for col in range(cols):
            if col > 0:
                left = updated[dim][col - 1]
            else:
                left = jnp.where(core == 1, beside[dim][cols - 1], 0.0)
            if col < cols - 1:
                right = updated[dim][col + 1]
            else:
                right = jnp.where(core == 0, beside[dim][0], 0.0)
            own = updated[dim][col]
            current.append(own + stiffness * (left + right + vertical[dim][col] - 4.0 * own))
        result.append(current)
    return result


def unpack(message, cols, start=0):
    return [[column(message, start + dim * cols + col) for col in range(cols)] for dim in range(2)]


def add(left, right):
    return [[a + b for a, b in zip(x, y)] for x, y in zip(left, right)]


def iteration_kernel(cols, first, last, starts, n_vertical, *refs):
    base_ref, stats_ref, kernel_ref, back_ref = refs[:4]
    refs = refs[4:]
    core = lax.rem(lax.axis_index("sec"), 2)
    if starts:
        field = [[stats_ref[col, 5 + dim] for col in range(cols)] for dim in range(2)]
    else:
        own_message, beside_message = refs[:2]
        vertical = unpack(refs[2][...], cols)
        for extra in refs[3 : 2 + n_vertical]:
            vertical = add(vertical, unpack(extra[...], cols))
        refs = refs[2 + n_vertical :]
        field = smoothed(unpack(own_message[...], cols), vertical, unpack(beside_message[...], cols), core, cols)
    out_ref, total_ref, moment_ref, edge_ref = refs
    lane = lanes((WINDOW, PATCH))
    frequency = (lane % HALF).astype(f32) * (1.0 / PATCH)
    high_lane = lane >= HALF
    nyquist_lane = lane == HALF
    zero_lane = lane % HALF == 0
    rows, turn_cos, turn_sin, ripple = [], [], [], []
    for col in range(cols):
        dy, dx = field[0][col], field[1][col]
        cos_y, sin_y = cos_sin_turns(dy * 0.5)
        cos_x, sin_x = cos_sin_turns(dx * 0.5)
        cos_both = cos_y * cos_x - sin_y * sin_x
        energy = (
            stats_ref[col, 0]
            + cos_y * cos_y * stats_ref[col, 1]
            + cos_x * cos_x * stats_ref[col, 2]
            + cos_both * cos_both * stats_ref[col, 3]
        )
        scale = (sharpness / math.log(2.0)) / jnp.sqrt(energy * next_section(energy) + epsilon)
        gamma_y = cos_y * next_section(cos_y)
        gamma_x = cos_x * next_section(cos_x)
        gamma = cos_both * next_section(cos_both)
        corner = stats_ref[col, 4] * next_section(stats_ref[col, 4]) * (1.0 / (PATCH * PATCH))
        ripple.append((gamma - gamma_y * gamma_x) * corner * scale)
        cosine, sine = cos_sin_turns((dy - next_section(dy)) * frequency)
        harmonics = jnp.where(high_lane, sine, cosine) * 2.0
        harmonics = jnp.where(lane == 0, 1.0, jnp.where(nyquist_lane, gamma_y, harmonics))
        rows.append(fold(dot(jnp.concatenate(split(harmonics), axis=1), kernel_ref[...])))
        cosine, sine = cos_sin_turns((dx - next_section(dx)) * frequency)
        turn_cos.append(jnp.where(nyquist_lane, gamma_x, cosine) * scale)
        turn_sin.append(jnp.where(zero_lane, 0.0, jnp.where(high_lane, -sine, sine)) * scale)
    checker = alternating((WINDOW, PATCH), 0) * alternating((WINDOW, PATCH), 1)
    blocks = PATCH // WINDOW
    block_lag = [WINDOW * k - (PATCH if k >= blocks // 2 else 0) for k in range(blocks)]
    row_in_block = lax.broadcasted_iota(jnp.int32, (WINDOW, PATCH), 0).astype(f32)
    for col in range(cols):
        total_ref[col] = jnp.ones((WINDOW, PATCH), f32)
        moment_ref[col] = jnp.zeros((WINDOW, PATCH), f32)
        edge_ref[col] = jnp.zeros((WINDOW, PATCH), f32)
    for pair in range(first, last):
        for col in range(cols):
            row = slice(pair, pair + 1)
            shifter = pltpu.roll(jnp.broadcast_to(rows[col][row], (PATCH, PATCH)), 0, 1, stride=1, stride_axis=0)
            base = base_ref[col, pair]
            moved = fold(dot(jnp.concatenate(split(shifter), axis=1), jnp.concatenate([base, base], axis=0)))
            moved = moved * turn_cos[col][row] + pltpu.roll(moved, HALF, 1) * turn_sin[col][row]
            scores = fold(dot(jnp.concatenate(split(moved), axis=1), back_ref[...]))
            scores = scores.reshape(blocks, WINDOW, PATCH) + (ripple[col][row] * checker)[None]
            weights = jnp.exp2(scores)
            total = weights[0]
            moment = weights[0] * float(block_lag[0])
            for k in range(1, blocks):
                total = total + weights[k]
                moment = moment + weights[k] * float(block_lag[k])
            moment = moment + row_in_block * total
            total_ref[col, row, :] = jnp.sum(total, axis=0, keepdims=True)
            moment_ref[col, row, :] = jnp.sum(moment, axis=0, keepdims=True)
            edge_ref[col, row, :] = weights[blocks // 2, 0:1]
    sec_total = lax.axis_size("sec")
    section = lax.broadcasted_iota(jnp.int32, (WINDOW, PATCH), 0) + (lax.axis_index("sec") - core - HALO)
    lag = jnp.where(high_lane, lane - PATCH, lane).astype(f32)

    def spread(values):
        return jnp.broadcast_to(jnp.sum(values, axis=1, keepdims=True), (WINDOW, PATCH))

    updated = [[None] * cols for _ in range(2)]
    averaged = [[None] * cols for _ in range(2)]
    for col in range(cols):
        total = total_ref[col]
        inverse = 1.0 / spread(total)
        offsets = (spread(moment_ref[col]) * inverse, spread(total * lag) * inverse)
        edges = (spread(edge_ref[col]) * inverse, spread(jnp.where(nyquist_lane, total, 0.0)) * inverse)
        lower = stats_ref[col, 7] * (section > 0).astype(f32)
        upper = stats_ref[col, 8] * (section < sec_total - 1).astype(f32)
        for dim in range(2):
            reverse = previous_section(-(offsets[dim] + float(PATCH) * edges[dim]))
            mean = (lower * reverse + upper * offsets[dim]) / jnp.maximum(lower + upper, 1.0)
            averaged[dim][col] = mean
            updated[dim][col] = field[dim][col] + step_size * mean
    flat = [updated[dim][col] for dim in range(2) for col in range(cols)]
    flat += [averaged[dim][col] for dim in range(2) for col in range(cols)]
    out_ref[...] = pack_columns(flat)


def final_kernel(cols, n_vertical, *refs):
    own, beside = refs[0][...], refs[1][...]
    vertical = unpack(refs[2][...], cols)
    vertical_beside = unpack(refs[3][...], cols)
    for k in range(1, n_vertical):
        vertical = add(vertical, unpack(refs[2 + 2 * k][...], cols))
        vertical_beside = add(vertical_beside, unpack(refs[3 + 2 * k][...], cols))
    field_ref, mean_ref = refs[2 + 2 * n_vertical :]
    core = lax.rem(lax.axis_index("sec"), 2)
    mine, other = unpack(own, cols), unpack(beside, cols)
    here = smoothed(mine, vertical, other, core, cols)
    there = smoothed(other, vertical_beside, mine, 1 - core, cols)
    mean_here, mean_there = unpack(own, cols, 2 * cols), unpack(beside, cols, 2 * cols)
    lane = lanes((1, PATCH))

    def pick(values):
        return jnp.where(core == 0, values[HALO : HALO + 1], values[HALO + 1 : HALO + 2])

    for out, a, b in ((field_ref, here, there), (mean_ref, mean_here, mean_there)):
        for dim in range(2):
            row = jnp.zeros((1, PATCH), f32)
            for col in range(cols):
                first = pick(jnp.where(core == 0, a[dim][col], b[dim][col]))
                second = pick(jnp.where(core == 0, b[dim][col], a[dim][col]))
                row = jnp.where(lane == col, first, row)
                row = jnp.where(lane == cols + col, second, row)
            out[dim, 0] = row[:, : 2 * cols]


def vmem():
    return pl.BlockSpec(memory_space=pltpu.VMEM)


def smem():
    return pl.BlockSpec(memory_space=pltpu.SMEM)


def swap(pairs):
    return [(a, b) for a, b in pairs] + [(b, a) for a, b in pairs]


def per_device(section_images, displacement, fold_mask):
    n_sec, n_row = lax.axis_size("sec"), lax.axis_size("row")
    patch_cols = displacement.shape[-1]
    assert patch_cols % 2 == 0 and n_sec % 2 == 0
    assert section_images.shape[:2] == (1, PATCH)
    cols = patch_cols // 2
    chips = n_sec // 2
    constants = [jnp.asarray(t) for t in tables()]
    basis, down, up, kernel, back = constants

    def sections(pairs):
        return [(2 * a + c, 2 * b + c) for a, b in pairs for c in range(2)]

    swap_a = sections(swap([(j, j + 1) for j in range(0, chips - 1, 2)]))
    swap_b = sections(swap([(j, j + 1) for j in range(1, chips - 1, 2)]))
    far = [(2 * j + 1, 2 * j + 5) for j in range(chips - 2)] + [(2 * j + 4, 2 * j) for j in range(chips - 2)]
    cores = swap([(2 * j, 2 * j + 1) for j in range(chips)])

    def between_cores(x):
        return lax.ppermute(x, "sec", cores)

    payload = pl.pallas_call(
        lambda *refs: pack_kernel(cols, *refs),
        out_shape=jax.ShapeDtypeStruct((2, PATCH + EXTRA, cols * PATCH), bf16),
        in_specs=[smem(), smem(), vmem()],
        out_specs=vmem(),
        name="pack",
    )(displacement, fold_mask, section_images)
    received = [payload] + [lax.ppermute(payload, "sec", perm) for perm in (swap_a, swap_b, far)]
    operands = []
    for block in received:
        operands += [block, between_cores(block[1])]
    base, stats = pl.pallas_call(
        lambda *refs: pre_kernel(cols, *refs),
        out_shape=(
            jax.ShapeDtypeStruct((cols, WINDOW - 1, PATCH, 2 * PATCH), bf16),
            jax.ShapeDtypeStruct((cols, 9, WINDOW, PATCH), f32),
        ),
        in_specs=[vmem()] * 11,
        out_specs=(vmem(), vmem()),
        scratch_shapes=[
            pltpu.VMEM((WINDOW, cols, PATCH, PATCH), f32),
            pltpu.VMEM((WINDOW, cols, PATCH, PATCH), f32),
            pltpu.VMEM((cols, WINDOW, PATCH), f32),
            pltpu.VMEM((cols, WINDOW, PATCH), f32),
        ],
        name="pre",
    )(*operands, basis, down, up)

    row_perms = [swap([(r, r + 1) for r in range(0, n_row - 1, 2)])]
    if n_row > 2:
        row_perms.append(swap([(r, r + 1) for r in range(1, n_row - 1, 2)]))

    def diagonal(x, rows):
        pairs = [(s * n_row + a, t * n_row + b) for s, t in cores for a, b in rows]
        return lax.ppermute(x, ("sec", "row"), pairs)

    messages = []
    for step in range(ITERS):
        out = pl.pallas_call(
            lambda *refs, step=step: iteration_kernel(cols, step, WINDOW - 1 - step, step == 0, len(row_perms), *refs),
            out_shape=jax.ShapeDtypeStruct((WINDOW, PATCH), f32),
            in_specs=[vmem()] * (4 + len(messages)),
            out_specs=vmem(),
            scratch_shapes=[pltpu.VMEM((cols, WINDOW, PATCH), f32)] * 3,
            name="iteration",
        )(base, stats, kernel, back, *messages)
        if step < ITERS - 1:
            messages = [out, between_cores(out)] + [lax.ppermute(out, "row", perm) for perm in row_perms]
    messages = [out, between_cores(out)]
    for perm in row_perms:
        messages += [lax.ppermute(out, "row", perm), diagonal(out, perm)]
    shape = jax.ShapeDtypeStruct(displacement.shape, f32)
    return pl.pallas_call(
        lambda *refs: final_kernel(cols, len(row_perms), *refs),
        out_shape=(shape, shape),
        in_specs=[vmem()] * len(messages),
        out_specs=(vmem(), vmem()),
        name="final",
    )(*messages)


def solution(mesh):
    in_specs = (P("sec", "row", None), P(None, "sec", "row", None), P(None, "sec", "row", None))
    out_specs = (P(None, "sec", "row", None), P(None, "sec", "row", None))
    return jax.shard_map(
        per_device, mesh=mesh, in_specs=in_specs, out_specs=out_specs, check_vma=False
    )
```

profile of v0, /device:TPU:17, one launch (start us, length us, event | category | flops | bytes accessed | tf_op | source)
XLA Modules:
  0.0 50.9 jit_solution(6401472691038180738)
XLA Ops:
  0.6 1.7 %pack.1.refs_0_ = bf16[2,144,256]{2,1,0:T(8,128)(2,1)} custom-call(f32[2,1,1,4]{3,2,1,0:T(1,128)} %refs_0_.1, s32[2,1,1,4]{3,2,1,0:T(1,128)} %refs_1_.1, bf16[1,128,512]{2,1,0:T(8,128)(2,1)} %refs_2_.4), custom_call_target="tpu_custom_call" | custom-call | tf_op jit(solution)/shard_map/pack/pallas_call | solution.py:422
  2.3 3.2 %collective-permute-start.5 = (bf16[2,144,256]{2,1,0:T(8,128)(2,1)}, bf16[2,144,256]{2,1,0:T(8,128)(2,1)S(1)}, u32[]{:S(2)}, u32[]{:S(2)}) collective-permute-start(bf16[2,144,256]{2,1,0:T(8,128)(2,1)} %pack.1.refs_0_), channel_id=1, source_target_pairs={{2,10},{6,14},{10,18},{14,22},{18,26},{22,30},{8,0},{12,4},{16,8},... | collective-permute-start | bytes 442376 | tf_op jit(solution)/shard_map/ppermute | solution.py:429
  5.5 3.0 %collective-permute-start.3 = (bf16[2,144,256]{2,1,0:T(8,128)(2,1)}, bf16[2,144,256]{2,1,0:T(8,128)(2,1)S(1)}, u32[]{:S(2)}, u32[]{:S(2)}) collective-permute-start(bf16[2,144,256]{2,1,0:T(8,128)(2,1)} %pack.1.refs_0_), channel_id=1, source_target_pairs={{4,8},{6,10},{12,16},{14,18},{20,24},{22,26},{8,4},{10,6},{16,12},... | collective-permute-start | bytes 442376 | tf_op jit(solution)/shard_map/ppermute | solution.py:429
  8.5 0.2 collective-permute-start.1
  8.7 0.9 %slice_bitcast_fusion.3 = bf16[144,256]{1,0:T(8,128)(2,1)S(1)} fusion(bf16[2,144,256]{2,1,0:T(8,128)(2,1)} %pack.1.refs_0_), kind=kLoop, calls=%fused_computation.3 | loop fusion | bytes 147456 | tf_op jit(solution)/shard_map/squeeze | solution.py:432
  9.6 1.6 %collective-permute-start = (bf16[144,256]{1,0:T(8,128)(2,1)S(1)}, bf16[144,256]{1,0:T(8,128)(2,1)S(1)}, u32[]{:S(2)}, u32[]{:S(2)}) collective-permute-start(bf16[144,256]{1,0:T(8,128)(2,1)S(1)} %slice_bitcast_fusion.3), channel_id=1, source_target_pairs={{0,2},{4,6},{8,10},{12,14},{16,18},{20,22},{24,26},{28,30},{2,0},{... | collective-permute-start | bytes 221192 | tf_op jit(solution)/shard_map/ppermute | solution.py:420
  11.3 0.0 collective-permute-done.5.refs_6_
  11.3 0.0 copy-start
  11.3 0.1 collective-permute-start.6
  11.4 2.7 %collective-permute-done.3.refs_4_ = bf16[2,144,256]{2,1,0:T(8,128)(2,1)S(1)} collective-permute-done((bf16[2,144,256]{2,1,0:T(8,128)(2,1)}, bf16[2,144,256]{2,1,0:T(8,128)(2,1)S(1)}, u32[]{:S(2)}, u32[]{:S(2)}) %collective-permute-start.3) | collective-permute-done | bytes 147488 | tf_op jit(solution)/shard_map/ppermute | solution.py:429
  14.1 0.0 copy-start.1
  14.1 0.8 %collective-permute-start.4 = (bf16[144,256]{1,0:T(8,128)(2,1)S(1)}, bf16[144,256]{1,0:T(8,128)(2,1)S(1)}, u32[]{:S(2)}, u32[]{:S(2)}) collective-permute-start(bf16[144,256]{1,0:T(8,128)(2,1)S(1)} %slice_bitcast_fusion.1), channel_id=1, source_target_pairs={{0,2},{4,6},{8,10},{12,14},{16,18},{20,22},{24,26},{28,30},{2,0},{... | collective-permute-start | bytes 221192 | tf_op jit(solution)/shard_map/ppermute | solution.py:420
  14.9 2.5 %collective-permute-done.1.refs_2_ = bf16[2,144,256]{2,1,0:T(8,128)(2,1)S(1)} collective-permute-done((bf16[2,144,256]{2,1,0:T(8,128)(2,1)}, bf16[2,144,256]{2,1,0:T(8,128)(2,1)S(1)}, u32[]{:S(2)}, u32[]{:S(2)}) %collective-permute-start.1) | collective-permute-done | bytes 147488 | tf_op jit(solution)/shard_map/ppermute | solution.py:429
  17.5 0.0 copy-start.2
  17.5 0.0 copy-done
  17.5 0.5 %collective-permute-start.2 = (bf16[144,256]{1,0:T(8,128)(2,1)S(1)}, bf16[144,256]{1,0:T(8,128)(2,1)S(1)}, u32[]{:S(2)}, u32[]{:S(2)}) collective-permute-start(bf16[144,256]{1,0:T(8,128)(2,1)S(1)} %slice_bitcast_fusion.2), channel_id=1, source_target_pairs={{0,2},{4,6},{8,10},{12,14},{16,18},{20,22},{24,26},{28,30},{2,0},{... | collective-permute-start | bytes 221192 | tf_op jit(solution)/shard_map/ppermute | solution.py:420
  18.0 0.0 collective-permute-done.refs_1_
  18.0 0.0 copy-start.3
  18.0 0.0 collective-permute-done.6.refs_7_
  18.0 0.0 copy-start.4
  18.0 0.0 collective-permute-done.4.refs_5_
  18.0 0.0 copy-start.5
  18.0 0.9 %collective-permute-done.2.refs_3_ = bf16[144,256]{1,0:T(8,128)(2,1)S(1)} collective-permute-done((bf16[144,256]{1,0:T(8,128)(2,1)S(1)}, bf16[144,256]{1,0:T(8,128)(2,1)S(1)}, u32[]{:S(2)}, u32[]{:S(2)}) %collective-permute-start.2) | collective-permute-done | bytes 73760 | tf_op jit(solution)/shard_map/ppermute | solution.py:420
  18.9 0.0 copy-done.1
  18.9 0.0 copy-done.2
  18.9 0.0 copy-done.3
  18.9 0.0 copy-done.4
  18.9 0.0 copy-done.5
  18.9 0.0 copy-start.6
  18.9 0.6 %copy-done.6 = bf16[144,256]{1,0:T(8,128)(2,1)} copy-done((bf16[144,256]{1,0:T(8,128)(2,1)}, bf16[144,256]{1,0:T(8,128)(2,1)S(1)}, u32[]{:S(2)}) %copy-start.6) | copy-done | bytes 73752
  19.6 5.5 %pre.1 = (bf16[2,7,128,256]{3,2,1,0:T(8,128)(2,1)}, f32[2,9,8,128]{3,2,1,0:T(8,128)}) custom-call(bf16[2,144,256]{2,1,0:T(8,128)(2,1)} %pack.1.refs_0_, bf16[144,256]{1,0:T(8,128)(2,1)} %copy-done.3, bf16[2,144,256]{2,1,0:T(8,128)(2,1)} %copy-done.2, bf16[144,256]{1,0:T(8,128)(2,1)} %copy-done.6, bf16[2,144,256]{2,1,0:T(8,128)(2,1)} %copy-done.1, ...), custom_call_target="tpu_custom_call" | custom-call | tf_op jit(solution)/shard_map/pre/pallas_call | solution.py:433
  25.1 3.1 %iteration.3.refs_4_ = f32[8,128]{1,0:T(8,128)} custom-call(bf16[2,7,128,256]{3,2,1,0:T(8,128)(2,1)} %get-tuple-element.4.refs_0_, f32[2,9,8,128]{3,2,1,0:T(8,128)} %get-tuple-element.5.refs_1_, bf16[256,256]{1,0:T(8,128)(2,1)} %constant.13.clone.refs_2_, bf16[256,256]{1,0:T(8,128)(2,1)} %constant.14.clone.refs_3_), custom_call_target="tpu_custom_call" | custom-call | tf_op jit(solution)/shard_map/iteration/pallas_call | solution.py:460
  28.3 1.2 %collective-permute-start.8 = (f32[8,128]{1,0:T(8,128)}, f32[8,128]{1,0:T(8,128)S(1)}, u32[]{:S(2)}, u32[]{:S(2)}) collective-permute-start(f32[8,128]{1,0:T(8,128)} %iteration.3.refs_4_), channel_id=1, source_target_pairs={{0,1},{1,0},{2,3},{3,2},{4,5},{5,4},{6,7},{7,6},{8,9},{9,8},{10,11... | collective-permute-start | bytes 12296 | tf_op jit(solution)/shard_map/ppermute | solution.py:469
  29.5 0.6 %collective-permute-start.7 = (f32[8,128]{1,0:T(8,128)}, f32[8,128]{1,0:T(8,128)S(1)}, u32[]{:S(2)}, u32[]{:S(2)}) collective-permute-start(f32[8,128]{1,0:T(8,128)} %iteration.3.refs_4_), channel_id=1, source_target_pairs={{0,2},{4,6},{8,10},{12,14},{16,18},{20,22},{24,26},{28,30},{2,0},{... | collective-permute-start | bytes 12296 | tf_op jit(solution)/shard_map/ppermute | solution.py:420
  30.1 0.8 %collective-permute-done.8.refs_6_ = f32[8,128]{1,0:T(8,128)S(1)} collective-permute-done((f32[8,128]{1,0:T(8,128)}, f32[8,128]{1,0:T(8,128)S(1)}, u32[]{:S(2)}, u32[]{:S(2)}) %collective-permute-start.8) | collective-permute-done | bytes 4128 | tf_op jit(solution)/shard_map/ppermute | solution.py:469
  30.9 0.0 copy-start.9
  30.9 0.2 collective-permute-done.7.refs_5_
  31.1 0.4 copy-done.9
  31.5 0.0 copy-start.10
  31.5 0.6 %copy-done.10 = f32[8,128]{1,0:T(8,128)} copy-done((f32[8,128]{1,0:T(8,128)}, f32[8,128]{1,0:T(8,128)S(1)}, u32[]{:S(2)}) %copy-start.10) | copy-done | bytes 4120
  32.1 3.1 %iteration.4.refs_4_ = f32[8,128]{1,0:T(8,128)} custom-call(bf16[2,7,128,256]{3,2,1,0:T(8,128)(2,1)} %get-tuple-element.4.refs_0_, f32[2,9,8,128]{3,2,1,0:T(8,128)} %get-tuple-element.5.refs_1_, bf16[256,256]{1,0:T(8,128)(2,1)} %constant.13.clone.refs_2_, bf16[256,256]{1,0:T(8,128)(2,1)} %constant.14.clone.refs_3_, f32[8,128]{1,0:T(8,128)} %iteration.3.refs_4_, ...), custom_call_target="tpu_custom_call" | custom-call | tf_op jit(solution)/shard_map/iteration/pallas_call | solution.py:460
  35.2 1.2 %collective-permute-start.10 = (f32[8,128]{1,0:T(8,128)}, f32[8,128]{1,0:T(8,128)S(1)}, u32[]{:S(2)}, u32[]{:S(2)}) collective-permute-start(f32[8,128]{1,0:T(8,128)} %iteration.4.refs_4_), channel_id=1, source_target_pairs={{0,1},{1,0},{2,3},{3,2},{4,5},{5,4},{6,7},{7,6},{8,9},{9,8},{10,11... | collective-permute-start | bytes 12296 | tf_op jit(solution)/shard_map/ppermute | solution.py:469
  36.4 1.8 %collective-permute-start.9 = (f32[8,128]{1,0:T(8,128)}, f32[8,128]{1,0:T(8,128)S(1)}, u32[]{:S(2)}, u32[]{:S(2)}) collective-permute-start(f32[8,128]{1,0:T(8,128)} %iteration.4.refs_4_), channel_id=1, source_target_pairs={{0,2},{4,6},{8,10},{12,14},{16,18},{20,22},{24,26},{28,30},{2,0},{... | collective-permute-start | bytes 12296 | tf_op jit(solution)/shard_map/ppermute | solution.py:420
  38.2 0.0 collective-permute-done.10.refs_6_
  38.2 0.0 copy-start.7
  38.2 1.0 %collective-permute-done.9.refs_5_ = f32[8,128]{1,0:T(8,128)S(1)} collective-permute-done((f32[8,128]{1,0:T(8,128)}, f32[8,128]{1,0:T(8,128)S(1)}, u32[]{:S(2)}, u32[]{:S(2)}) %collective-permute-start.9) | collective-permute-done | bytes 4128 | tf_op jit(solution)/shard_map/ppermute | solution.py:420
  39.2 0.0 copy-done.7
  39.2 0.0 copy-start.8
  39.2 0.6 %copy-done.8 = f32[8,128]{1,0:T(8,128)} copy-done((f32[8,128]{1,0:T(8,128)}, f32[8,128]{1,0:T(8,128)S(1)}, u32[]{:S(2)}) %copy-start.8) | copy-done | bytes 4120
  39.8 2.9 %iteration.5.refs_0_ = f32[8,128]{1,0:T(8,128)} custom-call(bf16[2,7,128,256]{3,2,1,0:T(8,128)(2,1)} %get-tuple-element.4.refs_0_, f32[2,9,8,128]{3,2,1,0:T(8,128)} %get-tuple-element.5.refs_1_, bf16[256,256]{1,0:T(8,128)(2,1)} %constant.13.clone.refs_2_, bf16[256,256]{1,0:T(8,128)(2,1)} %constant.14.clone.refs_3_, f32[8,128]{1,0:T(8,128)} %iteration.4.refs_4_, ...), custom_call_target="tpu_custom_call" | custom-call | tf_op jit(solution)/shard_map/iteration/pallas_call | solution.py:460
  42.7 3.0 %collective-permute-start.13 = (f32[8,128]{1,0:T(8,128)}, f32[8,128]{1,0:T(8,128)S(1)}, u32[]{:S(2)}, u32[]{:S(2)}) collective-permute-start(f32[8,128]{1,0:T(8,128)} %iteration.5.refs_0_), channel_id=1, source_target_pairs={{0,3},{1,2},{4,7},{5,6},{8,11},{9,10},{12,15},{13,14},{16,19},{17,... | collective-permute-start | bytes 12296 | tf_op jit(solution)/shard_map/ppermute | solution.py:456
  45.7 0.2 collective-permute-start.12
  45.9 0.1 collective-permute-start.11
  46.1 1.3 %collective-permute-done.13.refs_3_ = f32[8,128]{1,0:T(8,128)S(1)} collective-permute-done((f32[8,128]{1,0:T(8,128)}, f32[8,128]{1,0:T(8,128)S(1)}, u32[]{:S(2)}, u32[]{:S(2)}) %collective-permute-start.13) | collective-permute-done | bytes 4128 | tf_op jit(solution)/shard_map/ppermute | solution.py:456
  47.4 0.0 copy-start.11
  47.4 0.9 %collective-permute-done.12.refs_2_ = f32[8,128]{1,0:T(8,128)S(1)} collective-permute-done((f32[8,128]{1,0:T(8,128)}, f32[8,128]{1,0:T(8,128)S(1)}, u32[]{:S(2)}, u32[]{:S(2)}) %collective-permute-start.12) | collective-permute-done | bytes 4128 | tf_op jit(solution)/shard_map/ppermute | solution.py:472
  48.3 0.0 copy-start.12
  48.3 0.0 collective-permute-done.11.refs_1_
  48.3 0.0 copy-done.11
  48.3 0.6 %copy-done.12 = f32[8,128]{1,0:T(8,128)} copy-done((f32[8,128]{1,0:T(8,128)}, f32[8,128]{1,0:T(8,128)S(1)}, u32[]{:S(2)}) %copy-start.12) | copy-done | bytes 4120
  48.9 0.0 copy-start.13
  48.9 0.6 %copy-done.13 = f32[8,128]{1,0:T(8,128)} copy-done((f32[8,128]{1,0:T(8,128)}, f32[8,128]{1,0:T(8,128)S(1)}, u32[]{:S(2)}) %copy-start.13) | copy-done | bytes 4120
  49.5 1.4 %final.1 = (f32[2,1,1,4]{3,2,1,0:T(1,128)}, f32[2,1,1,4]{3,2,1,0:T(1,128)}) custom-call(f32[8,128]{1,0:T(8,128)} %iteration.5.refs_0_, f32[8,128]{1,0:T(8,128)} %copy-done.13, f32[8,128]{1,0:T(8,128)} %copy-done.12, f32[8,128]{1,0:T(8,128)} %copy-done.11), custom_call_target="tpu_custom_call" | custom-call | tf_op jit(solution)/shard_map/final/pallas_call | solution.py:474
  (3 shorter events, 0.0 us)
Async XLA Ops:
  2.3 9.0 %collective-permute-start.5 = (bf16[2,144,256]{2,1,0:T(8,128)(2,1)}, bf16[2,144,256]{2,1,0:T(8,128)(2,1)S(1)}, u32[]{:S(2)}, u32[]{:S(2)}) collective-permute-start(bf16[2,144,256]{2,1,0:T(8,128)(2,1)} %pack.1.refs_0_), channel_id=1, source_target_pairs={{2,10},{6,14},{10,18},{14,22},{18,26},{22,30},{8,0},{12,4},{16,8},... | collective-permute-start | bytes 442376 | tf_op jit(solution)/shard_map/ppermute | solution.py:429
  5.5 8.6 %collective-permute-start.3 = (bf16[2,144,256]{2,1,0:T(8,128)(2,1)}, bf16[2,144,256]{2,1,0:T(8,128)(2,1)S(1)}, u32[]{:S(2)}, u32[]{:S(2)}) collective-permute-start(bf16[2,144,256]{2,1,0:T(8,128)(2,1)} %pack.1.refs_0_), channel_id=1, source_target_pairs={{4,8},{6,10},{12,16},{14,18},{20,24},{22,26},{8,4},{10,6},{16,12},... | collective-permute-start | bytes 442376 | tf_op jit(solution)/shard_map/ppermute | solution.py:429
  8.5 8.9 %collective-permute-start.1 = (bf16[2,144,256]{2,1,0:T(8,128)(2,1)}, bf16[2,144,256]{2,1,0:T(8,128)(2,1)S(1)}, u32[]{:S(2)}, u32[]{:S(2)}) collective-permute-start(bf16[2,144,256]{2,1,0:T(8,128)(2,1)} %pack.1.refs_0_), channel_id=1, source_target_pairs={{0,4},{2,6},{8,12},{10,14},{16,20},{18,22},{24,28},{26,30},{4,0},{... | collective-permute-start | bytes 442376 | tf_op jit(solution)/shard_map/ppermute | solution.py:429
  9.6 8.4 %collective-permute-start = (bf16[144,256]{1,0:T(8,128)(2,1)S(1)}, bf16[144,256]{1,0:T(8,128)(2,1)S(1)}, u32[]{:S(2)}, u32[]{:S(2)}) collective-permute-start(bf16[144,256]{1,0:T(8,128)(2,1)S(1)} %slice_bitcast_fusion.3), channel_id=1, source_target_pairs={{0,2},{4,6},{8,10},{12,14},{16,18},{20,22},{24,26},{28,30},{2,0},{... | collective-permute-start | bytes 221192 | tf_op jit(solution)/shard_map/ppermute | solution.py:420
  11.3 6.2 %copy-start = (bf16[2,144,256]{2,1,0:T(8,128)(2,1)}, bf16[2,144,256]{2,1,0:T(8,128)(2,1)S(1)}, u32[]{:S(2)}) copy-start(bf16[2,144,256]{2,1,0:T(8,128)(2,1)S(1)} %collective-permute-done.5.refs_6_) | copy-start | bytes 442372
  11.3 6.7 %collective-permute-start.6 = (bf16[144,256]{1,0:T(8,128)(2,1)S(1)}, bf16[144,256]{1,0:T(8,128)(2,1)S(1)}, u32[]{:S(2)}, u32[]{:S(2)}) collective-permute-start(bf16[144,256]{1,0:T(8,128)(2,1)S(1)} %slice_bitcast_fusion), channel_id=1, source_target_pairs={{0,2},{4,6},{8,10},{12,14},{16,18},{20,22},{24,26},{28,30},{2,0},{... | collective-permute-start | bytes 221192 | tf_op jit(solution)/shard_map/ppermute | solution.py:420
  14.1 4.8 %copy-start.1 = (bf16[2,144,256]{2,1,0:T(8,128)(2,1)}, bf16[2,144,256]{2,1,0:T(8,128)(2,1)S(1)}, u32[]{:S(2)}) copy-start(bf16[2,144,256]{2,1,0:T(8,128)(2,1)S(1)} %collective-permute-done.3.refs_4_) | copy-start | bytes 442372
  14.1 3.9 %collective-permute-start.4 = (bf16[144,256]{1,0:T(8,128)(2,1)S(1)}, bf16[144,256]{1,0:T(8,128)(2,1)S(1)}, u32[]{:S(2)}, u32[]{:S(2)}) collective-permute-start(bf16[144,256]{1,0:T(8,128)(2,1)S(1)} %slice_bitcast_fusion.1), channel_id=1, source_target_pairs={{0,2},{4,6},{8,10},{12,14},{16,18},{20,22},{24,26},{28,30},{2,0},{... | collective-permute-start | bytes 221192 | tf_op jit(solution)/shard_map/ppermute | solution.py:420
  17.5 1.5 %copy-start.2 = (bf16[2,144,256]{2,1,0:T(8,128)(2,1)}, bf16[2,144,256]{2,1,0:T(8,128)(2,1)S(1)}, u32[]{:S(2)}) copy-start(bf16[2,144,256]{2,1,0:T(8,128)(2,1)S(1)} %collective-permute-done.1.refs_2_) | copy-start | bytes 442372
  17.5 1.4 %collective-permute-start.2 = (bf16[144,256]{1,0:T(8,128)(2,1)S(1)}, bf16[144,256]{1,0:T(8,128)(2,1)S(1)}, u32[]{:S(2)}, u32[]{:S(2)}) collective-permute-start(bf16[144,256]{1,0:T(8,128)(2,1)S(1)} %slice_bitcast_fusion.2), channel_id=1, source_target_pairs={{0,2},{4,6},{8,10},{12,14},{16,18},{20,22},{24,26},{28,30},{2,0},{... | collective-permute-start | bytes 221192 | tf_op jit(solution)/shard_map/ppermute | solution.py:420
  18.0 0.9 %copy-start.3 = (bf16[144,256]{1,0:T(8,128)(2,1)}, bf16[144,256]{1,0:T(8,128)(2,1)S(1)}, u32[]{:S(2)}) copy-start(bf16[144,256]{1,0:T(8,128)(2,1)S(1)} %collective-permute-done.refs_1_) | copy-start | bytes 221188
  18.0 0.9 %copy-start.4 = (bf16[144,256]{1,0:T(8,128)(2,1)}, bf16[144,256]{1,0:T(8,128)(2,1)S(1)}, u32[]{:S(2)}) copy-start(bf16[144,256]{1,0:T(8,128)(2,1)S(1)} %collective-permute-done.6.refs_7_) | copy-start | bytes 221188
  18.0 0.9 %copy-start.5 = (bf16[144,256]{1,0:T(8,128)(2,1)}, bf16[144,256]{1,0:T(8,128)(2,1)S(1)}, u32[]{:S(2)}) copy-start(bf16[144,256]{1,0:T(8,128)(2,1)S(1)} %collective-permute-done.4.refs_5_) | copy-start | bytes 221188
  18.9 0.6 %copy-start.6 = (bf16[144,256]{1,0:T(8,128)(2,1)}, bf16[144,256]{1,0:T(8,128)(2,1)S(1)}, u32[]{:S(2)}) copy-start(bf16[144,256]{1,0:T(8,128)(2,1)S(1)} %collective-permute-done.2.refs_3_) | copy-start | bytes 221188
  28.3 2.7 %collective-permute-start.8 = (f32[8,128]{1,0:T(8,128)}, f32[8,128]{1,0:T(8,128)S(1)}, u32[]{:S(2)}, u32[]{:S(2)}) collective-permute-start(f32[8,128]{1,0:T(8,128)} %iteration.3.refs_4_), channel_id=1, source_target_pairs={{0,1},{1,0},{2,3},{3,2},{4,5},{5,4},{6,7},{7,6},{8,9},{9,8},{10,11... | collective-permute-start | bytes 12296 | tf_op jit(solution)/shard_map/ppermute | solution.py:469
  29.5 1.7 %collective-permute-start.7 = (f32[8,128]{1,0:T(8,128)}, f32[8,128]{1,0:T(8,128)S(1)}, u32[]{:S(2)}, u32[]{:S(2)}) collective-permute-start(f32[8,128]{1,0:T(8,128)} %iteration.3.refs_4_), channel_id=1, source_target_pairs={{0,2},{4,6},{8,10},{12,14},{16,18},{20,22},{24,26},{28,30},{2,0},{... | collective-permute-start | bytes 12296 | tf_op jit(solution)/shard_map/ppermute | solution.py:420
  30.9 0.6 %copy-start.9 = (f32[8,128]{1,0:T(8,128)}, f32[8,128]{1,0:T(8,128)S(1)}, u32[]{:S(2)}) copy-start(f32[8,128]{1,0:T(8,128)S(1)} %collective-permute-done.8.refs_6_) | copy-start | bytes 12292
  31.5 0.6 %copy-start.10 = (f32[8,128]{1,0:T(8,128)}, f32[8,128]{1,0:T(8,128)S(1)}, u32[]{:S(2)}) copy-start(f32[8,128]{1,0:T(8,128)S(1)} %collective-permute-done.7.refs_5_) | copy-start | bytes 12292
  35.2 3.0 %collective-permute-start.10 = (f32[8,128]{1,0:T(8,128)}, f32[8,128]{1,0:T(8,128)S(1)}, u32[]{:S(2)}, u32[]{:S(2)}) collective-permute-start(f32[8,128]{1,0:T(8,128)} %iteration.4.refs_4_), channel_id=1, source_target_pairs={{0,1},{1,0},{2,3},{3,2},{4,5},{5,4},{6,7},{7,6},{8,9},{9,8},{10,11... | collective-permute-start | bytes 12296 | tf_op jit(solution)/shard_map/ppermute | solution.py:469
  36.4 2.8 %collective-permute-start.9 = (f32[8,128]{1,0:T(8,128)}, f32[8,128]{1,0:T(8,128)S(1)}, u32[]{:S(2)}, u32[]{:S(2)}) collective-permute-start(f32[8,128]{1,0:T(8,128)} %iteration.4.refs_4_), channel_id=1, source_target_pairs={{0,2},{4,6},{8,10},{12,14},{16,18},{20,22},{24,26},{28,30},{2,0},{... | collective-permute-start | bytes 12296 | tf_op jit(solution)/shard_map/ppermute | solution.py:420
  38.2 1.0 %copy-start.7 = (f32[8,128]{1,0:T(8,128)}, f32[8,128]{1,0:T(8,128)S(1)}, u32[]{:S(2)}) copy-start(f32[8,128]{1,0:T(8,128)S(1)} %collective-permute-done.10.refs_6_) | copy-start | bytes 12292
  39.2 0.6 %copy-start.8 = (f32[8,128]{1,0:T(8,128)}, f32[8,128]{1,0:T(8,128)S(1)}, u32[]{:S(2)}) copy-start(f32[8,128]{1,0:T(8,128)S(1)} %collective-permute-done.9.refs_5_) | copy-start | bytes 12292
  42.7 4.7 %collective-permute-start.13 = (f32[8,128]{1,0:T(8,128)}, f32[8,128]{1,0:T(8,128)S(1)}, u32[]{:S(2)}, u32[]{:S(2)}) collective-permute-start(f32[8,128]{1,0:T(8,128)} %iteration.5.refs_0_), channel_id=1, source_target_pairs={{0,3},{1,2},{4,7},{5,6},{8,11},{9,10},{12,15},{13,14},{16,19},{17,... | collective-permute-start | bytes 12296 | tf_op jit(solution)/shard_map/ppermute | solution.py:456
  45.7 2.7 %collective-permute-start.12 = (f32[8,128]{1,0:T(8,128)}, f32[8,128]{1,0:T(8,128)S(1)}, u32[]{:S(2)}, u32[]{:S(2)}) collective-permute-start(f32[8,128]{1,0:T(8,128)} %iteration.5.refs_0_), channel_id=1, source_target_pairs={{0,1},{1,0},{2,3},{3,2},{4,5},{5,4},{6,7},{7,6},{8,9},{9,8},{10,11... | collective-permute-start | bytes 12296 | tf_op jit(solution)/shard_map/ppermute | solution.py:472
  45.9 2.4 %collective-permute-start.11 = (f32[8,128]{1,0:T(8,128)}, f32[8,128]{1,0:T(8,128)S(1)}, u32[]{:S(2)}, u32[]{:S(2)}) collective-permute-start(f32[8,128]{1,0:T(8,128)} %iteration.5.refs_0_), channel_id=1, source_target_pairs={{0,2},{4,6},{8,10},{12,14},{16,18},{20,22},{24,26},{28,30},{2,0},{... | collective-permute-start | bytes 12296 | tf_op jit(solution)/shard_map/ppermute | solution.py:420
  47.4 0.9 %copy-start.11 = (f32[8,128]{1,0:T(8,128)}, f32[8,128]{1,0:T(8,128)S(1)}, u32[]{:S(2)}) copy-start(f32[8,128]{1,0:T(8,128)S(1)} %collective-permute-done.13.refs_3_) | copy-start | bytes 12292
  48.3 0.6 %copy-start.12 = (f32[8,128]{1,0:T(8,128)}, f32[8,128]{1,0:T(8,128)S(1)}, u32[]{:S(2)}) copy-start(f32[8,128]{1,0:T(8,128)S(1)} %collective-permute-done.12.refs_2_) | copy-start | bytes 12292
  48.9 0.6 %copy-start.13 = (f32[8,128]{1,0:T(8,128)}, f32[8,128]{1,0:T(8,128)S(1)}, u32[]{:S(2)}) copy-start(f32[8,128]{1,0:T(8,128)S(1)} %collective-permute-done.11.refs_1_) | copy-start | bytes 12292
where the time goes:
time: 51.2 us; the launch traced here: 50.9 us
  Pallas kernels  17.7 us (35%)
  starting transfers between devices  17.7 us (35%)
  waiting for transfers between devices  10.5 us (21%)
  local copies, waits for them, and re-layouts  4.32 us (8%)
  between operations  0.74 us (1%)
    pallas_call x3, Pallas kernels, per_device(): pl.pallas_call(lambda *refs, step=step: iteration_kernel(cols, step, WIND...  9.11 us
    ppermute x3, starting transfers between devices, per_device(): lax.ppermute(payload, 'sec', perm)  6.42 us
    ppermute x7, starting transfers between devices, between_cores(): return lax.ppermute(x, 'sec', cores)  5.6 us
    pallas_call x1, Pallas kernels, per_device(): pl.pallas_call(lambda *refs: pre_kernel(cols, *refs), out_shape=(jax.Shap...  5.54 us
    ppermute x3, waiting for transfers between devices, per_device(): lax.ppermute(payload, 'sec', perm)  5.28 us
    unnamed x28, local copies, waits for them, and re-layouts  3.38 us
    ppermute x1, starting transfers between devices, diagonal(): return lax.ppermute(x, ('sec', 'row'), pairs)  2.98 us
    ppermute x2, starting transfers between devices, per_device(): lax.ppermute(out, 'row', perm)  2.42 us
  transfers between devices with their start and end apart: 14, of which 8 were waited for; matrix products, arithmetic and copies ran while one was open for 2% of the time, Pallas kernels for 0%

commit v1 on v0

--- a/solution.py
+++ b/solution.py
@@ -61,7 +61,7 @@
 
     down = np.concatenate(split_table(np.concatenate([cosine, -sine], axis=0)), axis=1)
     up = np.concatenate(split_table(np.concatenate([cosine, -sine], axis=1)), axis=0)
-    return doubled(basis), down, up, doubled(kernel), doubled(back)
+    return np.stack([doubled(basis), down, up]), np.stack([doubled(kernel), doubled(back)])
 
 
 def split(values):
@@ -86,34 +86,34 @@
     return (1 - 2 * (lax.broadcasted_iota(jnp.int32, shape, dim) % 2)).astype(f32)
 
 
-def pack_kernel(cols, shift_ref, mask_ref, image_ref, out_ref):
-    core = lax.rem(lax.axis_index("sec"), 2)
-    width = cols * PATCH
-    for part in range(2):
-        half = lax.rem(core + part, 2)
-
-        @pl.when(half == 0)
-        def _(part=part):
-            out_ref[part, :PATCH, :] = image_ref[0, :, :width]
-
-        @pl.when(half == 1)
-        def _(part=part):
-            out_ref[part, :PATCH, :] = image_ref[0, :, width:]
-
-        for col in range(cols):
-            place = half * cols + col
-            row = lax.broadcasted_iota(jnp.int32, (EXTRA, PATCH), 0)
-            values = jnp.zeros((EXTRA, PATCH), f32)
-            for dim in range(2):
-                shift = jnp.full((EXTRA, PATCH), shift_ref[dim, 0, 0, place], f32)
-                high = shift.astype(bf16).astype(f32)
-                middle = (shift - high).astype(bf16).astype(f32)
-                low = (shift - high) - middle
-                mask = jnp.full((EXTRA, PATCH), mask_ref[dim, 0, 0, place].astype(f32), f32)
-                for at, part_value in enumerate((high, middle, low)):
-                    values = jnp.where(row == 3 * dim + at, part_value, values)
-                values = jnp.where(row == 6 + dim, mask, values)
-            out_ref[part, PATCH:, col * PATCH : (col + 1) * PATCH] = values.astype(bf16)
+def half_of():
+    return lax.rem(lax.axis_index("sec") + lax.axis_index("row"), 2)
+
+
+def pack_kernel(shift_ref, mask_ref, image_ref, out_ref, shift, mask, sems):
+    copies = [
+        pltpu.make_async_copy(image_ref.at[0], out_ref.at[:PATCH], sems.at[0]),
+        pltpu.make_async_copy(shift_ref, shift, sems.at[1]),
+        pltpu.make_async_copy(mask_ref, mask, sems.at[2]),
+    ]
+    for copy in copies:
+        copy.start()
+    copies[1].wait()
+    copies[2].wait()
+    row = lax.broadcasted_iota(jnp.int32, (EXTRA, PATCH), 0)
+    for col in range(shift_ref.shape[-1]):
+        values = jnp.zeros((EXTRA, PATCH), f32)
+        for dim in range(2):
+            value = jnp.full((EXTRA, PATCH), shift[dim, 0, 0, col], f32)
+            high = value.astype(bf16).astype(f32)
+            middle = (value - high).astype(bf16).astype(f32)
+            low = (value - high) - middle
+            allowed = jnp.full((EXTRA, PATCH), mask[dim, 0, 0, col].astype(f32), f32)
+            for at, part in enumerate((high, middle, low)):
+                values = jnp.where(row == 3 * dim + at, part, values)
+            values = jnp.where(row == 6 + dim, allowed, values)
+        out_ref[PATCH:, col * PATCH : (col + 1) * PATCH] = values.astype(bf16)
+    copies[0].wait()
 
 
 def forward_patch(pixels, basis_ref, down_ref):
@@ -133,60 +133,45 @@
     return real, imag, energy_row, nyquist_row
 
 
-def pre_kernel(cols, *refs):
-    (own, own_x, near_a, near_ax, near_b, near_bx, far, far_x, basis_ref, down_ref, up_ref) = refs[:11]
-    (base_ref, stats_ref) = refs[11:13]
-    real_ref, imag_ref, energy_ref, nyquist_ref = refs[13:]
+def spectra_kernel(cols, stage, *refs):
+    here_ref, beside_ref, tables_ref = refs[:3]
+    basis_ref, down_ref, up_ref = [tables_ref.at[k] for k in range(3)]
+    real_ref, imag_ref, row_ref, base_ref = refs[-4:]
+    if stage == 0:
+        row_ref[...] = jnp.zeros(row_ref.shape, f32)
     sec = lax.axis_index("sec")
     core = lax.rem(sec, 2)
     odd = lax.rem(sec // 2, 2)
-    after_a = 5 - 4 * odd
-    after_b = 1 + 4 * odd
-    blocks = (
-        (own.at[0], HALO + core),
-        (own_x, HALO + 1 - core),
-        (near_a.at[0], after_a + core),
-        (near_ax, after_a + 1 - core),
-        (near_b.at[0], after_b + core),
-        (near_bx, after_b + 1 - core),
-        (far.at[0], (WINDOW - 1) * (1 - core)),
-        (far_x, (WINDOW - 1) * core),
-    )
-    for block, slot in blocks:
+    half = half_of()
+    if stage == 0:
+        slots = (HALO + core, HALO + 1 - core)
+        pairs = (HALO,)
+    elif stage == 1:
+        slots = (5 - 4 * odd + core, 6 - 4 * odd - core)
+        pairs = (4 - 3 * odd, 5 - 3 * odd)
+    elif stage == 2:
+        slots = (1 + 4 * odd + core, 2 + 4 * odd - core)
+        pairs = (1 + 3 * odd, 2 + 3 * odd)
+    else:
+        slots = ((WINDOW - 1) * core, (WINDOW - 1) * (1 - core))
+        pairs = (0, WINDOW - 2)
+    for block, slot in zip((here_ref, beside_ref), slots):
         for col in range(cols):
-            where = slice(col * PATCH, (col + 1) * PATCH)
-            real, imag, energy_row, nyquist_row = forward_patch(block[:PATCH, where], basis_ref, down_ref)
+            start = pl.multiple_of((half * cols + col) * PATCH, PATCH)
+            real, imag, energy_row, nyquist_row = forward_patch(
+                block[:PATCH, pl.ds(start, PATCH)], basis_ref, down_ref
+            )
             real_ref[slot, col] = real
             imag_ref[slot, col] = imag
-            energy_ref[col, pl.ds(slot, 1), :] = energy_row
-            nyquist_ref[col, pl.ds(slot, 1), :] = nyquist_row
-            small = block[PATCH:, where].astype(f32)
+            row_ref[col, 0, pl.ds(slot, 1), :] = energy_row
+            row_ref[col, 1, pl.ds(slot, 1), :] = nyquist_row
+            small = block[PATCH:, pl.ds(start, PATCH)].astype(f32)
             for dim in range(2):
                 shift = small[3 * dim : 3 * dim + 1] + small[3 * dim + 1 : 3 * dim + 2] + small[3 * dim + 2 : 3 * dim + 3]
-                stats_ref[col, 5 + dim, pl.ds(slot, 1), :] = shift
-                stats_ref[col, 7 + dim, pl.ds(slot, 1), :] = small[6 + dim : 7 + dim]
-    lane = lanes((WINDOW, PATCH))
-    weight = jnp.where(lane % HALF == 0, 1.0, 2.0)
-    at_nyquist = jnp.where(lane == HALF, 1.0, 0.0)
-    area = float(PATCH * PATCH)
-
-    def spread(values):
-        return jnp.broadcast_to(jnp.sum(values, axis=1, keepdims=True), (WINDOW, PATCH))
-
-    for col in range(cols):
-        energy, nyquist = energy_ref[col], nyquist_ref[col]
-        corner = spread(nyquist * at_nyquist)
-        corner_energy = corner * corner / area
-        row_energy = spread(weight * (1.0 - at_nyquist) * nyquist * nyquist) / area
-        col_energy = jnp.maximum(spread(energy * at_nyquist) / PATCH - corner_energy, 0.0)
-        whole = spread(weight * energy) / PATCH
-        stats_ref[col, 0] = jnp.maximum(whole - row_energy - col_energy - corner_energy, 0.0)
-        stats_ref[col, 1] = row_energy
-        stats_ref[col, 2] = col_energy
-        stats_ref[col, 3] = corner_energy
-        stats_ref[col, 4] = corner
+                row_ref[col, 2 + dim, pl.ds(slot, 1), :] = shift
+                row_ref[col, 4 + dim, pl.ds(slot, 1), :] = small[6 + dim : 7 + dim]
     low_lane = lanes((1, PATCH)) <= HALF
-    for pair in range(WINDOW - 1):
+    for pair in pairs:
         for col in range(cols):
             sr, si = real_ref[pair, col], imag_ref[pair, col]
             nr, ni = real_ref[pair + 1, col], imag_ref[pair + 1, col]
@@ -197,6 +182,25 @@
             wide = fold(dot(up_ref[...], jnp.concatenate([top, bottom], axis=0)))
             base = wide[:PATCH] + wide[PATCH:]
             base_ref[col, pair] = jnp.concatenate(split(base), axis=1)
+
+
+def energies(row_ref, col):
+    lane = lanes((WINDOW, PATCH))
+    weight = jnp.where(lane % HALF == 0, 1.0, 2.0)
+    at_nyquist = jnp.where(lane == HALF, 1.0, 0.0)
+    area = float(PATCH * PATCH)
+
+    def spread(values):
+        return jnp.broadcast_to(jnp.sum(values, axis=1, keepdims=True), (WINDOW, PATCH))
+
+    energy, nyquist = row_ref[col, 0], row_ref[col, 1]
+    corner = spread(nyquist * at_nyquist)
+    corner_energy = corner * corner / area
+    row_energy = spread(weight * (1.0 - at_nyquist) * nyquist * nyquist) / area
+    col_energy = jnp.maximum(spread(energy * at_nyquist) / PATCH - corner_energy, 0.0)
+    whole = spread(weight * energy) / PATCH
+    bulk = jnp.maximum(whole - row_energy - col_energy - corner_energy, 0.0)
+    return bulk, row_energy, col_energy, corner_energy, corner
 
 
 def cos_sin_turns(turns):
@@ -233,7 +237,7 @@
     return packed
 
 
-def smoothed(updated, vertical, beside, core, cols):
+def smoothed(updated, vertical, beside, half, cols):
     result = []
     for dim in range(2):
         current = []
@@ -241,11 +245,11 @@
             if col > 0:
                 left = updated[dim][col - 1]
             else:
-                left = jnp.where(core == 1, beside[dim][cols - 1], 0.0)
+                left = jnp.where(half == 1, beside[dim][cols - 1], 0.0)
             if col < cols - 1:
                 right = updated[dim][col + 1]
             else:
-                right = jnp.where(core == 0, beside[dim][0], 0.0)
+                right = jnp.where(half == 0, beside[dim][0], 0.0)
             own = updated[dim][col]
             current.append(own + stiffness * (left + right + vertical[dim][col] - 4.0 * own))
         result.append(current)
@@ -261,18 +265,20 @@
 
 
 def iteration_kernel(cols, first, last, starts, n_vertical, *refs):
-    base_ref, stats_ref, kernel_ref, back_ref = refs[:4]
-    refs = refs[4:]
+    base_ref, row_ref, tables_ref = refs[:3]
+    kernel_ref, back_ref = tables_ref.at[0], tables_ref.at[1]
+    refs = refs[3:]
     core = lax.rem(lax.axis_index("sec"), 2)
+    half = half_of()
     if starts:
-        field = [[stats_ref[col, 5 + dim] for col in range(cols)] for dim in range(2)]
+        field = [[row_ref[col, 2 + dim] for col in range(cols)] for dim in range(2)]
     else:
         own_message, beside_message = refs[:2]
         vertical = unpack(refs[2][...], cols)
         for extra in refs[3 : 2 + n_vertical]:
             vertical = add(vertical, unpack(extra[...], cols))
         refs = refs[2 + n_vertical :]
-        field = smoothed(unpack(own_message[...], cols), vertical, unpack(beside_message[...], cols), core, cols)
+        field = smoothed(unpack(own_message[...], cols), vertical, unpack(beside_message[...], cols), half, cols)
     out_ref, total_ref, moment_ref, edge_ref = refs
     lane = lanes((WINDOW, PATCH))
     frequency = (lane % HALF).astype(f32) * (1.0 / PATCH)
@@ -285,17 +291,13 @@
         cos_y, sin_y = cos_sin_turns(dy * 0.5)
         cos_x, sin_x = cos_sin_turns(dx * 0.5)
         cos_both = cos_y * cos_x - sin_y * sin_x
-        energy = (
-            stats_ref[col, 0]
-            + cos_y * cos_y * stats_ref[col, 1]
-            + cos_x * cos_x * stats_ref[col, 2]
-            + cos_both * cos_both * stats_ref[col, 3]
-        )
+        bulk, row_energy, col_energy, corner_energy, nyquist = energies(row_ref, col)
+        energy = bulk + cos_y * cos_y * row_energy + cos_x * cos_x * col_energy + cos_both * cos_both * corner_energy
         scale = (sharpness / math.log(2.0)) / jnp.sqrt(energy * next_section(energy) + epsilon)
         gamma_y = cos_y * next_section(cos_y)
         gamma_x = cos_x * next_section(cos_x)
         gamma = cos_both * next_section(cos_both)
-        corner = stats_ref[col, 4] * next_section(stats_ref[col, 4]) * (1.0 / (PATCH * PATCH))
+        corner = nyquist * next_section(nyquist) * (1.0 / (PATCH * PATCH))
         ripple.append((gamma - gamma_y * gamma_x) * corner * scale)
         cosine, sine = cos_sin_turns((dy - next_section(dy)) * frequency)
         harmonics = jnp.where(high_lane, sine, cosine) * 2.0
@@ -345,8 +347,8 @@
         inverse = 1.0 / spread(total)
         offsets = (spread(moment_ref[col]) * inverse, spread(total * lag) * inverse)
         edges = (spread(edge_ref[col]) * inverse, spread(jnp.where(nyquist_lane, total, 0.0)) * inverse)
-        lower = stats_ref[col, 7] * (section > 0).astype(f32)
-        upper = stats_ref[col, 8] * (section < sec_total - 1).astype(f32)
+        lower = row_ref[col, 4] * (section > 0).astype(f32)
+        upper = row_ref[col, 5] * (section < sec_total - 1).astype(f32)
         for dim in range(2):
             reverse = previous_section(-(offsets[dim] + float(PATCH) * edges[dim]))
             mean = (lower * reverse + upper * offsets[dim]) / jnp.maximum(lower + upper, 1.0)
@@ -367,8 +369,9 @@
     field_ref, mean_ref = refs[2 + 2 * n_vertical :]
     core = lax.rem(lax.axis_index("sec"), 2)
     mine, other = unpack(own, cols), unpack(beside, cols)
-    here = smoothed(mine, vertical, other, core, cols)
-    there = smoothed(other, vertical_beside, mine, 1 - core, cols)
+    half = half_of()
+    here = smoothed(mine, vertical, other, half, cols)
+    there = smoothed(other, vertical_beside, mine, 1 - half, cols)
     mean_here, mean_there = unpack(own, cols, 2 * cols), unpack(beside, cols, 2 * cols)
     lane = lanes((1, PATCH))
 
@@ -379,19 +382,23 @@
         for dim in range(2):
             row = jnp.zeros((1, PATCH), f32)
             for col in range(cols):
-                first = pick(jnp.where(core == 0, a[dim][col], b[dim][col]))
-                second = pick(jnp.where(core == 0, b[dim][col], a[dim][col]))
+                first = pick(jnp.where(half == 0, a[dim][col], b[dim][col]))
+                second = pick(jnp.where(half == 0, b[dim][col], a[dim][col]))
                 row = jnp.where(lane == col, first, row)
                 row = jnp.where(lane == cols + col, second, row)
             out[dim, 0] = row[:, : 2 * cols]
 
 
+def limit(mebibytes):
+    return pltpu.CompilerParams(vmem_limit_bytes=mebibytes << 20)
+
+
+def anywhere():
+    return pl.BlockSpec(memory_space=pl.ANY)
+
+
 def vmem():
     return pl.BlockSpec(memory_space=pltpu.VMEM)
-
-
-def smem():
-    return pl.BlockSpec(memory_space=pltpu.SMEM)
 
 
 def swap(pairs):
@@ -405,47 +412,54 @@
     assert section_images.shape[:2] == (1, PATCH)
     cols = patch_cols // 2
     chips = n_sec // 2
-    constants = [jnp.asarray(t) for t in tables()]
-    basis, down, up, kernel, back = constants
+    spectrum_tables, shift_tables = [jnp.asarray(table) for table in tables()]
 
     def sections(pairs):
         return [(2 * a + c, 2 * b + c) for a, b in pairs for c in range(2)]
 
     swap_a = sections(swap([(j, j + 1) for j in range(0, chips - 1, 2)]))
     swap_b = sections(swap([(j, j + 1) for j in range(1, chips - 1, 2)]))
-    far = [(2 * j + 1, 2 * j + 5) for j in range(chips - 2)] + [(2 * j + 4, 2 * j) for j in range(chips - 2)]
+    far = swap([(2 * j + 1, 2 * j + 4) for j in range(chips - 2)])
     cores = swap([(2 * j, 2 * j + 1) for j in range(chips)])
 
     def between_cores(x):
         return lax.ppermute(x, "sec", cores)
 
     payload = pl.pallas_call(
-        lambda *refs: pack_kernel(cols, *refs),
-        out_shape=jax.ShapeDtypeStruct((2, PATCH + EXTRA, cols * PATCH), bf16),
-        in_specs=[smem(), smem(), vmem()],
+        pack_kernel,
+        out_shape=jax.ShapeDtypeStruct((PATCH + EXTRA, patch_cols * PATCH), bf16),
+        in_specs=[anywhere()] * 3,
         out_specs=vmem(),
+        scratch_shapes=[
+            pltpu.SMEM(displacement.shape, f32),
+            pltpu.SMEM(fold_mask.shape, jnp.int32),
+            pltpu.SemaphoreType.DMA((3,)),
+        ],
+        compiler_params=limit(4),
         name="pack",
-    )(displacement, fold_mask, section_images)
-    received = [payload] + [lax.ppermute(payload, "sec", perm) for perm in (swap_a, swap_b, far)]
-    operands = []
-    for block in received:
-        operands += [block, between_cores(block[1])]
-    base, stats = pl.pallas_call(
-        lambda *refs: pre_kernel(cols, *refs),
-        out_shape=(
-            jax.ShapeDtypeStruct((cols, WINDOW - 1, PATCH, 2 * PATCH), bf16),
-            jax.ShapeDtypeStruct((cols, 9, WINDOW, PATCH), f32),
-        ),
-        in_specs=[vmem()] * 11,
-        out_specs=(vmem(), vmem()),
-        scratch_shapes=[
-            pltpu.VMEM((WINDOW, cols, PATCH, PATCH), f32),
-            pltpu.VMEM((WINDOW, cols, PATCH, PATCH), f32),
-            pltpu.VMEM((cols, WINDOW, PATCH), f32),
-            pltpu.VMEM((cols, WINDOW, PATCH), f32),
-        ],
-        name="pre",
-    )(*operands, basis, down, up)
+    )(*[pltpu.with_memory_space_constraint(x, pltpu.HBM) for x in (displacement, fold_mask, section_images)])
+    received = [payload]
+    for perm in (swap_a, swap_b, far):
+        received.append(lax.ppermute(payload, "sec", perm))
+    state = []
+    for stage, block in enumerate(received):
+        beside = between_cores(block)
+        state = pl.pallas_call(
+            lambda *refs, stage=stage: spectra_kernel(cols, stage, *refs),
+            out_shape=(
+                jax.ShapeDtypeStruct((WINDOW, cols, PATCH, PATCH), f32),
+                jax.ShapeDtypeStruct((WINDOW, cols, PATCH, PATCH), f32),
+                jax.ShapeDtypeStruct((cols, 6, WINDOW, PATCH), f32),
+                jax.ShapeDtypeStruct((cols, WINDOW - 1, PATCH, 2 * PATCH), bf16),
+            ),
+            in_specs=[vmem()] * (3 + len(state)),
+            out_specs=[vmem()] * 4,
+            input_output_aliases={3 + k: k for k in range(len(state))},
+            compiler_params=limit(16),
+            cost_estimate=pl.CostEstimate(flops=500000000, bytes_accessed=1000000, transcendentals=0),
+            name="spectra",
+        )(block, beside, spectrum_tables, *state)
+    base, stats = state[3], state[2]
 
     row_perms = [swap([(r, r + 1) for r in range(0, n_row - 1, 2)])]
     if n_row > 2:
@@ -460,22 +474,24 @@
         out = pl.pallas_call(
             lambda *refs, step=step: iteration_kernel(cols, step, WINDOW - 1 - step, step == 0, len(row_perms), *refs),
             out_shape=jax.ShapeDtypeStruct((WINDOW, PATCH), f32),
-            in_specs=[vmem()] * (4 + len(messages)),
+            in_specs=[vmem()] * (3 + len(messages)),
             out_specs=vmem(),
             scratch_shapes=[pltpu.VMEM((cols, WINDOW, PATCH), f32)] * 3,
+            compiler_params=limit(8),
             name="iteration",
-        )(base, stats, kernel, back, *messages)
-        if step < ITERS - 1:
-            messages = [out, between_cores(out)] + [lax.ppermute(out, "row", perm) for perm in row_perms]
-    messages = [out, between_cores(out)]
-    for perm in row_perms:
-        messages += [lax.ppermute(out, "row", perm), diagonal(out, perm)]
+        )(base, stats, shift_tables, *messages)
+        beside = between_cores(out)
+        rows = [diagonal(out, perm) for perm in row_perms]
+        messages = [out, beside] + rows
+    straight = [lax.ppermute(out, "row", perm) for perm in row_perms]
+    messages = messages[:2] + [message for pair in zip(rows, straight) for message in pair]
     shape = jax.ShapeDtypeStruct(displacement.shape, f32)
     return pl.pallas_call(
         lambda *refs: final_kernel(cols, len(row_perms), *refs),
         out_shape=(shape, shape),
         in_specs=[vmem()] * len(messages),
         out_specs=(vmem(), vmem()),
+        compiler_params=limit(4),
         name="final",
     )(*messages)
 
@@ -483,6 +499,4 @@
 def solution(mesh):
     in_specs = (P("sec", "row", None), P(None, "sec", "row", None), P(None, "sec", "row", None))
     out_specs = (P(None, "sec", "row", None), P(None, "sec", "row", None))
-    return jax.shard_map(
-        per_device, mesh=mesh, in_specs=in_specs, out_specs=out_specs, check_vma=False
-    )
+    return jax.shard_map(per_device, mesh=mesh, in_specs=in_specs, out_specs=out_specs, check_vma=False)

time: 51.2 us -> 35.3 us (0.69)
  the two profiles are of different devices: /device:TPU:17 before, /device:TPU:20 now
where the time goes in v1:
time: 35.3 us; the launch traced here: 35.1 us
  starting transfers between devices  12.9 us (37%)
  waiting for transfers between devices  10.5 us (30%)
  Pallas kernels  9.87 us (28%)
  local copies, waits for them, and re-layouts  1 us (3%)
  between operations  0.76 us (2%)
    ppermute x3, starting transfers between devices, per_device(): received.append(lax.ppermute(payload, 'sec', perm))  6.92 us
    pallas_call x4, Pallas kernels, per_device(): pl.pallas_call(lambda *refs, stage=stage: spectra_kernel(cols, stage, *re...  4.81 us
    ppermute x3, waiting for transfers between devices, diagonal(): return lax.ppermute(x, ('sec', 'row'), pairs)  4.3 us
    ppermute x3, waiting for transfers between devices, per_device(): received.append(lax.ppermute(payload, 'sec', perm))  4.16 us
    ppermute x3, starting transfers between devices, diagonal(): return lax.ppermute(x, ('sec', 'row'), pairs)  3.91 us
    pallas_call x3, Pallas kernels, per_device(): pl.pallas_call(lambda *refs, step=step: iteration_kernel(cols, step, WIND...  3.46 us
    ppermute x1, waiting for transfers between devices, per_device(): straight = [lax.ppermute(out, 'row', perm) for perm in row_perms]  2.06 us
    ppermute x7, starting transfers between devices, between_cores(): return lax.ppermute(x, 'sec', cores)  1.52 us
  transfers between devices with their start and end apart: 14, of which 7 were waited for; matrix products, arithmetic and copies ran while one was open for 0% of the time, Pallas kernels for 10%

profile of v1, /device:TPU:20, one launch (start us, length us, event | category | flops | bytes accessed | tf_op | source)
XLA Modules:
  0.0 35.1 jit_solution(7083781092351835876)
XLA Ops:
  0.6 0.9 %pack.1.refs_0_ = bf16[144,512]{1,0:T(8,128)(2,1)S(1)} custom-call(f32[2,1,1,4]{3,2,1,0:T(1,128)} %shift_ref.1, s32[2,1,1,4]{3,2,1,0:T(1,128)} %mask_ref.1, bf16[1,128,512]{2,1,0:T(8,128)(2,1)} %image_ref.1), custom_call_target="tpu_custom_call" | custom-call | tf_op jit(solution)/shard_map/pack/pallas_call | solution.py:428
  1.6 0.6 %collective-permute-start.4 = (bf16[144,512]{1,0:T(8,128)(2,1)S(1)}, bf16[144,512]{1,0:T(8,128)(2,1)S(1)}, u32[]{:S(2)}, u32[]{:S(2)}) collective-permute-start(bf16[144,512]{1,0:T(8,128)(2,1)S(1)} %pack.1.refs_0_), channel_id=1, source_target_pairs={{0,4},{2,6},{8,12},{10,14},{16,20},{18,22},{24,28},{26,30},{4,0},{... | collective-permute-start | bytes 442376 | tf_op jit(solution)/shard_map/ppermute | solution.py:443
  2.1 4.4 %collective-permute-start.2 = (bf16[144,512]{1,0:T(8,128)(2,1)S(1)}, bf16[144,512]{1,0:T(8,128)(2,1)S(1)}, u32[]{:S(2)}, u32[]{:S(2)}) collective-permute-start(bf16[144,512]{1,0:T(8,128)(2,1)S(1)} %pack.1.refs_0_), channel_id=1, source_target_pairs={{4,8},{6,10},{12,16},{14,18},{20,24},{22,26},{8,4},{10,6},{16,12},... | collective-permute-start | bytes 442376 | tf_op jit(solution)/shard_map/ppermute | solution.py:443
  6.6 1.9 %collective-permute-start = (bf16[144,512]{1,0:T(8,128)(2,1)S(1)}, bf16[144,512]{1,0:T(8,128)(2,1)S(1)}, u32[]{:S(2)}, u32[]{:S(2)}) collective-permute-start(bf16[144,512]{1,0:T(8,128)(2,1)S(1)} %pack.1.refs_0_), channel_id=1, source_target_pairs={{2,8},{6,12},{10,16},{14,20},{18,24},{22,28},{8,2},{12,6},{16,10},... | collective-permute-start | bytes 442376 | tf_op jit(solution)/shard_map/ppermute | solution.py:443
  8.5 0.1 collective-permute-start.6
  8.6 1.8 %collective-permute-done.4.refs_0_ = bf16[144,512]{1,0:T(8,128)(2,1)S(1)} collective-permute-done((bf16[144,512]{1,0:T(8,128)(2,1)S(1)}, bf16[144,512]{1,0:T(8,128)(2,1)S(1)}, u32[]{:S(2)}, u32[]{:S(2)}) %collective-permute-start.4) | collective-permute-done | bytes 147488 | tf_op jit(solution)/shard_map/ppermute | solution.py:443
  10.4 0.0 collective-permute-start.5
  10.4 0.2 collective-permute-done.2.refs_0_
  10.6 0.3 collective-permute-start.3
  10.9 2.1 %collective-permute-done.refs_0_ = bf16[144,512]{1,0:T(8,128)(2,1)S(1)} collective-permute-done((bf16[144,512]{1,0:T(8,128)(2,1)S(1)}, bf16[144,512]{1,0:T(8,128)(2,1)S(1)}, u32[]{:S(2)}, u32[]{:S(2)}) %collective-permute-start) | collective-permute-done | bytes 147488 | tf_op jit(solution)/shard_map/ppermute | solution.py:443
  13.0 0.0 collective-permute-start.1
  13.0 0.0 collective-permute-done.6.refs_1_
  13.0 0.0 copy-start
  13.1 1.0 %copy-done = bf16[3,256,256]{2,1,0:T(8,128)(2,1)S(1)} copy-done((bf16[3,256,256]{2,1,0:T(8,128)(2,1)S(1)}, bf16[3,256,256]{2,1,0:T(8,128)(2,1)}, u32[]{:S(2)}) %copy-start) | copy-done | bytes 393240
  14.0 1.2 %spectra.4 = (f32[8,2,128,128]{3,2,1,0:T(8,128)S(1)}, f32[8,2,128,128]{3,2,1,0:T(8,128)S(1)}, f32[2,6,8,128]{3,2,1,0:T(8,128)S(1)}, bf16[2,7,128,256]{3,2,1,0:T(8,128)(2,1)S(1)}) custom-call(bf16[144,512]{1,0:T(8,128)(2,1)S(1)} %pack.1.refs_0_, bf16[144,512]{1,0:T(8,128)(2,1)S(1)} %collective-permute-done.6.refs_1_, bf16[3,256,256]{2,1,0:T(8,128)(2,1)S(1)} %copy-done), custom_call_target="tpu_custom_call" | custom-call | flops 500000000 | bytes 1000000 | tf_op jit(solution)/shard_map/spectra/pallas_call | solution.py:447
  15.2 0.0 collective-permute-done.5.refs_1_
  15.2 1.2 %spectra.5 = (f32[8,2,128,128]{3,2,1,0:T(8,128)S(1)}, f32[8,2,128,128]{3,2,1,0:T(8,128)S(1)}, f32[2,6,8,128]{3,2,1,0:T(8,128)S(1)}, bf16[2,7,128,256]{3,2,1,0:T(8,128)(2,1)S(1)}) custom-call(bf16[144,512]{1,0:T(8,128)(2,1)S(1)} %collective-permute-done.4.refs_0_, ...), custom_call_target="tpu_custom_call", output_to_operand_aliasing={{0}: (3, {}), {1}: (4, {}), {2}: (5, {}), {3}: (6, {})} | custom-call | flops 500000000 | bytes 1000000 | tf_op jit(solution)/shard_map/spectra/pallas_call | solution.py:447
  16.4 0.0 collective-permute-done.3.refs_1_
  16.4 1.2 %spectra.6 = (f32[8,2,128,128]{3,2,1,0:T(8,128)S(1)}, f32[8,2,128,128]{3,2,1,0:T(8,128)S(1)}, f32[2,6,8,128]{3,2,1,0:T(8,128)S(1)}, bf16[2,7,128,256]{3,2,1,0:T(8,128)(2,1)S(1)}) custom-call(bf16[144,512]{1,0:T(8,128)(2,1)S(1)} %collective-permute-done.2.refs_0_, ...), custom_call_target="tpu_custom_call", output_to_operand_aliasing={{0}: (3, {}), {1}: (4, {}), {2}: (5, {}), {3}: (6, {})} | custom-call | flops 500000000 | bytes 1000000 | tf_op jit(solution)/shard_map/spectra/pallas_call | solution.py:447
  17.6 0.0 collective-permute-done.1.refs_1_
  17.6 0.0 copy-start.1
  17.7 1.3 %spectra.7 = (f32[8,2,128,128]{3,2,1,0:T(8,128)S(1)}, f32[8,2,128,128]{3,2,1,0:T(8,128)S(1)}, f32[2,6,8,128]{3,2,1,0:T(8,128)S(1)}, bf16[2,7,128,256]{3,2,1,0:T(8,128)(2,1)S(1)}) custom-call(bf16[144,512]{1,0:T(8,128)(2,1)S(1)} %collective-permute-done.refs_0_, ...), custom_call_target="tpu_custom_call", output_to_operand_aliasing={{0}: (3, {}), {1}: (4, {}), {2}: (5, {}), {3}: (6, {})} | custom-call | flops 500000000 | bytes 1000000 | tf_op jit(solution)/shard_map/spectra/pallas_call | solution.py:447
  18.9 0.0 copy-done.1
  18.9 1.3 %iteration.3.refs_3_ = f32[8,128]{1,0:T(8,128)S(1)} custom-call(bf16[2,7,128,256]{3,2,1,0:T(8,128)(2,1)S(1)} %get-tuple-element.28.refs_0_, f32[2,6,8,128]{3,2,1,0:T(8,128)S(1)} %get-tuple-element.29.refs_1_, bf16[2,256,256]{2,1,0:T(8,128)(2,1)S(1)} %copy-done.1), custom_call_target="tpu_custom_call" | custom-call | tf_op jit(solution)/shard_map/iteration/pallas_call | solution.py:474
  20.2 0.6 %collective-permute-start.7 = (f32[8,128]{1,0:T(8,128)S(1)}, f32[8,128]{1,0:T(8,128)S(1)}, u32[]{:S(2)}, u32[]{:S(2)}) collective-permute-start(f32[8,128]{1,0:T(8,128)S(1)} %iteration.3.refs_3_), channel_id=1, source_target_pairs={{0,2},{4,6},{8,10},{12,14},{16,18},{20,22},{24,26},{28,30},{2,0},{... | collective-permute-start | bytes 12296 | tf_op jit(solution)/shard_map/ppermute | solution.py:426
  20.8 1.2 %collective-permute-start.8 = (f32[8,128]{1,0:T(8,128)S(1)}, f32[8,128]{1,0:T(8,128)S(1)}, u32[]{:S(2)}, u32[]{:S(2)}) collective-permute-start(f32[8,128]{1,0:T(8,128)S(1)} %iteration.3.refs_3_), channel_id=1, source_target_pairs={{0,3},{1,2},{4,7},{5,6},{8,11},{9,10},{12,15},{13,14},{16,19},{17,... | collective-permute-start | bytes 12296 | tf_op jit(solution)/shard_map/ppermute | solution.py:470
  22.0 0.0 collective-permute-done.7.refs_4_
  22.0 1.9 %collective-permute-done.8.refs_5_ = f32[8,128]{1,0:T(8,128)S(1)} collective-permute-done((f32[8,128]{1,0:T(8,128)S(1)}, f32[8,128]{1,0:T(8,128)S(1)}, u32[]{:S(2)}, u32[]{:S(2)}) %collective-permute-start.8) | collective-permute-done | bytes 4128 | tf_op jit(solution)/shard_map/ppermute | solution.py:470
  23.9 1.2 %iteration.4.refs_3_ = f32[8,128]{1,0:T(8,128)S(1)} custom-call(bf16[2,7,128,256]{3,2,1,0:T(8,128)(2,1)S(1)} %get-tuple-element.28.refs_0_, f32[2,6,8,128]{3,2,1,0:T(8,128)S(1)} %get-tuple-element.29.refs_1_, bf16[2,256,256]{2,1,0:T(8,128)(2,1)S(1)} %copy-done.1, f32[8,128]{1,0:T(8,128)S(1)} %iteration.3.refs_3_, ...), custom_call_target="tpu_custom_call" | custom-call | tf_op jit(solution)/shard_map/iteration/pallas_call | solution.py:474
  25.0 1.3 %collective-permute-start.10 = (f32[8,128]{1,0:T(8,128)S(1)}, f32[8,128]{1,0:T(8,128)S(1)}, u32[]{:S(2)}, u32[]{:S(2)}) collective-permute-start(f32[8,128]{1,0:T(8,128)S(1)} %iteration.4.refs_3_), channel_id=1, source_target_pairs={{0,3},{1,2},{4,7},{5,6},{8,11},{9,10},{12,15},{13,14},{16,19},{17,... | collective-permute-start | bytes 12296 | tf_op jit(solution)/shard_map/ppermute | solution.py:470
  26.3 0.4 %collective-permute-start.9 = (f32[8,128]{1,0:T(8,128)S(1)}, f32[8,128]{1,0:T(8,128)S(1)}, u32[]{:S(2)}, u32[]{:S(2)}) collective-permute-start(f32[8,128]{1,0:T(8,128)S(1)} %iteration.4.refs_3_), channel_id=1, source_target_pairs={{0,2},{4,6},{8,10},{12,14},{16,18},{20,22},{24,26},{28,30},{2,0},{... | collective-permute-start | bytes 12296 | tf_op jit(solution)/shard_map/ppermute | solution.py:426
  26.7 1.4 %collective-permute-done.10.refs_5_ = f32[8,128]{1,0:T(8,128)S(1)} collective-permute-done((f32[8,128]{1,0:T(8,128)S(1)}, f32[8,128]{1,0:T(8,128)S(1)}, u32[]{:S(2)}, u32[]{:S(2)}) %collective-permute-start.10) | collective-permute-done | bytes 4128 | tf_op jit(solution)/shard_map/ppermute | solution.py:470
  28.1 0.0 collective-permute-done.9.refs_4_
  28.1 1.0 %iteration.5.refs_0_ = f32[8,128]{1,0:T(8,128)S(1)} custom-call(bf16[2,7,128,256]{3,2,1,0:T(8,128)(2,1)S(1)} %get-tuple-element.28.refs_0_, f32[2,6,8,128]{3,2,1,0:T(8,128)S(1)} %get-tuple-element.29.refs_1_, bf16[2,256,256]{2,1,0:T(8,128)(2,1)S(1)} %copy-done.1, f32[8,128]{1,0:T(8,128)S(1)} %iteration.4.refs_3_, ...), custom_call_target="tpu_custom_call" | custom-call | tf_op jit(solution)/shard_map/iteration/pallas_call | solution.py:474
  29.1 0.2 collective-permute-start.11
  29.3 1.5 %collective-permute-start.12 = (f32[8,128]{1,0:T(8,128)S(1)}, f32[8,128]{1,0:T(8,128)S(1)}, u32[]{:S(2)}, u32[]{:S(2)}) collective-permute-start(f32[8,128]{1,0:T(8,128)S(1)} %iteration.5.refs_0_), channel_id=1, source_target_pairs={{0,3},{1,2},{4,7},{5,6},{8,11},{9,10},{12,15},{13,14},{16,19},{17,... | collective-permute-start | bytes 12296 | tf_op jit(solution)/shard_map/ppermute | solution.py:470
  30.8 0.5 %collective-permute-start.13 = (f32[8,128]{1,0:T(8,128)S(1)}, f32[8,128]{1,0:T(8,128)S(1)}, u32[]{:S(2)}, u32[]{:S(2)}) collective-permute-start(f32[8,128]{1,0:T(8,128)S(1)} %iteration.5.refs_0_), channel_id=1, source_target_pairs={{0,1},{1,0},{2,3},{3,2},{4,5},{5,4},{6,7},{7,6},{8,9},{9,8},{10,11... | collective-permute-start | bytes 12296 | tf_op jit(solution)/shard_map/ppermute | solution.py:486
  31.3 0.0 collective-permute-done.11.refs_1_
  31.3 1.0 %collective-permute-done.12.refs_2_ = f32[8,128]{1,0:T(8,128)S(1)} collective-permute-done((f32[8,128]{1,0:T(8,128)S(1)}, f32[8,128]{1,0:T(8,128)S(1)}, u32[]{:S(2)}, u32[]{:S(2)}) %collective-permute-start.12) | collective-permute-done | bytes 4128 | tf_op jit(solution)/shard_map/ppermute | solution.py:470
  32.3 2.1 %collective-permute-done.13.refs_3_ = f32[8,128]{1,0:T(8,128)S(1)} collective-permute-done((f32[8,128]{1,0:T(8,128)S(1)}, f32[8,128]{1,0:T(8,128)S(1)}, u32[]{:S(2)}, u32[]{:S(2)}) %collective-permute-start.13) | collective-permute-done | bytes 4128 | tf_op jit(solution)/shard_map/ppermute | solution.py:486
  34.4 0.7 %final.1 = (f32[2,1,1,4]{3,2,1,0:T(1,128)}, f32[2,1,1,4]{3,2,1,0:T(1,128)}) custom-call(f32[8,128]{1,0:T(8,128)S(1)} %iteration.5.refs_0_, f32[8,128]{1,0:T(8,128)S(1)} %collective-permute-done.11.refs_1_, f32[8,128]{1,0:T(8,128)S(1)} %collective-permute-done.12.refs_2_, f32[8,128]{1,0:T(8,128)S(1)} %collective-permute-done.13.refs_3_), custom_call_target="tpu_custom_call" | custom-call | tf_op jit(solution)/shard_map/final/pallas_call | solution.py:489
Async XLA Ops:
  1.6 8.8 %collective-permute-start.4 = (bf16[144,512]{1,0:T(8,128)(2,1)S(1)}, bf16[144,512]{1,0:T(8,128)(2,1)S(1)}, u32[]{:S(2)}, u32[]{:S(2)}) collective-permute-start(bf16[144,512]{1,0:T(8,128)(2,1)S(1)} %pack.1.refs_0_), channel_id=1, source_target_pairs={{0,4},{2,6},{8,12},{10,14},{16,20},{18,22},{24,28},{26,30},{4,0},{... | collective-permute-start | bytes 442376 | tf_op jit(solution)/shard_map/ppermute | solution.py:443
  2.1 8.5 %collective-permute-start.2 = (bf16[144,512]{1,0:T(8,128)(2,1)S(1)}, bf16[144,512]{1,0:T(8,128)(2,1)S(1)}, u32[]{:S(2)}, u32[]{:S(2)}) collective-permute-start(bf16[144,512]{1,0:T(8,128)(2,1)S(1)} %pack.1.refs_0_), channel_id=1, source_target_pairs={{4,8},{6,10},{12,16},{14,18},{20,24},{22,26},{8,4},{10,6},{16,12},... | collective-permute-start | bytes 442376 | tf_op jit(solution)/shard_map/ppermute | solution.py:443
  6.6 6.5 %collective-permute-start = (bf16[144,512]{1,0:T(8,128)(2,1)S(1)}, bf16[144,512]{1,0:T(8,128)(2,1)S(1)}, u32[]{:S(2)}, u32[]{:S(2)}) collective-permute-start(bf16[144,512]{1,0:T(8,128)(2,1)S(1)} %pack.1.refs_0_), channel_id=1, source_target_pairs={{2,8},{6,12},{10,16},{14,20},{18,24},{22,28},{8,2},{12,6},{16,10},... | collective-permute-start | bytes 442376 | tf_op jit(solution)/shard_map/ppermute | solution.py:443
  8.5 4.5 %collective-permute-start.6 = (bf16[144,512]{1,0:T(8,128)(2,1)S(1)}, bf16[144,512]{1,0:T(8,128)(2,1)S(1)}, u32[]{:S(2)}, u32[]{:S(2)}) collective-permute-start(bf16[144,512]{1,0:T(8,128)(2,1)S(1)} %pack.1.refs_0_), channel_id=1, source_target_pairs={{0,2},{4,6},{8,10},{12,14},{16,18},{20,22},{24,26},{28,30},{2,0},{... | collective-permute-start | bytes 442376 | tf_op jit(solution)/shard_map/ppermute | solution.py:426
  10.4 4.8 %collective-permute-start.5 = (bf16[144,512]{1,0:T(8,128)(2,1)S(1)}, bf16[144,512]{1,0:T(8,128)(2,1)S(1)}, u32[]{:S(2)}, u32[]{:S(2)}) collective-permute-start(bf16[144,512]{1,0:T(8,128)(2,1)S(1)} %collective-permute-done.4.refs_0_), channel_id=1, source_target_pairs={{0,2},{4,6},{8,10},{12,14},{16,18},{20,22},{24,26},{28,30},{2,0},{... | collective-permute-start | bytes 442376 | tf_op jit(solution)/shard_map/ppermute | solution.py:426
  10.6 5.8 %collective-permute-start.3 = (bf16[144,512]{1,0:T(8,128)(2,1)S(1)}, bf16[144,512]{1,0:T(8,128)(2,1)S(1)}, u32[]{:S(2)}, u32[]{:S(2)}) collective-permute-start(bf16[144,512]{1,0:T(8,128)(2,1)S(1)} %collective-permute-done.2.refs_0_), channel_id=1, source_target_pairs={{0,2},{4,6},{8,10},{12,14},{16,18},{20,22},{24,26},{28,30},{2,0},{... | collective-permute-start | bytes 442376 | tf_op jit(solution)/shard_map/ppermute | solution.py:426
  13.0 4.6 %collective-permute-start.1 = (bf16[144,512]{1,0:T(8,128)(2,1)S(1)}, bf16[144,512]{1,0:T(8,128)(2,1)S(1)}, u32[]{:S(2)}, u32[]{:S(2)}) collective-permute-start(bf16[144,512]{1,0:T(8,128)(2,1)S(1)} %collective-permute-done.refs_0_), channel_id=1, source_target_pairs={{0,2},{4,6},{8,10},{12,14},{16,18},{20,22},{24,26},{28,30},{2,0},{... | collective-permute-start | bytes 442376 | tf_op jit(solution)/shard_map/ppermute | solution.py:426
  13.0 1.0 %copy-start = (bf16[3,256,256]{2,1,0:T(8,128)(2,1)S(1)}, bf16[3,256,256]{2,1,0:T(8,128)(2,1)}, u32[]{:S(2)}) copy-start(bf16[3,256,256]{2,1,0:T(8,128)(2,1)} %constant.4.clone.refs_2_) | copy-start | bytes 1179652
  17.6 1.3 %copy-start.1 = (bf16[2,256,256]{2,1,0:T(8,128)(2,1)S(1)}, bf16[2,256,256]{2,1,0:T(8,128)(2,1)}, u32[]{:S(2)}) copy-start(bf16[2,256,256]{2,1,0:T(8,128)(2,1)} %constant.5.clone.refs_2_) | copy-start | bytes 786436
  20.2 1.8 %collective-permute-start.7 = (f32[8,128]{1,0:T(8,128)S(1)}, f32[8,128]{1,0:T(8,128)S(1)}, u32[]{:S(2)}, u32[]{:S(2)}) collective-permute-start(f32[8,128]{1,0:T(8,128)S(1)} %iteration.3.refs_3_), channel_id=1, source_target_pairs={{0,2},{4,6},{8,10},{12,14},{16,18},{20,22},{24,26},{28,30},{2,0},{... | collective-permute-start | bytes 12296 | tf_op jit(solution)/shard_map/ppermute | solution.py:426
  20.8 3.0 %collective-permute-start.8 = (f32[8,128]{1,0:T(8,128)S(1)}, f32[8,128]{1,0:T(8,128)S(1)}, u32[]{:S(2)}, u32[]{:S(2)}) collective-permute-start(f32[8,128]{1,0:T(8,128)S(1)} %iteration.3.refs_3_), channel_id=1, source_target_pairs={{0,3},{1,2},{4,7},{5,6},{8,11},{9,10},{12,15},{13,14},{16,19},{17,... | collective-permute-start | bytes 12296 | tf_op jit(solution)/shard_map/ppermute | solution.py:470
  25.0 3.1 %collective-permute-start.10 = (f32[8,128]{1,0:T(8,128)S(1)}, f32[8,128]{1,0:T(8,128)S(1)}, u32[]{:S(2)}, u32[]{:S(2)}) collective-permute-start(f32[8,128]{1,0:T(8,128)S(1)} %iteration.4.refs_3_), channel_id=1, source_target_pairs={{0,3},{1,2},{4,7},{5,6},{8,11},{9,10},{12,15},{13,14},{16,19},{17,... | collective-permute-start | bytes 12296 | tf_op jit(solution)/shard_map/ppermute | solution.py:470
  26.3 1.8 %collective-permute-start.9 = (f32[8,128]{1,0:T(8,128)S(1)}, f32[8,128]{1,0:T(8,128)S(1)}, u32[]{:S(2)}, u32[]{:S(2)}) collective-permute-start(f32[8,128]{1,0:T(8,128)S(1)} %iteration.4.refs_3_), channel_id=1, source_target_pairs={{0,2},{4,6},{8,10},{12,14},{16,18},{20,22},{24,26},{28,30},{2,0},{... | collective-permute-start | bytes 12296 | tf_op jit(solution)/shard_map/ppermute | solution.py:426
  29.1 2.2 %collective-permute-start.11 = (f32[8,128]{1,0:T(8,128)S(1)}, f32[8,128]{1,0:T(8,128)S(1)}, u32[]{:S(2)}, u32[]{:S(2)}) collective-permute-start(f32[8,128]{1,0:T(8,128)S(1)} %iteration.5.refs_0_), channel_id=1, source_target_pairs={{0,2},{4,6},{8,10},{12,14},{16,18},{20,22},{24,26},{28,30},{2,0},{... | collective-permute-start | bytes 12296 | tf_op jit(solution)/shard_map/ppermute | solution.py:426
  29.3 3.0 %collective-permute-start.12 = (f32[8,128]{1,0:T(8,128)S(1)}, f32[8,128]{1,0:T(8,128)S(1)}, u32[]{:S(2)}, u32[]{:S(2)}) collective-permute-start(f32[8,128]{1,0:T(8,128)S(1)} %iteration.5.refs_0_), channel_id=1, source_target_pairs={{0,3},{1,2},{4,7},{5,6},{8,11},{9,10},{12,15},{13,14},{16,19},{17,... | collective-permute-start | bytes 12296 | tf_op jit(solution)/shard_map/ppermute | solution.py:470
  30.8 3.6 %collective-permute-start.13 = (f32[8,128]{1,0:T(8,128)S(1)}, f32[8,128]{1,0:T(8,128)S(1)}, u32[]{:S(2)}, u32[]{:S(2)}) collective-permute-start(f32[8,128]{1,0:T(8,128)S(1)} %iteration.5.refs_0_), channel_id=1, source_target_pairs={{0,1},{1,0},{2,3},{3,2},{4,5},{5,4},{6,7},{7,6},{8,9},{9,8},{10,11... | collective-permute-start | bytes 12296 | tf_op jit(solution)/shard_map/ppermute | solution.py:486

commit v2 on v1

--- a/solution.py
+++ b/solution.py
@@ -14,6 +14,7 @@
 HALO = 3
 WINDOW = 8
 EXTRA = 16
+GROUP = 7
 
 step_size = 0.5
 stiffness = 0.2
@@ -49,19 +50,13 @@
     back[HALF + 1 :] = -2.0 * sine[1:HALF]
     back /= n * n
 
-    kernel = np.zeros((n, n))
-    kernel[:HALF] = cosine[:HALF]
-    kernel[HALF] = sign
-    kernel[HALF + 1 :] = -sine[1:HALF]
-    kernel /= n
-
     def doubled(table):
         pair = np.concatenate(split_table(table), axis=1)
         return np.concatenate([pair, pair], axis=0)
 
     down = np.concatenate(split_table(np.concatenate([cosine, -sine], axis=0)), axis=1)
     up = np.concatenate(split_table(np.concatenate([cosine, -sine], axis=1)), axis=0)
-    return np.stack([doubled(basis), down, up]), np.stack([doubled(kernel), doubled(back)])
+    return np.stack([doubled(basis), down, up]), doubled(back)
 
 
 def split(values):
@@ -116,61 +111,70 @@
     copies[0].wait()
 
 
-def forward_patch(pixels, basis_ref, down_ref):
-    values = pixels.astype(f32)
-    total = jnp.sum(jnp.sum(values, axis=0, keepdims=True), axis=1, keepdims=True)
-    values = values - total * (1.0 / (PATCH * PATCH))
-    rows = fold(dot(jnp.concatenate(split(values), axis=1), basis_ref[...]))
-    energy_row = jnp.sum(rows * rows, axis=0, keepdims=True)
-    nyquist_row = jnp.sum(rows * alternating(rows.shape, 0), axis=0, keepdims=True)
-    pair = jnp.concatenate(split(rows), axis=1)
-    both = fold(dot(down_ref[...], jnp.concatenate([pair, pair], axis=0)))
-    first, second = both[:PATCH], both[PATCH:]
+def forward_patches(patches, basis, down):
+    count = len(patches)
+    values = [patch.astype(f32) for patch in patches]
+    totals = [jnp.sum(jnp.sum(value, axis=0, keepdims=True), axis=1, keepdims=True) for value in values]
+    values = [value - total * (1.0 / (PATCH * PATCH)) for value, total in zip(values, totals)]
+    left = jnp.concatenate([jnp.concatenate(split(value), axis=1) for value in values], axis=0)
+    rows = fold(dot(left, basis))
+    rows = [rows[k * PATCH : (k + 1) * PATCH] for k in range(count)]
+    pairs = [jnp.concatenate(split(row), axis=1) for row in rows]
+    both = [fold(dot(down, jnp.concatenate([pair, pair], axis=0))) for pair in pairs]
     lane = lanes((1, PATCH))
     sigma = jnp.where(lane > HALF, 1.0, -1.0) * jnp.where(lane % HALF == 0, 0.0, 1.0)
-    real = first + sigma * pltpu.roll(second, HALF, 1)
-    imag = second - sigma * pltpu.roll(first, HALF, 1)
-    return real, imag, energy_row, nyquist_row
-
-
-def spectra_kernel(cols, stage, *refs):
-    here_ref, beside_ref, tables_ref = refs[:3]
-    basis_ref, down_ref, up_ref = [tables_ref.at[k] for k in range(3)]
-    real_ref, imag_ref, row_ref, base_ref = refs[-4:]
-    if stage == 0:
-        row_ref[...] = jnp.zeros(row_ref.shape, f32)
+    sign = alternating((PATCH, PATCH), 0)
+    result = []
+    for row, wide in zip(rows, both):
+        first, second = wide[:PATCH], wide[PATCH:]
+        real = first + sigma * pltpu.roll(second, HALF, 1)
+        imag = second - sigma * pltpu.roll(first, HALF, 1)
+        energy_row = jnp.sum(row * row, axis=0, keepdims=True)
+        nyquist_row = jnp.sum(row * sign, axis=0, keepdims=True)
+        result.append((real, imag, energy_row, nyquist_row))
+    return result
+
+
+def slot_of(name):
     sec = lax.axis_index("sec")
     core = lax.rem(sec, 2)
     odd = lax.rem(sec // 2, 2)
+    source, swapped = name
+    if swapped:
+        core = 1 - core
+    if source == "own":
+        return HALO + core
+    if source == "a":
+        return 5 - 4 * odd + core
+    if source == "b":
+        return 1 + 4 * odd + core
+    return (WINDOW - 1) * core
+
+
+def spectra_kernel(cols, names, pairs, starts, *refs):
+    blocks, tables_ref = refs[: len(names)], refs[len(names)]
+    basis_ref, down_ref, up_ref = [tables_ref.at[k] for k in range(3)]
+    real_ref, imag_ref, row_ref, base_ref = refs[-4:]
+    if starts:
+        row_ref[...] = jnp.zeros(row_ref.shape, f32)
     half = half_of()
-    if stage == 0:
-        slots = (HALO + core, HALO + 1 - core)
-        pairs = (HALO,)
-    elif stage == 1:
-        slots = (5 - 4 * odd + core, 6 - 4 * odd - core)
-        pairs = (4 - 3 * odd, 5 - 3 * odd)
-    elif stage == 2:
-        slots = (1 + 4 * odd + core, 2 + 4 * odd - core)
-        pairs = (1 + 3 * odd, 2 + 3 * odd)
-    else:
-        slots = ((WINDOW - 1) * core, (WINDOW - 1) * (1 - core))
-        pairs = (0, WINDOW - 2)
-    for block, slot in zip((here_ref, beside_ref), slots):
-        for col in range(cols):
-            start = pl.multiple_of((half * cols + col) * PATCH, PATCH)
-            real, imag, energy_row, nyquist_row = forward_patch(
-                block[:PATCH, pl.ds(start, PATCH)], basis_ref, down_ref
-            )
-            real_ref[slot, col] = real
-            imag_ref[slot, col] = imag
-            row_ref[col, 0, pl.ds(slot, 1), :] = energy_row
-            row_ref[col, 1, pl.ds(slot, 1), :] = nyquist_row
-            small = block[PATCH:, pl.ds(start, PATCH)].astype(f32)
-            for dim in range(2):
-                shift = small[3 * dim : 3 * dim + 1] + small[3 * dim + 1 : 3 * dim + 2] + small[3 * dim + 2 : 3 * dim + 3]
-                row_ref[col, 2 + dim, pl.ds(slot, 1), :] = shift
-                row_ref[col, 4 + dim, pl.ds(slot, 1), :] = small[6 + dim : 7 + dim]
+    slots = [slot_of(name) for name in names]
+    places = [(block, slot, col) for block, slot in zip(blocks, slots) for col in range(cols)]
+    starts = [pl.multiple_of((half * cols + col) * PATCH, PATCH) for col in range(cols)]
+    patches = [block[:PATCH, pl.ds(starts[col], PATCH)] for block, slot, col in places]
+    results = forward_patches(patches, basis_ref[...], down_ref[...])
+    for (block, slot, col), (real, imag, energy_row, nyquist_row) in zip(places, results):
+        real_ref[slot, col] = real
+        imag_ref[slot, col] = imag
+        row_ref[col, 0, pl.ds(slot, 1), :] = energy_row
+        row_ref[col, 1, pl.ds(slot, 1), :] = nyquist_row
+        small = block[PATCH:, pl.ds(starts[col], PATCH)].astype(f32)
+        for dim in range(2):
+            shift = small[3 * dim : 3 * dim + 1] + small[3 * dim + 1 : 3 * dim + 2] + small[3 * dim + 2 : 3 * dim + 3]
+            row_ref[col, 2 + dim, pl.ds(slot, 1), :] = shift
+            row_ref[col, 4 + dim, pl.ds(slot, 1), :] = small[6 + dim : 7 + dim]
     low_lane = lanes((1, PATCH)) <= HALF
+    products = []
     for pair in pairs:
         for col in range(cols):
             sr, si = real_ref[pair, col], imag_ref[pair, col]
@@ -179,9 +183,11 @@
             cross = si * nr - sr * ni
             top = jnp.concatenate(split(jnp.where(low_lane, same, cross)), axis=1)
             bottom = jnp.concatenate(split(jnp.where(low_lane, cross, -same)), axis=1)
-            wide = fold(dot(up_ref[...], jnp.concatenate([top, bottom], axis=0)))
-            base = wide[:PATCH] + wide[PATCH:]
-            base_ref[col, pair] = jnp.concatenate(split(base), axis=1)
+            products.append(jnp.concatenate([top, bottom], axis=0))
+    wides = [fold(dot(up_ref[...], product)) for product in products]
+    bases = [jnp.concatenate(split(wide[:PATCH] + wide[PATCH:]), axis=1) for wide in wides]
+    for k, base in enumerate(bases):
+        base_ref[k % cols, pairs[k // cols]] = base
 
 
 def energies(row_ref, col):
@@ -203,18 +209,34 @@
     return bulk, row_energy, col_energy, corner_energy, corner
 
 
-def cos_sin_turns(turns):
-    rest = turns - jnp.round(turns)
-    z = rest * math.pi
+def sine_cosine(z):
     zz = z * z
     sine = jnp.full_like(z, 1.0 / 6227020800.0)
     for factor in (-1.0 / 39916800.0, 1.0 / 362880.0, -1.0 / 5040.0, 1.0 / 120.0, -1.0 / 6.0, 1.0):
         sine = sine * zz + factor
-    sine = sine * z
     cosine = jnp.full_like(z, 1.0 / 479001600.0)
     for factor in (-1.0 / 3628800.0, 1.0 / 40320.0, -1.0 / 720.0, 1.0 / 24.0, -0.5, 1.0):
         cosine = cosine * zz + factor
+    return sine * z, cosine
+
+
+def cos_sin_turns(turns):
+    sine, cosine = sine_cosine((turns - jnp.round(turns)) * math.pi)
     return 1.0 - 2.0 * sine * sine, 2.0 * sine * cosine
+
+
+def shift_row(delta, gamma, lane):
+    whole = jnp.round(delta)
+    rest = delta - whole
+    lag = lane.astype(f32) + whole
+    lag = lag - PATCH * jnp.round(lag * (1.0 / PATCH))
+    parity = (1 - 2 * (lag.astype(jnp.int32) & 1)).astype(f32)
+    top, bottom = sine_cosine(rest * math.pi)
+    sine, cosine = sine_cosine((lag + rest) * (math.pi / PATCH))
+    centre = sine == 0.0
+    ratio = jnp.where(centre, float(PATCH), top) / jnp.where(centre, 1.0, sine)
+    nyquist = (1 - 2 * (lane & 1)).astype(f32) * gamma
+    return (parity * (ratio * cosine - bottom) + nyquist) * (1.0 / PATCH)
 
 
 def next_section(values):
@@ -265,8 +287,7 @@
 
 
 def iteration_kernel(cols, first, last, starts, n_vertical, *refs):
-    base_ref, row_ref, tables_ref = refs[:3]
-    kernel_ref, back_ref = tables_ref.at[0], tables_ref.at[1]
+    base_ref, row_ref, back_ref = refs[:3]
     refs = refs[3:]
     core = lax.rem(lax.axis_index("sec"), 2)
     half = half_of()
@@ -299,10 +320,7 @@
         gamma = cos_both * next_section(cos_both)
         corner = nyquist * next_section(nyquist) * (1.0 / (PATCH * PATCH))
         ripple.append((gamma - gamma_y * gamma_x) * corner * scale)
-        cosine, sine = cos_sin_turns((dy - next_section(dy)) * frequency)
-        harmonics = jnp.where(high_lane, sine, cosine) * 2.0
-        harmonics = jnp.where(lane == 0, 1.0, jnp.where(nyquist_lane, gamma_y, harmonics))
-        rows.append(fold(dot(jnp.concatenate(split(harmonics), axis=1), kernel_ref[...])))
+        rows.append(shift_row(dy - next_section(dy), gamma_y, lane))
         cosine, sine = cos_sin_turns((dx - next_section(dx)) * frequency)
         turn_cos.append(jnp.where(nyquist_lane, gamma_x, cosine) * scale)
         turn_sin.append(jnp.where(zero_lane, 0.0, jnp.where(high_lane, -sine, sine)) * scale)
@@ -314,21 +332,31 @@
         total_ref[col] = jnp.ones((WINDOW, PATCH), f32)
         moment_ref[col] = jnp.zeros((WINDOW, PATCH), f32)
         edge_ref[col] = jnp.zeros((WINDOW, PATCH), f32)
-    for pair in range(first, last):
-        for col in range(cols):
+    tasks = [(pair, col) for pair in range(first, last) for col in range(cols)]
+    size = -(-len(tasks) // -(-len(tasks) // GROUP))
+    for at in range(0, len(tasks), size):
+        group = tasks[at : at + size]
+        moved = []
+        for pair, col in group:
             row = slice(pair, pair + 1)
             shifter = pltpu.roll(jnp.broadcast_to(rows[col][row], (PATCH, PATCH)), 0, 1, stride=1, stride_axis=0)
             base = base_ref[col, pair]
-            moved = fold(dot(jnp.concatenate(split(shifter), axis=1), jnp.concatenate([base, base], axis=0)))
-            moved = moved * turn_cos[col][row] + pltpu.roll(moved, HALF, 1) * turn_sin[col][row]
-            scores = fold(dot(jnp.concatenate(split(moved), axis=1), back_ref[...]))
-            scores = scores.reshape(blocks, WINDOW, PATCH) + (ripple[col][row] * checker)[None]
-            weights = jnp.exp2(scores)
+            moved.append(fold(dot(jnp.concatenate(split(shifter), axis=1), jnp.concatenate([base, base], axis=0))))
+        turned = []
+        for (pair, col), value in zip(group, moved):
+            row = slice(pair, pair + 1)
+            value = value * turn_cos[col][row] + pltpu.roll(value, HALF, 1) * turn_sin[col][row]
+            turned.append(jnp.concatenate(split(value), axis=1))
+        wide = fold(dot(jnp.concatenate(turned, axis=0), back_ref[...]))
+        for k, (pair, col) in enumerate(group):
+            row = slice(pair, pair + 1)
+            scores = wide[k * PATCH : (k + 1) * PATCH].reshape(blocks, WINDOW, PATCH)
+            weights = jnp.exp2(scores + (ripple[col][row] * checker)[None])
             total = weights[0]
             moment = weights[0] * float(block_lag[0])
-            for k in range(1, blocks):
-                total = total + weights[k]
-                moment = moment + weights[k] * float(block_lag[k])
+            for m in range(1, blocks):
+                total = total + weights[m]
+                moment = moment + weights[m] * float(block_lag[m])
             moment = moment + row_in_block * total
             total_ref[col, row, :] = jnp.sum(total, axis=0, keepdims=True)
             moment_ref[col, row, :] = jnp.sum(moment, axis=0, keepdims=True)
@@ -412,7 +440,7 @@
     assert section_images.shape[:2] == (1, PATCH)
     cols = patch_cols // 2
     chips = n_sec // 2
-    spectrum_tables, shift_tables = [jnp.asarray(table) for table in tables()]
+    spectrum_tables, back_table = [jnp.asarray(table) for table in tables()]
 
     def sections(pairs):
         return [(2 * a + c, 2 * b + c) for a, b in pairs for c in range(2)]
@@ -436,29 +464,39 @@
             pltpu.SemaphoreType.DMA((3,)),
         ],
         compiler_params=limit(4),
+        cost_estimate=pl.CostEstimate(flops=0, bytes_accessed=8000000, transcendentals=0),
         name="pack",
     )(*[pltpu.with_memory_space_constraint(x, pltpu.HBM) for x in (displacement, fold_mask, section_images)])
-    received = [payload]
-    for perm in (swap_a, swap_b, far):
-        received.append(lax.ppermute(payload, "sec", perm))
+    blocks = {("own", 0): payload}
+    for source, perm in (("a", swap_a), ("b", swap_b), ("far", far)):
+        blocks[source, 0] = lax.ppermute(payload, "sec", perm)
+    for source in ("own", "a", "b", "far"):
+        blocks[source, 1] = between_cores(blocks[source, 0])
     state = []
-    for stage, block in enumerate(received):
-        beside = between_cores(block)
+    every = tuple(range(WINDOW - 1))
+    for stage, (names, pairs) in enumerate(
+        (
+            ((("own", 0), ("own", 1)), (HALO,)),
+            ((("a", 0),), ()),
+            ((("b", 0), ("far", 0)), ()),
+            ((("a", 1), ("b", 1), ("far", 1)), every[:HALO] + every[HALO + 1 :]),
+        )
+    ):
         state = pl.pallas_call(
-            lambda *refs, stage=stage: spectra_kernel(cols, stage, *refs),
+            lambda *refs, names=names, pairs=pairs, stage=stage: spectra_kernel(cols, names, pairs, stage == 0, *refs),
             out_shape=(
                 jax.ShapeDtypeStruct((WINDOW, cols, PATCH, PATCH), f32),
                 jax.ShapeDtypeStruct((WINDOW, cols, PATCH, PATCH), f32),
                 jax.ShapeDtypeStruct((cols, 6, WINDOW, PATCH), f32),
                 jax.ShapeDtypeStruct((cols, WINDOW - 1, PATCH, 2 * PATCH), bf16),
             ),
-            in_specs=[vmem()] * (3 + len(state)),
+            in_specs=[vmem()] * (len(names) + 1 + len(state)),
             out_specs=[vmem()] * 4,
-            input_output_aliases={3 + k: k for k in range(len(state))},
+            input_output_aliases={len(names) + 1 + k: k for k in range(len(state))},
             compiler_params=limit(16),
             cost_estimate=pl.CostEstimate(flops=500000000, bytes_accessed=1000000, transcendentals=0),
             name="spectra",
-        )(block, beside, spectrum_tables, *state)
+        )(*[blocks[name] for name in names], spectrum_tables, *state)
     base, stats = state[3], state[2]
 
     row_perms = [swap([(r, r + 1) for r in range(0, n_row - 1, 2)])]
@@ -479,7 +517,7 @@
             scratch_shapes=[pltpu.VMEM((cols, WINDOW, PATCH), f32)] * 3,
             compiler_params=limit(8),
             name="iteration",
-        )(base, stats, shift_tables, *messages)
+        )(base, stats, back_table, *messages)
         beside = between_cores(out)
         rows = [diagonal(out, perm) for perm in row_perms]
         messages = [out, beside] + rows

time: 35.3 us -> 33.9 us (0.960)
  Pallas kernels: 9.87 us -> 8.46 us
    pallas_call x4, Pallas kernels: 4.81 us -> 3.72 us  [per_device(): pl.pallas_call(lambda *refs, names=names, pairs=pairs, stage=stage: spect...]
  transfers between devices with their start and end apart: 14 -> 14, of which waited for: 7 -> 7; matrix products, arithmetic and copies ran while one was open for 0% -> 0% of each run, Pallas kernels for 10% -> 7%
where the time goes in v2:
time: 33.9 us; the launch traced here: 33.7 us
  starting transfers between devices  12.9 us (38%)
  waiting for transfers between devices  10.5 us (31%)
  Pallas kernels  8.46 us (25%)
  local copies, waits for them, and re-layouts  1 us (3%)
  between operations  0.76 us (2%)
    ppermute x3, starting transfers between devices, per_device(): blocks[source, 0] = lax.ppermute(payload, 'sec', perm)  6.92 us
    ppermute x3, waiting for transfers between devices, diagonal(): return lax.ppermute(x, ('sec', 'row'), pairs)  4.28 us
    ppermute x3, waiting for transfers between devices, per_device(): blocks[source, 0] = lax.ppermute(payload, 'sec', perm)  4.16 us
    ppermute x3, starting transfers between devices, diagonal(): return lax.ppermute(x, ('sec', 'row'), pairs)  3.95 us
    pallas_call x4, Pallas kernels, per_device(): pl.pallas_call(lambda *refs, names=names, pairs=pairs, stage=stage: spect...  3.72 us
    pallas_call x3, Pallas kernels, per_device(): pl.pallas_call(lambda *refs, step=step: iteration_kernel(cols, step, WIND...  3.14 us
    ppermute x1, waiting for transfers between devices, per_device(): straight = [lax.ppermute(out, 'row', perm) for perm in row_perms]  2.07 us
    ppermute x7, starting transfers between devices, between_cores(): return lax.ppermute(x, 'sec', cores)  1.52 us
  transfers between devices with their start and end apart: 14, of which 7 were waited for; matrix products, arithmetic and copies ran while one was open for 0% of the time, Pallas kernels for 7%

profile of v2, /device:TPU:20, one launch (start us, length us, event | category | flops | bytes accessed | tf_op | source)
XLA Modules:
  0.0 33.7 jit_solution(17987233554579765667)
XLA Ops:
  0.6 0.9 %pack.1.refs_0_ = bf16[144,512]{1,0:T(8,128)(2,1)S(1)} custom-call(f32[2,1,1,4]{3,2,1,0:T(1,128)} %shift_ref.1, s32[2,1,1,4]{3,2,1,0:T(1,128)} %mask_ref.1, bf16[1,128,512]{2,1,0:T(8,128)(2,1)} %image_ref.1), custom_call_target="tpu_custom_call" | custom-call | bytes 8000000 | tf_op jit(solution)/shard_map/pack/pallas_call | solution.py:456
  1.6 0.6 %collective-permute-start = (bf16[144,512]{1,0:T(8,128)(2,1)S(1)}, bf16[144,512]{1,0:T(8,128)(2,1)S(1)}, u32[]{:S(2)}, u32[]{:S(2)}) collective-permute-start(bf16[144,512]{1,0:T(8,128)(2,1)S(1)} %pack.1.refs_0_), channel_id=1, source_target_pairs={{0,4},{2,6},{8,12},{10,14},{16,20},{18,22},{24,28},{26,30},{4,0},{... | collective-permute-start | bytes 442376 | tf_op jit(solution)/shard_map/ppermute | solution.py:472
  2.1 4.4 %collective-permute-start.2 = (bf16[144,512]{1,0:T(8,128)(2,1)S(1)}, bf16[144,512]{1,0:T(8,128)(2,1)S(1)}, u32[]{:S(2)}, u32[]{:S(2)}) collective-permute-start(bf16[144,512]{1,0:T(8,128)(2,1)S(1)} %pack.1.refs_0_), channel_id=1, source_target_pairs={{4,8},{6,10},{12,16},{14,18},{20,24},{22,26},{8,4},{10,6},{16,12},... | collective-permute-start | bytes 442376 | tf_op jit(solution)/shard_map/ppermute | solution.py:472
  6.6 1.9 %collective-permute-start.4 = (bf16[144,512]{1,0:T(8,128)(2,1)S(1)}, bf16[144,512]{1,0:T(8,128)(2,1)S(1)}, u32[]{:S(2)}, u32[]{:S(2)}) collective-permute-start(bf16[144,512]{1,0:T(8,128)(2,1)S(1)} %pack.1.refs_0_), channel_id=1, source_target_pairs={{2,8},{6,12},{10,16},{14,20},{18,24},{22,28},{8,2},{12,6},{16,10},... | collective-permute-start | bytes 442376 | tf_op jit(solution)/shard_map/ppermute | solution.py:472
  8.5 0.1 collective-permute-start.6
  8.6 1.8 %collective-permute-done.refs_0_ = bf16[144,512]{1,0:T(8,128)(2,1)S(1)} collective-permute-done((bf16[144,512]{1,0:T(8,128)(2,1)S(1)}, bf16[144,512]{1,0:T(8,128)(2,1)S(1)}, u32[]{:S(2)}, u32[]{:S(2)}) %collective-permute-start) | collective-permute-done | bytes 147488 | tf_op jit(solution)/shard_map/ppermute | solution.py:472
  10.4 0.0 collective-permute-start.1
  10.4 0.2 collective-permute-done.2.refs_0_
  10.6 0.3 collective-permute-start.3
  10.9 2.1 %collective-permute-done.4.refs_1_ = bf16[144,512]{1,0:T(8,128)(2,1)S(1)} collective-permute-done((bf16[144,512]{1,0:T(8,128)(2,1)S(1)}, bf16[144,512]{1,0:T(8,128)(2,1)S(1)}, u32[]{:S(2)}, u32[]{:S(2)}) %collective-permute-start.4) | collective-permute-done | bytes 147488 | tf_op jit(solution)/shard_map/ppermute | solution.py:472
  13.0 0.0 collective-permute-start.5
  13.0 0.0 collective-permute-done.6.refs_1_
  13.0 0.0 copy-start
  13.1 1.0 %copy-done = bf16[3,256,256]{2,1,0:T(8,128)(2,1)S(1)} copy-done((bf16[3,256,256]{2,1,0:T(8,128)(2,1)S(1)}, bf16[3,256,256]{2,1,0:T(8,128)(2,1)}, u32[]{:S(2)}) %copy-start) | copy-done | bytes 393240
  14.0 1.0 %spectra.4 = (f32[8,2,128,128]{3,2,1,0:T(8,128)S(1)}, f32[8,2,128,128]{3,2,1,0:T(8,128)S(1)}, f32[2,6,8,128]{3,2,1,0:T(8,128)S(1)}, bf16[2,7,128,256]{3,2,1,0:T(8,128)(2,1)S(1)}) custom-call(bf16[144,512]{1,0:T(8,128)(2,1)S(1)} %pack.1.refs_0_, bf16[144,512]{1,0:T(8,128)(2,1)S(1)} %collective-permute-done.6.refs_1_, bf16[3,256,256]{2,1,0:T(8,128)(2,1)S(1)} %copy-done), custom_call_target="tpu_custom_call" | custom-call | flops 500000000 | bytes 1000000 | tf_op jit(solution)/shard_map/spectra/pallas_call | solution.py:485
  15.0 0.6 %spectra.5 = (f32[8,2,128,128]{3,2,1,0:T(8,128)S(1)}, f32[8,2,128,128]{3,2,1,0:T(8,128)S(1)}, f32[2,6,8,128]{3,2,1,0:T(8,128)S(1)}, bf16[2,7,128,256]{3,2,1,0:T(8,128)(2,1)S(1)}) custom-call(bf16[144,512]{1,0:T(8,128)(2,1)S(1)} %collective-permute-done.refs_0_, ...), custom_call_target="tpu_custom_call", output_to_operand_aliasing={{0}: (2, {}), {1}: (3, {}), {2}: (4, {}), {3}: (5, {})} | custom-call | flops 500000000 | bytes 1000000 | tf_op jit(solution)/shard_map/spectra/pallas_call | solution.py:485
  15.6 0.7 %spectra.6 = (f32[8,2,128,128]{3,2,1,0:T(8,128)S(1)}, f32[8,2,128,128]{3,2,1,0:T(8,128)S(1)}, f32[2,6,8,128]{3,2,1,0:T(8,128)S(1)}, bf16[2,7,128,256]{3,2,1,0:T(8,128)(2,1)S(1)}) custom-call(bf16[144,512]{1,0:T(8,128)(2,1)S(1)} %collective-permute-done.2.refs_0_, ...), custom_call_target="tpu_custom_call", output_to_operand_aliasing={{0}: (3, {}), {1}: (4, {}), {2}: (5, {}), {3}: (6, {})} | custom-call | flops 500000000 | bytes 1000000 | tf_op jit(solution)/shard_map/spectra/pallas_call | solution.py:485
  16.3 0.0 collective-permute-done.1.refs_0_
  16.3 0.0 collective-permute-done.3.refs_1_
  16.3 0.0 collective-permute-done.5.refs_2_
  16.3 0.0 copy-start.1
  16.3 1.5 %spectra.7 = (f32[8,2,128,128]{3,2,1,0:T(8,128)S(1)}, f32[8,2,128,128]{3,2,1,0:T(8,128)S(1)}, f32[2,6,8,128]{3,2,1,0:T(8,128)S(1)}, bf16[2,7,128,256]{3,2,1,0:T(8,128)(2,1)S(1)}) custom-call(bf16[144,512]{1,0:T(8,128)(2,1)S(1)} %collective-permute-done.1.refs_0_, ...), custom_call_target="tpu_custom_call", output_to_operand_aliasing={{0}: (4, {}), {1}: (5, {}), {2}: (6, {}), {3}: (7, {})} | custom-call | flops 500000000 | bytes 1000000 | tf_op jit(solution)/shard_map/spectra/pallas_call | solution.py:485
  17.8 0.0 copy-done.1
  17.8 1.2 %iteration.3.refs_3_ = f32[8,128]{1,0:T(8,128)S(1)} custom-call(bf16[2,7,128,256]{3,2,1,0:T(8,128)(2,1)S(1)} %get-tuple-element.28.refs_0_, f32[2,6,8,128]{3,2,1,0:T(8,128)S(1)} %get-tuple-element.29.refs_1_, bf16[256,256]{1,0:T(8,128)(2,1)S(1)} %copy-done.1), custom_call_target="tpu_custom_call" | custom-call | tf_op jit(solution)/shard_map/iteration/pallas_call | solution.py:512
  19.0 0.6 %collective-permute-start.7 = (f32[8,128]{1,0:T(8,128)S(1)}, f32[8,128]{1,0:T(8,128)S(1)}, u32[]{:S(2)}, u32[]{:S(2)}) collective-permute-start(f32[8,128]{1,0:T(8,128)S(1)} %iteration.3.refs_3_), channel_id=1, source_target_pairs={{0,2},{4,6},{8,10},{12,14},{16,18},{20,22},{24,26},{28,30},{2,0},{... | collective-permute-start | bytes 12296 | tf_op jit(solution)/shard_map/ppermute | solution.py:454
  19.6 1.2 %collective-permute-start.8 = (f32[8,128]{1,0:T(8,128)S(1)}, f32[8,128]{1,0:T(8,128)S(1)}, u32[]{:S(2)}, u32[]{:S(2)}) collective-permute-start(f32[8,128]{1,0:T(8,128)S(1)} %iteration.3.refs_3_), channel_id=1, source_target_pairs={{0,3},{1,2},{4,7},{5,6},{8,11},{9,10},{12,15},{13,14},{16,19},{17,... | collective-permute-start | bytes 12296 | tf_op jit(solution)/shard_map/ppermute | solution.py:508
  20.8 0.0 collective-permute-done.7.refs_4_
  20.8 1.9 %collective-permute-done.8.refs_5_ = f32[8,128]{1,0:T(8,128)S(1)} collective-permute-done((f32[8,128]{1,0:T(8,128)S(1)}, f32[8,128]{1,0:T(8,128)S(1)}, u32[]{:S(2)}, u32[]{:S(2)}) %collective-permute-start.8) | collective-permute-done | bytes 4128 | tf_op jit(solution)/shard_map/ppermute | solution.py:508
  22.6 1.1 %iteration.4.refs_3_ = f32[8,128]{1,0:T(8,128)S(1)} custom-call(bf16[2,7,128,256]{3,2,1,0:T(8,128)(2,1)S(1)} %get-tuple-element.28.refs_0_, f32[2,6,8,128]{3,2,1,0:T(8,128)S(1)} %get-tuple-element.29.refs_1_, bf16[256,256]{1,0:T(8,128)(2,1)S(1)} %copy-done.1, f32[8,128]{1,0:T(8,128)S(1)} %iteration.3.refs_3_, f32[8,128]{1,0:T(8,128)S(1)} %collective-permute-done.7.refs_4_, ...), custom_call_target="tpu_custom_call" | custom-call | tf_op jit(solution)/shard_map/iteration/pallas_call | solution.py:512
  23.8 1.3 %collective-permute-start.10 = (f32[8,128]{1,0:T(8,128)S(1)}, f32[8,128]{1,0:T(8,128)S(1)}, u32[]{:S(2)}, u32[]{:S(2)}) collective-permute-start(f32[8,128]{1,0:T(8,128)S(1)} %iteration.4.refs_3_), channel_id=1, source_target_pairs={{0,3},{1,2},{4,7},{5,6},{8,11},{9,10},{12,15},{13,14},{16,19},{17,... | collective-permute-start | bytes 12296 | tf_op jit(solution)/shard_map/ppermute | solution.py:508
  25.1 0.4 %collective-permute-start.9 = (f32[8,128]{1,0:T(8,128)S(1)}, f32[8,128]{1,0:T(8,128)S(1)}, u32[]{:S(2)}, u32[]{:S(2)}) collective-permute-start(f32[8,128]{1,0:T(8,128)S(1)} %iteration.4.refs_3_), channel_id=1, source_target_pairs={{0,2},{4,6},{8,10},{12,14},{16,18},{20,22},{24,26},{28,30},{2,0},{... | collective-permute-start | bytes 12296 | tf_op jit(solution)/shard_map/ppermute | solution.py:454
  25.5 1.4 %collective-permute-done.10.refs_5_ = f32[8,128]{1,0:T(8,128)S(1)} collective-permute-done((f32[8,128]{1,0:T(8,128)S(1)}, f32[8,128]{1,0:T(8,128)S(1)}, u32[]{:S(2)}, u32[]{:S(2)}) %collective-permute-start.10) | collective-permute-done | bytes 4128 | tf_op jit(solution)/shard_map/ppermute | solution.py:508
  26.9 0.0 collective-permute-done.9.refs_4_
  26.9 0.8 %iteration.5.refs_0_ = f32[8,128]{1,0:T(8,128)S(1)} custom-call(bf16[2,7,128,256]{3,2,1,0:T(8,128)(2,1)S(1)} %get-tuple-element.28.refs_0_, f32[2,6,8,128]{3,2,1,0:T(8,128)S(1)} %get-tuple-element.29.refs_1_, bf16[256,256]{1,0:T(8,128)(2,1)S(1)} %copy-done.1, f32[8,128]{1,0:T(8,128)S(1)} %iteration.4.refs_3_, f32[8,128]{1,0:T(8,128)S(1)} %collective-permute-done.9.refs_4_, ...), custom_call_target="tpu_custom_call" | custom-call | tf_op jit(solution)/shard_map/iteration/pallas_call | solution.py:512
  27.7 0.2 collective-permute-start.11
  27.9 1.5 %collective-permute-start.12 = (f32[8,128]{1,0:T(8,128)S(1)}, f32[8,128]{1,0:T(8,128)S(1)}, u32[]{:S(2)}, u32[]{:S(2)}) collective-permute-start(f32[8,128]{1,0:T(8,128)S(1)} %iteration.5.refs_0_), channel_id=1, source_target_pairs={{0,3},{1,2},{4,7},{5,6},{8,11},{9,10},{12,15},{13,14},{16,19},{17,... | collective-permute-start | bytes 12296 | tf_op jit(solution)/shard_map/ppermute | solution.py:508
  29.4 0.5 %collective-permute-start.13 = (f32[8,128]{1,0:T(8,128)S(1)}, f32[8,128]{1,0:T(8,128)S(1)}, u32[]{:S(2)}, u32[]{:S(2)}) collective-permute-start(f32[8,128]{1,0:T(8,128)S(1)} %iteration.5.refs_0_), channel_id=1, source_target_pairs={{0,1},{1,0},{2,3},{3,2},{4,5},{5,4},{6,7},{7,6},{8,9},{9,8},{10,11... | collective-permute-start | bytes 12296 | tf_op jit(solution)/shard_map/ppermute | solution.py:524
  29.9 0.0 collective-permute-done.11.refs_1_
  29.9 1.0 %collective-permute-done.12.refs_2_ = f32[8,128]{1,0:T(8,128)S(1)} collective-permute-done((f32[8,128]{1,0:T(8,128)S(1)}, f32[8,128]{1,0:T(8,128)S(1)}, u32[]{:S(2)}, u32[]{:S(2)}) %collective-permute-start.12) | collective-permute-done | bytes 4128 | tf_op jit(solution)/shard_map/ppermute | solution.py:508
  30.9 2.1 %collective-permute-done.13.refs_3_ = f32[8,128]{1,0:T(8,128)S(1)} collective-permute-done((f32[8,128]{1,0:T(8,128)S(1)}, f32[8,128]{1,0:T(8,128)S(1)}, u32[]{:S(2)}, u32[]{:S(2)}) %collective-permute-start.13) | collective-permute-done | bytes 4128 | tf_op jit(solution)/shard_map/ppermute | solution.py:524
  33.0 0.7 %final.1 = (f32[2,1,1,4]{3,2,1,0:T(1,128)}, f32[2,1,1,4]{3,2,1,0:T(1,128)}) custom-call(f32[8,128]{1,0:T(8,128)S(1)} %iteration.5.refs_0_, f32[8,128]{1,0:T(8,128)S(1)} %collective-permute-done.11.refs_1_, f32[8,128]{1,0:T(8,128)S(1)} %collective-permute-done.12.refs_2_, f32[8,128]{1,0:T(8,128)S(1)} %collective-permute-done.13.refs_3_), custom_call_target="tpu_custom_call" | custom-call | tf_op jit(solution)/shard_map/final/pallas_call | solution.py:527
Async XLA Ops:
  1.6 8.8 %collective-permute-start = (bf16[144,512]{1,0:T(8,128)(2,1)S(1)}, bf16[144,512]{1,0:T(8,128)(2,1)S(1)}, u32[]{:S(2)}, u32[]{:S(2)}) collective-permute-start(bf16[144,512]{1,0:T(8,128)(2,1)S(1)} %pack.1.refs_0_), channel_id=1, source_target_pairs={{0,4},{2,6},{8,12},{10,14},{16,20},{18,22},{24,28},{26,30},{4,0},{... | collective-permute-start | bytes 442376 | tf_op jit(solution)/shard_map/ppermute | solution.py:472
  2.1 8.5 %collective-permute-start.2 = (bf16[144,512]{1,0:T(8,128)(2,1)S(1)}, bf16[144,512]{1,0:T(8,128)(2,1)S(1)}, u32[]{:S(2)}, u32[]{:S(2)}) collective-permute-start(bf16[144,512]{1,0:T(8,128)(2,1)S(1)} %pack.1.refs_0_), channel_id=1, source_target_pairs={{4,8},{6,10},{12,16},{14,18},{20,24},{22,26},{8,4},{10,6},{16,12},... | collective-permute-start | bytes 442376 | tf_op jit(solution)/shard_map/ppermute | solution.py:472
  6.6 6.5 %collective-permute-start.4 = (bf16[144,512]{1,0:T(8,128)(2,1)S(1)}, bf16[144,512]{1,0:T(8,128)(2,1)S(1)}, u32[]{:S(2)}, u32[]{:S(2)}) collective-permute-start(bf16[144,512]{1,0:T(8,128)(2,1)S(1)} %pack.1.refs_0_), channel_id=1, source_target_pairs={{2,8},{6,12},{10,16},{14,20},{18,24},{22,28},{8,2},{12,6},{16,10},... | collective-permute-start | bytes 442376 | tf_op jit(solution)/shard_map/ppermute | solution.py:472
  8.5 4.5 %collective-permute-start.6 = (bf16[144,512]{1,0:T(8,128)(2,1)S(1)}, bf16[144,512]{1,0:T(8,128)(2,1)S(1)}, u32[]{:S(2)}, u32[]{:S(2)}) collective-permute-start(bf16[144,512]{1,0:T(8,128)(2,1)S(1)} %pack.1.refs_0_), channel_id=1, source_target_pairs={{0,2},{4,6},{8,10},{12,14},{16,18},{20,22},{24,26},{28,30},{2,0},{... | collective-permute-start | bytes 442376 | tf_op jit(solution)/shard_map/ppermute | solution.py:454
  10.4 5.9 %collective-permute-start.1 = (bf16[144,512]{1,0:T(8,128)(2,1)S(1)}, bf16[144,512]{1,0:T(8,128)(2,1)S(1)}, u32[]{:S(2)}, u32[]{:S(2)}) collective-permute-start(bf16[144,512]{1,0:T(8,128)(2,1)S(1)} %collective-permute-done.refs_0_), channel_id=1, source_target_pairs={{0,2},{4,6},{8,10},{12,14},{16,18},{20,22},{24,26},{28,30},{2,0},{... | collective-permute-start | bytes 442376 | tf_op jit(solution)/shard_map/ppermute | solution.py:454
  10.6 5.7 %collective-permute-start.3 = (bf16[144,512]{1,0:T(8,128)(2,1)S(1)}, bf16[144,512]{1,0:T(8,128)(2,1)S(1)}, u32[]{:S(2)}, u32[]{:S(2)}) collective-permute-start(bf16[144,512]{1,0:T(8,128)(2,1)S(1)} %collective-permute-done.2.refs_0_), channel_id=1, source_target_pairs={{0,2},{4,6},{8,10},{12,14},{16,18},{20,22},{24,26},{28,30},{2,0},{... | collective-permute-start | bytes 442376 | tf_op jit(solution)/shard_map/ppermute | solution.py:454
  13.0 3.3 %collective-permute-start.5 = (bf16[144,512]{1,0:T(8,128)(2,1)S(1)}, bf16[144,512]{1,0:T(8,128)(2,1)S(1)}, u32[]{:S(2)}, u32[]{:S(2)}) collective-permute-start(bf16[144,512]{1,0:T(8,128)(2,1)S(1)} %collective-permute-done.4.refs_1_), channel_id=1, source_target_pairs={{0,2},{4,6},{8,10},{12,14},{16,18},{20,22},{24,26},{28,30},{2,0},{... | collective-permute-start | bytes 442376 | tf_op jit(solution)/shard_map/ppermute | solution.py:454
  13.0 1.0 %copy-start = (bf16[3,256,256]{2,1,0:T(8,128)(2,1)S(1)}, bf16[3,256,256]{2,1,0:T(8,128)(2,1)}, u32[]{:S(2)}) copy-start(bf16[3,256,256]{2,1,0:T(8,128)(2,1)} %constant.4.clone.refs_2_.refs_1_.refs_3_) | copy-start | bytes 1179652
  16.3 1.5 %copy-start.1 = (bf16[256,256]{1,0:T(8,128)(2,1)S(1)}, bf16[256,256]{1,0:T(8,128)(2,1)}, u32[]{:S(2)}) copy-start(bf16[256,256]{1,0:T(8,128)(2,1)} %constant.5.clone.refs_2_) | copy-start | bytes 393220
  19.0 1.8 %collective-permute-start.7 = (f32[8,128]{1,0:T(8,128)S(1)}, f32[8,128]{1,0:T(8,128)S(1)}, u32[]{:S(2)}, u32[]{:S(2)}) collective-permute-start(f32[8,128]{1,0:T(8,128)S(1)} %iteration.3.refs_3_), channel_id=1, source_target_pairs={{0,2},{4,6},{8,10},{12,14},{16,18},{20,22},{24,26},{28,30},{2,0},{... | collective-permute-start | bytes 12296 | tf_op jit(solution)/shard_map/ppermute | solution.py:454
  19.6 3.0 %collective-permute-start.8 = (f32[8,128]{1,0:T(8,128)S(1)}, f32[8,128]{1,0:T(8,128)S(1)}, u32[]{:S(2)}, u32[]{:S(2)}) collective-permute-start(f32[8,128]{1,0:T(8,128)S(1)} %iteration.3.refs_3_), channel_id=1, source_target_pairs={{0,3},{1,2},{4,7},{5,6},{8,11},{9,10},{12,15},{13,14},{16,19},{17,... | collective-permute-start | bytes 12296 | tf_op jit(solution)/shard_map/ppermute | solution.py:508
  23.8 3.1 %collective-permute-start.10 = (f32[8,128]{1,0:T(8,128)S(1)}, f32[8,128]{1,0:T(8,128)S(1)}, u32[]{:S(2)}, u32[]{:S(2)}) collective-permute-start(f32[8,128]{1,0:T(8,128)S(1)} %iteration.4.refs_3_), channel_id=1, source_target_pairs={{0,3},{1,2},{4,7},{5,6},{8,11},{9,10},{12,15},{13,14},{16,19},{17,... | collective-permute-start | bytes 12296 | tf_op jit(solution)/shard_map/ppermute | solution.py:508
  25.1 1.8 %collective-permute-start.9 = (f32[8,128]{1,0:T(8,128)S(1)}, f32[8,128]{1,0:T(8,128)S(1)}, u32[]{:S(2)}, u32[]{:S(2)}) collective-permute-start(f32[8,128]{1,0:T(8,128)S(1)} %iteration.4.refs_3_), channel_id=1, source_target_pairs={{0,2},{4,6},{8,10},{12,14},{16,18},{20,22},{24,26},{28,30},{2,0},{... | collective-permute-start | bytes 12296 | tf_op jit(solution)/shard_map/ppermute | solution.py:454
  27.7 2.2 %collective-permute-start.11 = (f32[8,128]{1,0:T(8,128)S(1)}, f32[8,128]{1,0:T(8,128)S(1)}, u32[]{:S(2)}, u32[]{:S(2)}) collective-permute-start(f32[8,128]{1,0:T(8,128)S(1)} %iteration.5.refs_0_), channel_id=1, source_target_pairs={{0,2},{4,6},{8,10},{12,14},{16,18},{20,22},{24,26},{28,30},{2,0},{... | collective-permute-start | bytes 12296 | tf_op jit(solution)/shard_map/ppermute | solution.py:454
  27.9 3.0 %collective-permute-start.12 = (f32[8,128]{1,0:T(8,128)S(1)}, f32[8,128]{1,0:T(8,128)S(1)}, u32[]{:S(2)}, u32[]{:S(2)}) collective-permute-start(f32[8,128]{1,0:T(8,128)S(1)} %iteration.5.refs_0_), channel_id=1, source_target_pairs={{0,3},{1,2},{4,7},{5,6},{8,11},{9,10},{12,15},{13,14},{16,19},{17,... | collective-permute-start | bytes 12296 | tf_op jit(solution)/shard_map/ppermute | solution.py:508
  29.4 3.6 %collective-permute-start.13 = (f32[8,128]{1,0:T(8,128)S(1)}, f32[8,128]{1,0:T(8,128)S(1)}, u32[]{:S(2)}, u32[]{:S(2)}) collective-permute-start(f32[8,128]{1,0:T(8,128)S(1)} %iteration.5.refs_0_), channel_id=1, source_target_pairs={{0,1},{1,0},{2,3},{3,2},{4,5},{5,4},{6,7},{7,6},{8,9},{9,8},{10,11... | collective-permute-start | bytes 12296 | tf_op jit(solution)/shard_map/ppermute | solution.py:524

commit v3 on v2

--- a/solution.py
+++ b/solution.py
@@ -15,6 +15,7 @@
 WINDOW = 8
 EXTRA = 16
 GROUP = 7
+DEPTH = 1
 
 step_size = 0.5
 stiffness = 0.2
@@ -175,6 +176,11 @@
             row_ref[col, 4 + dim, pl.ds(slot, 1), :] = small[6 + dim : 7 + dim]
     low_lane = lanes((1, PATCH)) <= HALF
     products = []
+
+    def finish(k):
+        wide = fold(dot(up_ref[...], products[k]))
+        base_ref[k % cols, pairs[k // cols]] = jnp.concatenate(split(wide[:PATCH] + wide[PATCH:]), axis=1)
+
     for pair in pairs:
         for col in range(cols):
             sr, si = real_ref[pair, col], imag_ref[pair, col]
@@ -184,10 +190,10 @@
             top = jnp.concatenate(split(jnp.where(low_lane, same, cross)), axis=1)
             bottom = jnp.concatenate(split(jnp.where(low_lane, cross, -same)), axis=1)
             products.append(jnp.concatenate([top, bottom], axis=0))
-    wides = [fold(dot(up_ref[...], product)) for product in products]
-    bases = [jnp.concatenate(split(wide[:PATCH] + wide[PATCH:]), axis=1) for wide in wides]
-    for k, base in enumerate(bases):
-        base_ref[k % cols, pairs[k // cols]] = base
+            if len(products) > DEPTH:
+                finish(len(products) - 1 - DEPTH)
+    for k in range(max(len(products) - DEPTH, 0), len(products)):
+        finish(k)
 
 
 def energies(row_ref, col):
@@ -473,35 +479,50 @@
     for source in ("own", "a", "b", "far"):
         blocks[source, 1] = between_cores(blocks[source, 0])
     state = []
+    row_perms = [swap([(r, r + 1) for r in range(0, n_row - 1, 2)])]
+    if n_row > 2:
+        row_perms.append(swap([(r, r + 1) for r in range(1, n_row - 1, 2)]))
     every = tuple(range(WINDOW - 1))
-    for stage, (names, pairs) in enumerate(
-        (
-            ((("own", 0), ("own", 1)), (HALO,)),
-            ((("a", 0),), ()),
-            ((("b", 0), ("far", 0)), ()),
-            ((("a", 1), ("b", 1), ("far", 1)), every[:HALO] + every[HALO + 1 :]),
-        )
-    ):
+    stages = (
+        ((("own", 0), ("own", 1)), (HALO,)),
+        ((("a", 0),), ()),
+        ((("b", 0), ("far", 0)), ()),
+        ((("a", 1), ("b", 1), ("far", 1)), every[:HALO] + every[HALO + 1 :]),
+    )
+    state_shapes = [
+        jax.ShapeDtypeStruct((WINDOW, cols, PATCH, PATCH), f32),
+        jax.ShapeDtypeStruct((WINDOW, cols, PATCH, PATCH), f32),
+        jax.ShapeDtypeStruct((cols, 6, WINDOW, PATCH), f32),
+        jax.ShapeDtypeStruct((cols, WINDOW - 1, PATCH, 2 * PATCH), bf16),
+    ]
+    message_shape = jax.ShapeDtypeStruct((WINDOW, PATCH), f32)
+    sums = [pltpu.VMEM((cols, WINDOW, PATCH), f32)] * 3
+    for stage, (names, pairs) in enumerate(stages):
+        last = stage == len(stages) - 1
+        operands = [blocks[name] for name in names] + [spectrum_tables]
+
+        def stage_kernel(*refs, names=names, pairs=pairs, stage=stage, last=last):
+            if not last:
+                spectra_kernel(cols, names, pairs, stage == 0, *refs)
+                return
+            count = len(names) + 1
+            outs = refs[count + 5 :]
+            spectra_kernel(cols, names, pairs, False, *refs[:count], *outs[:4])
+            iteration_kernel(cols, 0, WINDOW - 1, True, 0, outs[3], outs[2], refs[count], *outs[4:])
+
+        first_alias = len(operands) + last
         state = pl.pallas_call(
-            lambda *refs, names=names, pairs=pairs, stage=stage: spectra_kernel(cols, names, pairs, stage == 0, *refs),
-            out_shape=(
-                jax.ShapeDtypeStruct((WINDOW, cols, PATCH, PATCH), f32),
-                jax.ShapeDtypeStruct((WINDOW, cols, PATCH, PATCH), f32),
-                jax.ShapeDtypeStruct((cols, 6, WINDOW, PATCH), f32),
-                jax.ShapeDtypeStruct((cols, WINDOW - 1, PATCH, 2 * PATCH), bf16),
-            ),
-            in_specs=[vmem()] * (len(names) + 1 + len(state)),
-            out_specs=[vmem()] * 4,
-            input_output_aliases={len(names) + 1 + k: k for k in range(len(state))},
+            stage_kernel,
+            out_shape=state_shapes + [message_shape] * last,
+            in_specs=[vmem()] * (first_alias + len(state)),
+            out_specs=[vmem()] * (4 + last),
+            scratch_shapes=sums * last,
+            input_output_aliases={first_alias + k: k for k in range(len(state))},
             compiler_params=limit(16),
             cost_estimate=pl.CostEstimate(flops=500000000, bytes_accessed=1000000, transcendentals=0),
             name="spectra",
-        )(*[blocks[name] for name in names], spectrum_tables, *state)
-    base, stats = state[3], state[2]
-
-    row_perms = [swap([(r, r + 1) for r in range(0, n_row - 1, 2)])]
-    if n_row > 2:
-        row_perms.append(swap([(r, r + 1) for r in range(1, n_row - 1, 2)]))
+        )(*operands, *[back_table] * last, *state)
+    base, stats, out = state[3], state[2], state[4]
 
     def diagonal(x, rows):
         pairs = [(s * n_row + a, t * n_row + b) for s, t in cores for a, b in rows]
@@ -509,19 +530,20 @@
 
     messages = []
     for step in range(ITERS):
-        out = pl.pallas_call(
-            lambda *refs, step=step: iteration_kernel(cols, step, WINDOW - 1 - step, step == 0, len(row_perms), *refs),
-            out_shape=jax.ShapeDtypeStruct((WINDOW, PATCH), f32),
-            in_specs=[vmem()] * (3 + len(messages)),
-            out_specs=vmem(),
-            scratch_shapes=[pltpu.VMEM((cols, WINDOW, PATCH), f32)] * 3,
-            compiler_params=limit(8),
-            name="iteration",
-        )(base, stats, back_table, *messages)
+        if step > 0:
+            out = pl.pallas_call(
+                lambda *refs, step=step: iteration_kernel(cols, step, WINDOW - 1 - step, False, len(row_perms), *refs),
+                out_shape=message_shape,
+                in_specs=[vmem()] * (3 + len(messages)),
+                out_specs=vmem(),
+                scratch_shapes=sums,
+                compiler_params=limit(8),
+                name="iteration",
+            )(base, stats, back_table, *messages)
         beside = between_cores(out)
         rows = [diagonal(out, perm) for perm in row_perms]
         messages = [out, beside] + rows
-    straight = [lax.ppermute(out, "row", perm) for perm in row_perms]
+    straight = [between_cores(message) for message in rows]
     messages = messages[:2] + [message for pair in zip(rows, straight) for message in pair]
     shape = jax.ShapeDtypeStruct(displacement.shape, f32)
     return pl.pallas_call(

time: 33.9 us -> 33.2 us (0.979)
  the two profiles are of different devices: /device:TPU:20 before, /device:TPU:21 now
where the time goes in v3:
time: 33.2 us; the launch traced here: 33 us
  starting transfers between devices  16 us (48%)
  Pallas kernels  8.27 us (25%)
  waiting for transfers between devices  6.73 us (20%)
  local copies, waits for them, and re-layouts  1.17 us (4%)
  between operations  0.74 us (2%)
    ppermute x3, starting transfers between devices, per_device(): blocks[source, 0] = lax.ppermute(payload, 'sec', perm)  6.36 us
    ppermute x8, starting transfers between devices, between_cores(): return lax.ppermute(x, 'sec', cores)  4.97 us
    pallas_call x4, Pallas kernels, per_device(): pl.pallas_call(stage_kernel, out_shape=state_shapes + [message_shape] * l...  4.73 us
    ppermute x3, starting transfers between devices, diagonal(): return lax.ppermute(x, ('sec', 'row'), pairs)  4.7 us
    ppermute x3, waiting for transfers between devices, diagonal(): return lax.ppermute(x, ('sec', 'row'), pairs)  4.4 us
    pallas_call x2, Pallas kernels, per_device(): pl.pallas_call(lambda *refs, step=step: iteration_kernel(cols, step, WIND...  1.95 us
    ppermute x3, waiting for transfers between devices, per_device(): blocks[source, 0] = lax.ppermute(payload, 'sec', perm)  1.49 us
    unnamed x4, local copies, waits for them, and re-layouts  1.17 us
  transfers between devices with their start and end apart: 14, of which 5 were waited for; matrix products, arithmetic and copies ran while one was open for 0% of the time, Pallas kernels for 7%

profile of v3, /device:TPU:21, one launch (start us, length us, event | category | flops | bytes accessed | tf_op | source)
XLA Modules:
  0.0 33.0 jit_solution(5476415523130366313)
XLA Ops:
  0.6 0.9 %pack.1.refs_0_ = bf16[144,512]{1,0:T(8,128)(2,1)S(1)} custom-call(f32[2,1,1,4]{3,2,1,0:T(1,128)} %shift_ref.1, s32[2,1,1,4]{3,2,1,0:T(1,128)} %mask_ref.1, bf16[1,128,512]{2,1,0:T(8,128)(2,1)} %image_ref.1), custom_call_target="tpu_custom_call" | custom-call | bytes 8000000 | tf_op jit(solution)/shard_map/pack/pallas_call | solution.py:462
  1.6 0.3 collective-permute-start
  1.9 4.1 %collective-permute-start.2 = (bf16[144,512]{1,0:T(8,128)(2,1)S(1)}, bf16[144,512]{1,0:T(8,128)(2,1)S(1)}, u32[]{:S(2)}, u32[]{:S(2)}) collective-permute-start(bf16[144,512]{1,0:T(8,128)(2,1)S(1)} %pack.1.refs_0_), channel_id=1, source_target_pairs={{4,8},{6,10},{12,16},{14,18},{20,24},{22,26},{8,4},{10,6},{16,12},... | collective-permute-start | bytes 442376 | tf_op jit(solution)/shard_map/ppermute | solution.py:478
  6.0 1.9 %collective-permute-start.4 = (bf16[144,512]{1,0:T(8,128)(2,1)S(1)}, bf16[144,512]{1,0:T(8,128)(2,1)S(1)}, u32[]{:S(2)}, u32[]{:S(2)}) collective-permute-start(bf16[144,512]{1,0:T(8,128)(2,1)S(1)} %pack.1.refs_0_), channel_id=1, source_target_pairs={{2,8},{6,12},{10,16},{14,20},{18,24},{22,28},{8,2},{12,6},{16,10},... | collective-permute-start | bytes 442376 | tf_op jit(solution)/shard_map/ppermute | solution.py:478
  7.9 1.3 %collective-permute-start.6 = (bf16[144,512]{1,0:T(8,128)(2,1)S(1)}, bf16[144,512]{1,0:T(8,128)(2,1)S(1)}, u32[]{:S(2)}, u32[]{:S(2)}) collective-permute-start(bf16[144,512]{1,0:T(8,128)(2,1)S(1)} %pack.1.refs_0_), channel_id=1, source_target_pairs={{0,2},{4,6},{8,10},{12,14},{16,18},{20,22},{24,26},{28,30},{2,0},{... | collective-permute-start | bytes 442376 | tf_op jit(solution)/shard_map/ppermute | solution.py:460
  9.2 0.0 collective-permute-done.refs_0_
  9.3 1.8 %collective-permute-start.1 = (bf16[144,512]{1,0:T(8,128)(2,1)S(1)}, bf16[144,512]{1,0:T(8,128)(2,1)S(1)}, u32[]{:S(2)}, u32[]{:S(2)}) collective-permute-start(bf16[144,512]{1,0:T(8,128)(2,1)S(1)} %collective-permute-done.refs_0_), channel_id=1, source_target_pairs={{0,2},{4,6},{8,10},{12,14},{16,18},{20,22},{24,26},{28,30},{2,0},{... | collective-permute-start | bytes 442376 | tf_op jit(solution)/shard_map/ppermute | solution.py:460
  11.1 0.0 collective-permute-done.2.refs_0_
  11.1 0.2 collective-permute-start.3
  11.3 1.5 %collective-permute-done.4.refs_1_ = bf16[144,512]{1,0:T(8,128)(2,1)S(1)} collective-permute-done((bf16[144,512]{1,0:T(8,128)(2,1)S(1)}, bf16[144,512]{1,0:T(8,128)(2,1)S(1)}, u32[]{:S(2)}, u32[]{:S(2)}) %collective-permute-start.4) | collective-permute-done | bytes 147488 | tf_op jit(solution)/shard_map/ppermute | solution.py:478
  12.8 0.9 %collective-permute-start.5 = (bf16[144,512]{1,0:T(8,128)(2,1)S(1)}, bf16[144,512]{1,0:T(8,128)(2,1)S(1)}, u32[]{:S(2)}, u32[]{:S(2)}) collective-permute-start(bf16[144,512]{1,0:T(8,128)(2,1)S(1)} %collective-permute-done.4.refs_1_), channel_id=1, source_target_pairs={{0,2},{4,6},{8,10},{12,14},{16,18},{20,22},{24,26},{28,30},{2,0},{... | collective-permute-start | bytes 442376 | tf_op jit(solution)/shard_map/ppermute | solution.py:460
  13.7 0.0 collective-permute-done.6.refs_1_
  13.7 0.0 copy-start
  13.7 1.0 %copy-done = bf16[3,256,256]{2,1,0:T(8,128)(2,1)S(1)} copy-done((bf16[3,256,256]{2,1,0:T(8,128)(2,1)S(1)}, bf16[3,256,256]{2,1,0:T(8,128)(2,1)}, u32[]{:S(2)}) %copy-start) | copy-done | bytes 393240
  14.7 1.0 %spectra.4 = (f32[8,2,128,128]{3,2,1,0:T(8,128)S(1)}, f32[8,2,128,128]{3,2,1,0:T(8,128)S(1)}, f32[2,6,8,128]{3,2,1,0:T(8,128)S(1)}, bf16[2,7,128,256]{3,2,1,0:T(8,128)(2,1)S(1)}) custom-call(bf16[144,512]{1,0:T(8,128)(2,1)S(1)} %pack.1.refs_0_, bf16[144,512]{1,0:T(8,128)(2,1)S(1)} %collective-permute-done.6.refs_1_, bf16[3,256,256]{2,1,0:T(8,128)(2,1)S(1)} %copy-done), custom_call_target="tpu_custom_call" | custom-call | flops 500000000 | bytes 1000000 | tf_op jit(solution)/shard_map/spectra/pallas_call | solution.py:514
  15.7 0.6 %spectra.5 = (f32[8,2,128,128]{3,2,1,0:T(8,128)S(1)}, f32[8,2,128,128]{3,2,1,0:T(8,128)S(1)}, f32[2,6,8,128]{3,2,1,0:T(8,128)S(1)}, bf16[2,7,128,256]{3,2,1,0:T(8,128)(2,1)S(1)}) custom-call(bf16[144,512]{1,0:T(8,128)(2,1)S(1)} %collective-permute-done.refs_0_, ...), custom_call_target="tpu_custom_call", output_to_operand_aliasing={{0}: (2, {}), {1}: (3, {}), {2}: (4, {}), {3}: (5, {})} | custom-call | flops 500000000 | bytes 1000000 | tf_op jit(solution)/shard_map/spectra/pallas_call | solution.py:514
  16.3 0.0 copy-start.1
  16.3 0.7 %spectra.6 = (f32[8,2,128,128]{3,2,1,0:T(8,128)S(1)}, f32[8,2,128,128]{3,2,1,0:T(8,128)S(1)}, f32[2,6,8,128]{3,2,1,0:T(8,128)S(1)}, bf16[2,7,128,256]{3,2,1,0:T(8,128)(2,1)S(1)}) custom-call(bf16[144,512]{1,0:T(8,128)(2,1)S(1)} %collective-permute-done.2.refs_0_, ...), custom_call_target="tpu_custom_call", output_to_operand_aliasing={{0}: (3, {}), {1}: (4, {}), {2}: (5, {}), {3}: (6, {})} | custom-call | flops 500000000 | bytes 1000000 | tf_op jit(solution)/shard_map/spectra/pallas_call | solution.py:514
  17.0 0.0 collective-permute-done.1.refs_0_
  17.0 0.0 collective-permute-done.3.refs_1_
  17.0 0.0 collective-permute-done.5.refs_2_
  17.0 0.2 copy-done.1
  17.2 2.5 %spectra.7 = (f32[8,2,128,128]{3,2,1,0:T(8,128)S(1)}, f32[8,2,128,128]{3,2,1,0:T(8,128)S(1)}, f32[2,6,8,128]{3,2,1,0:T(8,128)S(1)}, bf16[2,7,128,256]{3,2,1,0:T(8,128)(2,1)S(1)}, f32[8,128]{1,0:T(8,128)S(1)}) custom-call(bf16[144,512]{1,0:T(8,128)(2,1)S(1)} %collective-permute-done.1.refs_0_,, ...), custom_call_target="tpu_custom_call", output_to_operand_aliasing={{0}: (5, {}), {1}: (6, {}), {2}: (7, {}), {3}: (8, {})} | custom-call | flops 500000000 | bytes 1000000 | tf_op jit(solution)/shard_map/spectra/pallas_call | solution.py:514
  19.7 0.1 collective-permute-start.7
  19.8 1.6 %collective-permute-start.8 = (f32[8,128]{1,0:T(8,128)S(1)}, f32[8,128]{1,0:T(8,128)S(1)}, u32[]{:S(2)}, u32[]{:S(2)}) collective-permute-start(f32[8,128]{1,0:T(8,128)S(1)} %get-tuple-element.31.refs_3_), channel_id=1, source_target_pairs={{0,3},{1,2},{4,7},{5,6},{8,11},{9,10},{12,15},{13,14},{16,19},{17,... | collective-permute-start | bytes 12296 | tf_op jit(solution)/shard_map/ppermute | solution.py:529
  21.4 0.0 collective-permute-done.7.refs_4_
  21.4 1.5 %collective-permute-done.8.refs_5_ = f32[8,128]{1,0:T(8,128)S(1)} collective-permute-done((f32[8,128]{1,0:T(8,128)S(1)}, f32[8,128]{1,0:T(8,128)S(1)}, u32[]{:S(2)}, u32[]{:S(2)}) %collective-permute-start.8) | collective-permute-done | bytes 4128 | tf_op jit(solution)/shard_map/ppermute | solution.py:529
  22.9 1.1 %iteration.2.refs_3_ = f32[8,128]{1,0:T(8,128)S(1)} custom-call(bf16[2,7,128,256]{3,2,1,0:T(8,128)(2,1)S(1)} %get-tuple-element.29.refs_0_, f32[2,6,8,128]{3,2,1,0:T(8,128)S(1)} %get-tuple-element.30.refs_1_, bf16[256,256]{1,0:T(8,128)(2,1)S(1)} %copy-done.1, f32[8,128]{1,0:T(8,128)S(1)} %get-tuple-element.31.refs_3_, ...), custom_call_target="tpu_custom_call" | custom-call | tf_op jit(solution)/shard_map/iteration/pallas_call | solution.py:534
  24.0 1.6 %collective-permute-start.10 = (f32[8,128]{1,0:T(8,128)S(1)}, f32[8,128]{1,0:T(8,128)S(1)}, u32[]{:S(2)}, u32[]{:S(2)}) collective-permute-start(f32[8,128]{1,0:T(8,128)S(1)} %iteration.2.refs_3_), channel_id=1, source_target_pairs={{0,3},{1,2},{4,7},{5,6},{8,11},{9,10},{12,15},{13,14},{16,19},{17,... | collective-permute-start | bytes 12296 | tf_op jit(solution)/shard_map/ppermute | solution.py:529
  25.6 0.1 collective-permute-start.9
  25.7 1.4 %collective-permute-done.10.refs_5_ = f32[8,128]{1,0:T(8,128)S(1)} collective-permute-done((f32[8,128]{1,0:T(8,128)S(1)}, f32[8,128]{1,0:T(8,128)S(1)}, u32[]{:S(2)}, u32[]{:S(2)}) %collective-permute-start.10) | collective-permute-done | bytes 4128 | tf_op jit(solution)/shard_map/ppermute | solution.py:529
  27.1 0.0 collective-permute-done.9.refs_4_
  27.1 0.8 %iteration.3.refs_0_ = f32[8,128]{1,0:T(8,128)S(1)} custom-call(bf16[2,7,128,256]{3,2,1,0:T(8,128)(2,1)S(1)} %get-tuple-element.29.refs_0_, f32[2,6,8,128]{3,2,1,0:T(8,128)S(1)} %get-tuple-element.30.refs_1_, bf16[256,256]{1,0:T(8,128)(2,1)S(1)} %copy-done.1, f32[8,128]{1,0:T(8,128)S(1)} %iteration.2.refs_3_, f32[8,128]{1,0:T(8,128)S(1)} %collective-permute-done.9.refs_4_, ...), custom_call_target="tpu_custom_call" | custom-call | tf_op jit(solution)/shard_map/iteration/pallas_call | solution.py:534
  28.0 1.6 %collective-permute-start.12 = (f32[8,128]{1,0:T(8,128)S(1)}, f32[8,128]{1,0:T(8,128)S(1)}, u32[]{:S(2)}, u32[]{:S(2)}) collective-permute-start(f32[8,128]{1,0:T(8,128)S(1)} %iteration.3.refs_0_), channel_id=1, source_target_pairs={{0,3},{1,2},{4,7},{5,6},{8,11},{9,10},{12,15},{13,14},{16,19},{17,... | collective-permute-start | bytes 12296 | tf_op jit(solution)/shard_map/ppermute | solution.py:529
  29.5 0.1 collective-permute-start.11
  29.6 1.4 %collective-permute-done.12.refs_2_ = f32[8,128]{1,0:T(8,128)S(1)} collective-permute-done((f32[8,128]{1,0:T(8,128)S(1)}, f32[8,128]{1,0:T(8,128)S(1)}, u32[]{:S(2)}, u32[]{:S(2)}) %collective-permute-start.12) | collective-permute-done | bytes 4128 | tf_op jit(solution)/shard_map/ppermute | solution.py:529
  31.1 0.4 %collective-permute-start.13 = (f32[8,128]{1,0:T(8,128)S(1)}, f32[8,128]{1,0:T(8,128)S(1)}, u32[]{:S(2)}, u32[]{:S(2)}) collective-permute-start(f32[8,128]{1,0:T(8,128)S(1)} %collective-permute-done.12.refs_2_), channel_id=1, source_target_pairs={{0,2},{4,6},{8,10},{12,14},{16,18},{20,22},{24,26},{28,30},{2,0},{... | collective-permute-start | bytes 12296 | tf_op jit(solution)/shard_map/ppermute | solution.py:460
  31.5 0.0 collective-permute-done.11.refs_1_
  31.5 0.8 %collective-permute-done.13.refs_3_ = f32[8,128]{1,0:T(8,128)S(1)} collective-permute-done((f32[8,128]{1,0:T(8,128)S(1)}, f32[8,128]{1,0:T(8,128)S(1)}, u32[]{:S(2)}, u32[]{:S(2)}) %collective-permute-start.13) | collective-permute-done | bytes 4128 | tf_op jit(solution)/shard_map/ppermute | solution.py:460
  32.3 0.7 %final.1 = (f32[2,1,1,4]{3,2,1,0:T(1,128)}, f32[2,1,1,4]{3,2,1,0:T(1,128)}) custom-call(f32[8,128]{1,0:T(8,128)S(1)} %iteration.3.refs_0_, f32[8,128]{1,0:T(8,128)S(1)} %collective-permute-done.11.refs_1_, f32[8,128]{1,0:T(8,128)S(1)} %collective-permute-done.12.refs_2_, f32[8,128]{1,0:T(8,128)S(1)} %collective-permute-done.13.refs_3_), custom_call_target="tpu_custom_call" | custom-call | tf_op jit(solution)/shard_map/final/pallas_call | solution.py:549
Async XLA Ops:
  1.6 7.7 %collective-permute-start = (bf16[144,512]{1,0:T(8,128)(2,1)S(1)}, bf16[144,512]{1,0:T(8,128)(2,1)S(1)}, u32[]{:S(2)}, u32[]{:S(2)}) collective-permute-start(bf16[144,512]{1,0:T(8,128)(2,1)S(1)} %pack.1.refs_0_), channel_id=1, source_target_pairs={{0,4},{2,6},{8,12},{10,14},{16,20},{18,22},{24,28},{26,30},{4,0},{... | collective-permute-start | bytes 442376 | tf_op jit(solution)/shard_map/ppermute | solution.py:478
  1.9 9.2 %collective-permute-start.2 = (bf16[144,512]{1,0:T(8,128)(2,1)S(1)}, bf16[144,512]{1,0:T(8,128)(2,1)S(1)}, u32[]{:S(2)}, u32[]{:S(2)}) collective-permute-start(bf16[144,512]{1,0:T(8,128)(2,1)S(1)} %pack.1.refs_0_), channel_id=1, source_target_pairs={{4,8},{6,10},{12,16},{14,18},{20,24},{22,26},{8,4},{10,6},{16,12},... | collective-permute-start | bytes 442376 | tf_op jit(solution)/shard_map/ppermute | solution.py:478
  6.0 6.8 %collective-permute-start.4 = (bf16[144,512]{1,0:T(8,128)(2,1)S(1)}, bf16[144,512]{1,0:T(8,128)(2,1)S(1)}, u32[]{:S(2)}, u32[]{:S(2)}) collective-permute-start(bf16[144,512]{1,0:T(8,128)(2,1)S(1)} %pack.1.refs_0_), channel_id=1, source_target_pairs={{2,8},{6,12},{10,16},{14,20},{18,24},{22,28},{8,2},{12,6},{16,10},... | collective-permute-start | bytes 442376 | tf_op jit(solution)/shard_map/ppermute | solution.py:478
  7.9 5.8 %collective-permute-start.6 = (bf16[144,512]{1,0:T(8,128)(2,1)S(1)}, bf16[144,512]{1,0:T(8,128)(2,1)S(1)}, u32[]{:S(2)}, u32[]{:S(2)}) collective-permute-start(bf16[144,512]{1,0:T(8,128)(2,1)S(1)} %pack.1.refs_0_), channel_id=1, source_target_pairs={{0,2},{4,6},{8,10},{12,14},{16,18},{20,22},{24,26},{28,30},{2,0},{... | collective-permute-start | bytes 442376 | tf_op jit(solution)/shard_map/ppermute | solution.py:460
  9.3 7.7 %collective-permute-start.1 = (bf16[144,512]{1,0:T(8,128)(2,1)S(1)}, bf16[144,512]{1,0:T(8,128)(2,1)S(1)}, u32[]{:S(2)}, u32[]{:S(2)}) collective-permute-start(bf16[144,512]{1,0:T(8,128)(2,1)S(1)} %collective-permute-done.refs_0_), channel_id=1, source_target_pairs={{0,2},{4,6},{8,10},{12,14},{16,18},{20,22},{24,26},{28,30},{2,0},{... | collective-permute-start | bytes 442376 | tf_op jit(solution)/shard_map/ppermute | solution.py:460
  11.1 5.9 %collective-permute-start.3 = (bf16[144,512]{1,0:T(8,128)(2,1)S(1)}, bf16[144,512]{1,0:T(8,128)(2,1)S(1)}, u32[]{:S(2)}, u32[]{:S(2)}) collective-permute-start(bf16[144,512]{1,0:T(8,128)(2,1)S(1)} %collective-permute-done.2.refs_0_), channel_id=1, source_target_pairs={{0,2},{4,6},{8,10},{12,14},{16,18},{20,22},{24,26},{28,30},{2,0},{... | collective-permute-start | bytes 442376 | tf_op jit(solution)/shard_map/ppermute | solution.py:460
  12.8 4.2 %collective-permute-start.5 = (bf16[144,512]{1,0:T(8,128)(2,1)S(1)}, bf16[144,512]{1,0:T(8,128)(2,1)S(1)}, u32[]{:S(2)}, u32[]{:S(2)}) collective-permute-start(bf16[144,512]{1,0:T(8,128)(2,1)S(1)} %collective-permute-done.4.refs_1_), channel_id=1, source_target_pairs={{0,2},{4,6},{8,10},{12,14},{16,18},{20,22},{24,26},{28,30},{2,0},{... | collective-permute-start | bytes 442376 | tf_op jit(solution)/shard_map/ppermute | solution.py:460
  13.7 1.0 %copy-start = (bf16[3,256,256]{2,1,0:T(8,128)(2,1)S(1)}, bf16[3,256,256]{2,1,0:T(8,128)(2,1)}, u32[]{:S(2)}) copy-start(bf16[3,256,256]{2,1,0:T(8,128)(2,1)} %constant.4.clone.refs_2_.refs_1_.refs_3_) | copy-start | bytes 1179652
  16.3 0.9 %copy-start.1 = (bf16[256,256]{1,0:T(8,128)(2,1)S(1)}, bf16[256,256]{1,0:T(8,128)(2,1)}, u32[]{:S(2)}) copy-start(bf16[256,256]{1,0:T(8,128)(2,1)} %constant.5.clone.refs_4_.refs_2_) | copy-start | bytes 393220
  19.7 1.7 %collective-permute-start.7 = (f32[8,128]{1,0:T(8,128)S(1)}, f32[8,128]{1,0:T(8,128)S(1)}, u32[]{:S(2)}, u32[]{:S(2)}) collective-permute-start(f32[8,128]{1,0:T(8,128)S(1)} %get-tuple-element.31.refs_3_), channel_id=1, source_target_pairs={{0,2},{4,6},{8,10},{12,14},{16,18},{20,22},{24,26},{28,30},{2,0},{... | collective-permute-start | bytes 12296 | tf_op jit(solution)/shard_map/ppermute | solution.py:460
  19.8 3.1 %collective-permute-start.8 = (f32[8,128]{1,0:T(8,128)S(1)}, f32[8,128]{1,0:T(8,128)S(1)}, u32[]{:S(2)}, u32[]{:S(2)}) collective-permute-start(f32[8,128]{1,0:T(8,128)S(1)} %get-tuple-element.31.refs_3_), channel_id=1, source_target_pairs={{0,3},{1,2},{4,7},{5,6},{8,11},{9,10},{12,15},{13,14},{16,19},{17,... | collective-permute-start | bytes 12296 | tf_op jit(solution)/shard_map/ppermute | solution.py:529
  24.0 3.1 %collective-permute-start.10 = (f32[8,128]{1,0:T(8,128)S(1)}, f32[8,128]{1,0:T(8,128)S(1)}, u32[]{:S(2)}, u32[]{:S(2)}) collective-permute-start(f32[8,128]{1,0:T(8,128)S(1)} %iteration.2.refs_3_), channel_id=1, source_target_pairs={{0,3},{1,2},{4,7},{5,6},{8,11},{9,10},{12,15},{13,14},{16,19},{17,... | collective-permute-start | bytes 12296 | tf_op jit(solution)/shard_map/ppermute | solution.py:529
  25.6 1.5 %collective-permute-start.9 = (f32[8,128]{1,0:T(8,128)S(1)}, f32[8,128]{1,0:T(8,128)S(1)}, u32[]{:S(2)}, u32[]{:S(2)}) collective-permute-start(f32[8,128]{1,0:T(8,128)S(1)} %iteration.2.refs_3_), channel_id=1, source_target_pairs={{0,2},{4,6},{8,10},{12,14},{16,18},{20,22},{24,26},{28,30},{2,0},{... | collective-permute-start | bytes 12296 | tf_op jit(solution)/shard_map/ppermute | solution.py:460
  28.0 3.1 %collective-permute-start.12 = (f32[8,128]{1,0:T(8,128)S(1)}, f32[8,128]{1,0:T(8,128)S(1)}, u32[]{:S(2)}, u32[]{:S(2)}) collective-permute-start(f32[8,128]{1,0:T(8,128)S(1)} %iteration.3.refs_0_), channel_id=1, source_target_pairs={{0,3},{1,2},{4,7},{5,6},{8,11},{9,10},{12,15},{13,14},{16,19},{17,... | collective-permute-start | bytes 12296 | tf_op jit(solution)/shard_map/ppermute | solution.py:529
  29.5 1.9 %collective-permute-start.11 = (f32[8,128]{1,0:T(8,128)S(1)}, f32[8,128]{1,0:T(8,128)S(1)}, u32[]{:S(2)}, u32[]{:S(2)}) collective-permute-start(f32[8,128]{1,0:T(8,128)S(1)} %iteration.3.refs_0_), channel_id=1, source_target_pairs={{0,2},{4,6},{8,10},{12,14},{16,18},{20,22},{24,26},{28,30},{2,0},{... | collective-permute-start | bytes 12296 | tf_op jit(solution)/shard_map/ppermute | solution.py:460
  31.1 1.2 %collective-permute-start.13 = (f32[8,128]{1,0:T(8,128)S(1)}, f32[8,128]{1,0:T(8,128)S(1)}, u32[]{:S(2)}, u32[]{:S(2)}) collective-permute-start(f32[8,128]{1,0:T(8,128)S(1)} %collective-permute-done.12.refs_2_), channel_id=1, source_target_pairs={{0,2},{4,6},{8,10},{12,14},{16,18},{20,22},{24,26},{28,30},{2,0},{... | collective-permute-start | bytes 12296 | tf_op jit(solution)/shard_map/ppermute | solution.py:460

commit v4 on v3

--- a/solution.py
+++ b/solution.py
@@ -14,7 +14,8 @@
 HALO = 3
 WINDOW = 8
 EXTRA = 16
-GROUP = 7
+FIRST_GROUP = 4
+GROUP = 10
 DEPTH = 1
 
 step_size = 0.5
@@ -112,27 +113,29 @@
     copies[0].wait()
 
 
-def forward_patches(patches, basis, down):
+def forward_patches(patches, basis, down, mean_row):
     count = len(patches)
-    values = [patch.astype(f32) for patch in patches]
-    totals = [jnp.sum(jnp.sum(value, axis=0, keepdims=True), axis=1, keepdims=True) for value in values]
-    values = [value - total * (1.0 / (PATCH * PATCH)) for value, total in zip(values, totals)]
-    left = jnp.concatenate([jnp.concatenate(split(value), axis=1) for value in values], axis=0)
-    rows = fold(dot(left, basis))
-    rows = [rows[k * PATCH : (k + 1) * PATCH] for k in range(count)]
-    pairs = [jnp.concatenate(split(row), axis=1) for row in rows]
-    both = [fold(dot(down, jnp.concatenate([pair, pair], axis=0))) for pair in pairs]
+    rows = fold(dot(jnp.concatenate(patches, axis=0), basis))
     lane = lanes((1, PATCH))
+    sign = alternating((WINDOW, PATCH), 0)
     sigma = jnp.where(lane > HALF, 1.0, -1.0) * jnp.where(lane % HALF == 0, 0.0, 1.0)
-    sign = alternating((PATCH, PATCH), 0)
+    centred, nyquist_rows, pairs = [], [], []
+    for k in range(count):
+        row = rows[k * PATCH : (k + 1) * PATCH]
+        part = jnp.sum(row.reshape(PATCH // WINDOW, WINDOW, PATCH), axis=0)
+        whole = jnp.sum(part, axis=0, keepdims=True)
+        row = row - (whole[:, :1] * (1.0 / (PATCH * PATCH))) * mean_row
+        nyquist_rows.append(jnp.sum(part * sign, axis=0, keepdims=True))
+        pair = jnp.concatenate(split(row), axis=1)
+        centred.append(row)
+        pairs.append(jnp.concatenate([pair, pair], axis=0))
+    both = [fold(dot(down, pair)) for pair in pairs]
     result = []
-    for row, wide in zip(rows, both):
+    for row, nyquist_row, wide in zip(centred, nyquist_rows, both):
         first, second = wide[:PATCH], wide[PATCH:]
         real = first + sigma * pltpu.roll(second, HALF, 1)
         imag = second - sigma * pltpu.roll(first, HALF, 1)
-        energy_row = jnp.sum(row * row, axis=0, keepdims=True)
-        nyquist_row = jnp.sum(row * sign, axis=0, keepdims=True)
-        result.append((real, imag, energy_row, nyquist_row))
+        result.append((real, imag, jnp.sum(row * row, axis=0, keepdims=True), nyquist_row))
     return result
 
 
@@ -155,6 +158,9 @@
 def spectra_kernel(cols, names, pairs, starts, *refs):
     blocks, tables_ref = refs[: len(names)], refs[len(names)]
     basis_ref, down_ref, up_ref = [tables_ref.at[k] for k in range(3)]
+    basis = basis_ref[:PATCH]
+    ones = jnp.sum(basis.astype(f32), axis=0, keepdims=True)
+    mean_row = ones[:, :PATCH] + ones[:, PATCH:]
     real_ref, imag_ref, row_ref, base_ref = refs[-4:]
     if starts:
         row_ref[...] = jnp.zeros(row_ref.shape, f32)
@@ -163,7 +169,7 @@
     places = [(block, slot, col) for block, slot in zip(blocks, slots) for col in range(cols)]
     starts = [pl.multiple_of((half * cols + col) * PATCH, PATCH) for col in range(cols)]
     patches = [block[:PATCH, pl.ds(starts[col], PATCH)] for block, slot, col in places]
-    results = forward_patches(patches, basis_ref[...], down_ref[...])
+    results = forward_patches(patches, basis, down_ref[...], mean_row)
     for (block, slot, col), (real, imag, energy_row, nyquist_row) in zip(places, results):
         real_ref[slot, col] = real
         imag_ref[slot, col] = imag
@@ -318,7 +324,7 @@
         cos_y, sin_y = cos_sin_turns(dy * 0.5)
         cos_x, sin_x = cos_sin_turns(dx * 0.5)
         cos_both = cos_y * cos_x - sin_y * sin_x
-        bulk, row_energy, col_energy, corner_energy, nyquist = energies(row_ref, col)
+        bulk, row_energy, col_energy, corner_energy, nyquist = [row_ref[col, 6 + k] for k in range(5)]
         energy = bulk + cos_y * cos_y * row_energy + cos_x * cos_x * col_energy + cos_both * cos_both * corner_energy
         scale = (sharpness / math.log(2.0)) / jnp.sqrt(energy * next_section(energy) + epsilon)
         gamma_y = cos_y * next_section(cos_y)
@@ -332,22 +338,27 @@
         turn_sin.append(jnp.where(zero_lane, 0.0, jnp.where(high_lane, -sine, sine)) * scale)
     checker = alternating((WINDOW, PATCH), 0) * alternating((WINDOW, PATCH), 1)
     blocks = PATCH // WINDOW
-    block_lag = [WINDOW * k - (PATCH if k >= blocks // 2 else 0) for k in range(blocks)]
+    block_order = [(blocks // 2 - 1 - k) % blocks for k in range(blocks)]
     row_in_block = lax.broadcasted_iota(jnp.int32, (WINDOW, PATCH), 0).astype(f32)
     for col in range(cols):
         total_ref[col] = jnp.ones((WINDOW, PATCH), f32)
         moment_ref[col] = jnp.zeros((WINDOW, PATCH), f32)
         edge_ref[col] = jnp.zeros((WINDOW, PATCH), f32)
     tasks = [(pair, col) for pair in range(first, last) for col in range(cols)]
-    size = -(-len(tasks) // -(-len(tasks) // GROUP))
+    most = FIRST_GROUP if starts else GROUP
+    size = -(-len(tasks) // -(-len(tasks) // most))
     for at in range(0, len(tasks), size):
         group = tasks[at : at + size]
         moved = []
         for pair, col in group:
             row = slice(pair, pair + 1)
-            shifter = pltpu.roll(jnp.broadcast_to(rows[col][row], (PATCH, PATCH)), 0, 1, stride=1, stride_axis=0)
+            parts = [part.astype(f32) for part in split(rows[col][row])]
+            parts = [
+                pltpu.roll(jnp.broadcast_to(part, (PATCH, PATCH)), 0, 1, stride=1, stride_axis=0).astype(bf16)
+                for part in parts
+            ]
             base = base_ref[col, pair]
-            moved.append(fold(dot(jnp.concatenate(split(shifter), axis=1), jnp.concatenate([base, base], axis=0))))
+            moved.append(fold(dot(jnp.concatenate(parts, axis=1), jnp.concatenate([base, base], axis=0))))
         turned = []
         for (pair, col), value in zip(group, moved):
             row = slice(pair, pair + 1)
@@ -358,12 +369,13 @@
             row = slice(pair, pair + 1)
             scores = wide[k * PATCH : (k + 1) * PATCH].reshape(blocks, WINDOW, PATCH)
             weights = jnp.exp2(scores + (ripple[col][row] * checker)[None])
-            total = weights[0]
-            moment = weights[0] * float(block_lag[0])
-            for m in range(1, blocks):
+            total = weights[block_order[0]]
+            moment = total
+            for m in block_order[1:-1]:
                 total = total + weights[m]
-                moment = moment + weights[m] * float(block_lag[m])
-            moment = moment + row_in_block * total
+                moment = moment + total
+            total = total + weights[block_order[-1]]
+            moment = float(WINDOW) * moment + (row_in_block - PATCH // 2) * total
             total_ref[col, row, :] = jnp.sum(total, axis=0, keepdims=True)
             moment_ref[col, row, :] = jnp.sum(moment, axis=0, keepdims=True)
             edge_ref[col, row, :] = weights[blocks // 2, 0:1]
@@ -486,13 +498,13 @@
     stages = (
         ((("own", 0), ("own", 1)), (HALO,)),
         ((("a", 0),), ()),
-        ((("b", 0), ("far", 0)), ()),
-        ((("a", 1), ("b", 1), ("far", 1)), every[:HALO] + every[HALO + 1 :]),
+        ((("a", 1), ("b", 0), ("far", 0)), ()),
+        ((("b", 1), ("far", 1)), every[:HALO] + every[HALO + 1 :]),
     )
     state_shapes = [
         jax.ShapeDtypeStruct((WINDOW, cols, PATCH, PATCH), f32),
         jax.ShapeDtypeStruct((WINDOW, cols, PATCH, PATCH), f32),
-        jax.ShapeDtypeStruct((cols, 6, WINDOW, PATCH), f32),
+        jax.ShapeDtypeStruct((cols, 11, WINDOW, PATCH), f32),
         jax.ShapeDtypeStruct((cols, WINDOW - 1, PATCH, 2 * PATCH), bf16),
     ]
     message_shape = jax.ShapeDtypeStruct((WINDOW, PATCH), f32)
@@ -508,6 +520,9 @@
             count = len(names) + 1
             outs = refs[count + 5 :]
             spectra_kernel(cols, names, pairs, False, *refs[:count], *outs[:4])
+            for col in range(cols):
+                for k, value in enumerate(energies(outs[2], col)):
+                    outs[2][col, 6 + k] = value
             iteration_kernel(cols, 0, WINDOW - 1, True, 0, outs[3], outs[2], refs[count], *outs[4:])
 
         first_alias = len(operands) + last

time: 33.2 us -> 32.7 us (0.985)
  Pallas kernels: 8.27 us -> 7.91 us
where the time goes in v4:
time: 32.7 us; the launch traced here: 32.5 us
  starting transfers between devices  16 us (49%)
  Pallas kernels  7.91 us (24%)
  waiting for transfers between devices  6.73 us (21%)
  local copies, waits for them, and re-layouts  1.1 us (3%)
  between operations  0.75 us (2%)
    ppermute x3, starting transfers between devices, per_device(): blocks[source, 0] = lax.ppermute(payload, 'sec', perm)  6.36 us
    ppermute x8, starting transfers between devices, between_cores(): return lax.ppermute(x, 'sec', cores)  4.97 us
    ppermute x3, starting transfers between devices, diagonal(): return lax.ppermute(x, ('sec', 'row'), pairs)  4.7 us
    pallas_call x4, Pallas kernels, per_device(): pl.pallas_call(stage_kernel, out_shape=state_shapes + [message_shape] * l...  4.53 us
    ppermute x3, waiting for transfers between devices, diagonal(): return lax.ppermute(x, ('sec', 'row'), pairs)  4.4 us
    pallas_call x2, Pallas kernels, per_device(): pl.pallas_call(lambda *refs, step=step: iteration_kernel(cols, step, WIND...  1.78 us
    ppermute x3, waiting for transfers between devices, per_device(): blocks[source, 0] = lax.ppermute(payload, 'sec', perm)  1.49 us
    unnamed x4, local copies, waits for them, and re-layouts  1.1 us
  transfers between devices with their start and end apart: 14, of which 5 were waited for; matrix products, arithmetic and copies ran while one was open for 0% of the time, Pallas kernels for 7%

profile of v4, /device:TPU:21, one launch (start us, length us, event | category | flops | bytes accessed | tf_op | source)
XLA Modules:
  0.0 32.5 jit_solution(1107716157390537883)
XLA Ops:
  0.6 0.9 %pack.1.refs_0_ = bf16[144,512]{1,0:T(8,128)(2,1)S(1)} custom-call(f32[2,1,1,4]{3,2,1,0:T(1,128)} %shift_ref.1, s32[2,1,1,4]{3,2,1,0:T(1,128)} %mask_ref.1, bf16[1,128,512]{2,1,0:T(8,128)(2,1)} %image_ref.1), custom_call_target="tpu_custom_call" | custom-call | bytes 8000000 | tf_op jit(solution)/shard_map/pack/pallas_call | solution.py:474
  1.6 0.3 collective-permute-start.4
  1.9 4.1 %collective-permute-start = (bf16[144,512]{1,0:T(8,128)(2,1)S(1)}, bf16[144,512]{1,0:T(8,128)(2,1)S(1)}, u32[]{:S(2)}, u32[]{:S(2)}) collective-permute-start(bf16[144,512]{1,0:T(8,128)(2,1)S(1)} %pack.1.refs_0_), channel_id=1, source_target_pairs={{4,8},{6,10},{12,16},{14,18},{20,24},{22,26},{8,4},{10,6},{16,12},... | collective-permute-start | bytes 442376 | tf_op jit(solution)/shard_map/ppermute | solution.py:490
  6.0 1.9 %collective-permute-start.2 = (bf16[144,512]{1,0:T(8,128)(2,1)S(1)}, bf16[144,512]{1,0:T(8,128)(2,1)S(1)}, u32[]{:S(2)}, u32[]{:S(2)}) collective-permute-start(bf16[144,512]{1,0:T(8,128)(2,1)S(1)} %pack.1.refs_0_), channel_id=1, source_target_pairs={{2,8},{6,12},{10,16},{14,20},{18,24},{22,28},{8,2},{12,6},{16,10},... | collective-permute-start | bytes 442376 | tf_op jit(solution)/shard_map/ppermute | solution.py:490
  7.9 1.3 %collective-permute-start.6 = (bf16[144,512]{1,0:T(8,128)(2,1)S(1)}, bf16[144,512]{1,0:T(8,128)(2,1)S(1)}, u32[]{:S(2)}, u32[]{:S(2)}) collective-permute-start(bf16[144,512]{1,0:T(8,128)(2,1)S(1)} %pack.1.refs_0_), channel_id=1, source_target_pairs={{0,2},{4,6},{8,10},{12,14},{16,18},{20,22},{24,26},{28,30},{2,0},{... | collective-permute-start | bytes 442376 | tf_op jit(solution)/shard_map/ppermute | solution.py:472
  9.2 0.0 collective-permute-done.4.refs_0_
  9.3 1.8 %collective-permute-start.5 = (bf16[144,512]{1,0:T(8,128)(2,1)S(1)}, bf16[144,512]{1,0:T(8,128)(2,1)S(1)}, u32[]{:S(2)}, u32[]{:S(2)}) collective-permute-start(bf16[144,512]{1,0:T(8,128)(2,1)S(1)} %collective-permute-done.4.refs_0_), channel_id=1, source_target_pairs={{0,2},{4,6},{8,10},{12,14},{16,18},{20,22},{24,26},{28,30},{2,0},{... | collective-permute-start | bytes 442376 | tf_op jit(solution)/shard_map/ppermute | solution.py:472
  11.1 0.0 collective-permute-done.refs_1_
  11.1 0.2 collective-permute-start.1
  11.3 1.5 %collective-permute-done.2.refs_2_ = bf16[144,512]{1,0:T(8,128)(2,1)S(1)} collective-permute-done((bf16[144,512]{1,0:T(8,128)(2,1)S(1)}, bf16[144,512]{1,0:T(8,128)(2,1)S(1)}, u32[]{:S(2)}, u32[]{:S(2)}) %collective-permute-start.2) | collective-permute-done | bytes 147488 | tf_op jit(solution)/shard_map/ppermute | solution.py:490
  12.8 0.9 %collective-permute-start.3 = (bf16[144,512]{1,0:T(8,128)(2,1)S(1)}, bf16[144,512]{1,0:T(8,128)(2,1)S(1)}, u32[]{:S(2)}, u32[]{:S(2)}) collective-permute-start(bf16[144,512]{1,0:T(8,128)(2,1)S(1)} %collective-permute-done.2.refs_2_), channel_id=1, source_target_pairs={{0,2},{4,6},{8,10},{12,14},{16,18},{20,22},{24,26},{28,30},{2,0},{... | collective-permute-start | bytes 442376 | tf_op jit(solution)/shard_map/ppermute | solution.py:472
  13.7 0.0 collective-permute-done.6.refs_1_
  13.7 0.0 copy-start
  13.7 1.0 %copy-done = bf16[3,256,256]{2,1,0:T(8,128)(2,1)S(1)} copy-done((bf16[3,256,256]{2,1,0:T(8,128)(2,1)S(1)}, bf16[3,256,256]{2,1,0:T(8,128)(2,1)}, u32[]{:S(2)}) %copy-start) | copy-done | bytes 393240
  14.7 1.0 %spectra.4 = (f32[8,2,128,128]{3,2,1,0:T(8,128)S(1)}, f32[8,2,128,128]{3,2,1,0:T(8,128)S(1)}, f32[2,11,8,128]{3,2,1,0:T(8,128)S(1)}, bf16[2,7,128,256]{3,2,1,0:T(8,128)(2,1)S(1)}) custom-call(bf16[144,512]{1,0:T(8,128)(2,1)S(1)} %pack.1.refs_0_, bf16[144,512]{1,0:T(8,128)(2,1)S(1)} %collective-permute-done.6.refs_1_, bf16[3,256,256]{2,1,0:T(8,128)(2,1)S(1)} %copy-done), custom_call_target="tpu_custom_call" | custom-call | flops 500000000 | bytes 1000000 | tf_op jit(solution)/shard_map/spectra/pallas_call | solution.py:529
  15.7 0.6 %spectra.5 = (f32[8,2,128,128]{3,2,1,0:T(8,128)S(1)}, f32[8,2,128,128]{3,2,1,0:T(8,128)S(1)}, f32[2,11,8,128]{3,2,1,0:T(8,128)S(1)}, bf16[2,7,128,256]{3,2,1,0:T(8,128)(2,1)S(1)}) custom-call(bf16[144,512]{1,0:T(8,128)(2,1)S(1)} %collective-permute-done.4.refs_0_, ...), custom_call_target="tpu_custom_call", output_to_operand_aliasing={{0}: (2, {}), {1}: (3, {}), {2}: (4, {}), {3}: (5, {})} | custom-call | flops 500000000 | bytes 1000000 | tf_op jit(solution)/shard_map/spectra/pallas_call | solution.py:529
  16.2 0.0 collective-permute-done.5.refs_0_
  16.3 0.0 copy-start.1
  16.3 0.8 %spectra.6 = (f32[8,2,128,128]{3,2,1,0:T(8,128)S(1)}, f32[8,2,128,128]{3,2,1,0:T(8,128)S(1)}, f32[2,11,8,128]{3,2,1,0:T(8,128)S(1)}, bf16[2,7,128,256]{3,2,1,0:T(8,128)(2,1)S(1)}) custom-call(bf16[144,512]{1,0:T(8,128)(2,1)S(1)} %collective-permute-done.5.refs_0_, ...), custom_call_target="tpu_custom_call", output_to_operand_aliasing={{0}: (4, {}), {1}: (5, {}), {2}: (6, {}), {3}: (7, {})} | custom-call | flops 500000000 | bytes 1000000 | tf_op jit(solution)/shard_map/spectra/pallas_call | solution.py:529
  17.0 0.0 collective-permute-done.1.refs_0_
  17.1 0.0 collective-permute-done.3.refs_1_
  17.1 0.1 copy-done.1
  17.2 2.2 %spectra.7 = (f32[8,2,128,128]{3,2,1,0:T(8,128)S(1)}, f32[8,2,128,128]{3,2,1,0:T(8,128)S(1)}, f32[2,11,8,128]{3,2,1,0:T(8,128)S(1)}, bf16[2,7,128,256]{3,2,1,0:T(8,128)(2,1)S(1)}, f32[8,128]{1,0:T(8,128)S(1)}) custom-call(bf16[144,512]{1,0:T(8,128)(2,1)S(1)} %collective-permute-done.1.refs_0_, ...), custom_call_target="tpu_custom_call", output_to_operand_aliasing={{0}: (4, {}), {1}: (5, {}), {2}: (6, {}), {3}: (7, {})} | custom-call | flops 500000000 | bytes 1000000 | tf_op jit(solution)/shard_map/spectra/pallas_call | solution.py:529
  19.4 0.1 collective-permute-start.7
  19.5 1.6 %collective-permute-start.8 = (f32[8,128]{1,0:T(8,128)S(1)}, f32[8,128]{1,0:T(8,128)S(1)}, u32[]{:S(2)}, u32[]{:S(2)}) collective-permute-start(f32[8,128]{1,0:T(8,128)S(1)} %get-tuple-element.31.refs_3_), channel_id=1, source_target_pairs={{0,3},{1,2},{4,7},{5,6},{8,11},{9,10},{12,15},{13,14},{16,19},{17,... | collective-permute-start | bytes 12296 | tf_op jit(solution)/shard_map/ppermute | solution.py:544
  21.1 0.0 collective-permute-done.7.refs_4_
  21.1 1.5 %collective-permute-done.8.refs_5_ = f32[8,128]{1,0:T(8,128)S(1)} collective-permute-done((f32[8,128]{1,0:T(8,128)S(1)}, f32[8,128]{1,0:T(8,128)S(1)}, u32[]{:S(2)}, u32[]{:S(2)}) %collective-permute-start.8) | collective-permute-done | bytes 4128 | tf_op jit(solution)/shard_map/ppermute | solution.py:544
  22.6 1.0 %iteration.2.refs_3_ = f32[8,128]{1,0:T(8,128)S(1)} custom-call(bf16[2,7,128,256]{3,2,1,0:T(8,128)(2,1)S(1)} %get-tuple-element.29.refs_0_, f32[2,11,8,128]{3,2,1,0:T(8,128)S(1)} %get-tuple-element.30.refs_1_, bf16[256,256]{1,0:T(8,128)(2,1)S(1)} %copy-done.1, f32[8,128]{1,0:T(8,128)S(1)} %get-tuple-element.31.refs_3_, ...), custom_call_target="tpu_custom_call" | custom-call | tf_op jit(solution)/shard_map/iteration/pallas_call | solution.py:549
  23.6 1.6 %collective-permute-start.10 = (f32[8,128]{1,0:T(8,128)S(1)}, f32[8,128]{1,0:T(8,128)S(1)}, u32[]{:S(2)}, u32[]{:S(2)}) collective-permute-start(f32[8,128]{1,0:T(8,128)S(1)} %iteration.2.refs_3_), channel_id=1, source_target_pairs={{0,3},{1,2},{4,7},{5,6},{8,11},{9,10},{12,15},{13,14},{16,19},{17,... | collective-permute-start | bytes 12296 | tf_op jit(solution)/shard_map/ppermute | solution.py:544
  25.2 0.1 collective-permute-start.9
  25.3 1.4 %collective-permute-done.10.refs_5_ = f32[8,128]{1,0:T(8,128)S(1)} collective-permute-done((f32[8,128]{1,0:T(8,128)S(1)}, f32[8,128]{1,0:T(8,128)S(1)}, u32[]{:S(2)}, u32[]{:S(2)}) %collective-permute-start.10) | collective-permute-done | bytes 4128 | tf_op jit(solution)/shard_map/ppermute | solution.py:544
  26.7 0.0 collective-permute-done.9.refs_4_
  26.7 0.8 %iteration.3.refs_0_ = f32[8,128]{1,0:T(8,128)S(1)} custom-call(bf16[2,7,128,256]{3,2,1,0:T(8,128)(2,1)S(1)} %get-tuple-element.29.refs_0_, f32[2,11,8,128]{3,2,1,0:T(8,128)S(1)} %get-tuple-element.30.refs_1_, bf16[256,256]{1,0:T(8,128)(2,1)S(1)} %copy-done.1, f32[8,128]{1,0:T(8,128)S(1)} %iteration.2.refs_3_, f32[8,128]{1,0:T(8,128)S(1)} %collective-permute-done.9.refs_4_, ...), custom_call_target="tpu_custom_call" | custom-call | tf_op jit(solution)/shard_map/iteration/pallas_call | solution.py:549
  27.5 1.6 %collective-permute-start.12 = (f32[8,128]{1,0:T(8,128)S(1)}, f32[8,128]{1,0:T(8,128)S(1)}, u32[]{:S(2)}, u32[]{:S(2)}) collective-permute-start(f32[8,128]{1,0:T(8,128)S(1)} %iteration.3.refs_0_), channel_id=1, source_target_pairs={{0,3},{1,2},{4,7},{5,6},{8,11},{9,10},{12,15},{13,14},{16,19},{17,... | collective-permute-start | bytes 12296 | tf_op jit(solution)/shard_map/ppermute | solution.py:544
  29.1 0.1 collective-permute-start.11
  29.2 1.4 %collective-permute-done.12.refs_2_ = f32[8,128]{1,0:T(8,128)S(1)} collective-permute-done((f32[8,128]{1,0:T(8,128)S(1)}, f32[8,128]{1,0:T(8,128)S(1)}, u32[]{:S(2)}, u32[]{:S(2)}) %collective-permute-start.12) | collective-permute-done | bytes 4128 | tf_op jit(solution)/shard_map/ppermute | solution.py:544
  30.6 0.4 %collective-permute-start.13 = (f32[8,128]{1,0:T(8,128)S(1)}, f32[8,128]{1,0:T(8,128)S(1)}, u32[]{:S(2)}, u32[]{:S(2)}) collective-permute-start(f32[8,128]{1,0:T(8,128)S(1)} %collective-permute-done.12.refs_2_), channel_id=1, source_target_pairs={{0,2},{4,6},{8,10},{12,14},{16,18},{20,22},{24,26},{28,30},{2,0},{... | collective-permute-start | bytes 12296 | tf_op jit(solution)/shard_map/ppermute | solution.py:472
  31.0 0.0 collective-permute-done.11.refs_1_
  31.0 0.8 %collective-permute-done.13.refs_3_ = f32[8,128]{1,0:T(8,128)S(1)} collective-permute-done((f32[8,128]{1,0:T(8,128)S(1)}, f32[8,128]{1,0:T(8,128)S(1)}, u32[]{:S(2)}, u32[]{:S(2)}) %collective-permute-start.13) | collective-permute-done | bytes 4128 | tf_op jit(solution)/shard_map/ppermute | solution.py:472
  31.8 0.7 %final.1 = (f32[2,1,1,4]{3,2,1,0:T(1,128)}, f32[2,1,1,4]{3,2,1,0:T(1,128)}) custom-call(f32[8,128]{1,0:T(8,128)S(1)} %iteration.3.refs_0_, f32[8,128]{1,0:T(8,128)S(1)} %collective-permute-done.11.refs_1_, f32[8,128]{1,0:T(8,128)S(1)} %collective-permute-done.12.refs_2_, f32[8,128]{1,0:T(8,128)S(1)} %collective-permute-done.13.refs_3_), custom_call_target="tpu_custom_call" | custom-call | tf_op jit(solution)/shard_map/final/pallas_call | solution.py:564
Async XLA Ops:
  1.6 7.7 %collective-permute-start.4 = (bf16[144,512]{1,0:T(8,128)(2,1)S(1)}, bf16[144,512]{1,0:T(8,128)(2,1)S(1)}, u32[]{:S(2)}, u32[]{:S(2)}) collective-permute-start(bf16[144,512]{1,0:T(8,128)(2,1)S(1)} %pack.1.refs_0_), channel_id=1, source_target_pairs={{0,4},{2,6},{8,12},{10,14},{16,20},{18,22},{24,28},{26,30},{4,0},{... | collective-permute-start | bytes 442376 | tf_op jit(solution)/shard_map/ppermute | solution.py:490
  1.9 9.2 %collective-permute-start = (bf16[144,512]{1,0:T(8,128)(2,1)S(1)}, bf16[144,512]{1,0:T(8,128)(2,1)S(1)}, u32[]{:S(2)}, u32[]{:S(2)}) collective-permute-start(bf16[144,512]{1,0:T(8,128)(2,1)S(1)} %pack.1.refs_0_), channel_id=1, source_target_pairs={{4,8},{6,10},{12,16},{14,18},{20,24},{22,26},{8,4},{10,6},{16,12},... | collective-permute-start | bytes 442376 | tf_op jit(solution)/shard_map/ppermute | solution.py:490
  6.0 6.8 %collective-permute-start.2 = (bf16[144,512]{1,0:T(8,128)(2,1)S(1)}, bf16[144,512]{1,0:T(8,128)(2,1)S(1)}, u32[]{:S(2)}, u32[]{:S(2)}) collective-permute-start(bf16[144,512]{1,0:T(8,128)(2,1)S(1)} %pack.1.refs_0_), channel_id=1, source_target_pairs={{2,8},{6,12},{10,16},{14,20},{18,24},{22,28},{8,2},{12,6},{16,10},... | collective-permute-start | bytes 442376 | tf_op jit(solution)/shard_map/ppermute | solution.py:490
  7.9 5.8 %collective-permute-start.6 = (bf16[144,512]{1,0:T(8,128)(2,1)S(1)}, bf16[144,512]{1,0:T(8,128)(2,1)S(1)}, u32[]{:S(2)}, u32[]{:S(2)}) collective-permute-start(bf16[144,512]{1,0:T(8,128)(2,1)S(1)} %pack.1.refs_0_), channel_id=1, source_target_pairs={{0,2},{4,6},{8,10},{12,14},{16,18},{20,22},{24,26},{28,30},{2,0},{... | collective-permute-start | bytes 442376 | tf_op jit(solution)/shard_map/ppermute | solution.py:472
  9.3 7.0 %collective-permute-start.5 = (bf16[144,512]{1,0:T(8,128)(2,1)S(1)}, bf16[144,512]{1,0:T(8,128)(2,1)S(1)}, u32[]{:S(2)}, u32[]{:S(2)}) collective-permute-start(bf16[144,512]{1,0:T(8,128)(2,1)S(1)} %collective-permute-done.4.refs_0_), channel_id=1, source_target_pairs={{0,2},{4,6},{8,10},{12,14},{16,18},{20,22},{24,26},{28,30},{2,0},{... | collective-permute-start | bytes 442376 | tf_op jit(solution)/shard_map/ppermute | solution.py:472
  11.1 6.0 %collective-permute-start.1 = (bf16[144,512]{1,0:T(8,128)(2,1)S(1)}, bf16[144,512]{1,0:T(8,128)(2,1)S(1)}, u32[]{:S(2)}, u32[]{:S(2)}) collective-permute-start(bf16[144,512]{1,0:T(8,128)(2,1)S(1)} %collective-permute-done.refs_1_), channel_id=1, source_target_pairs={{0,2},{4,6},{8,10},{12,14},{16,18},{20,22},{24,26},{28,30},{2,0},{... | collective-permute-start | bytes 442376 | tf_op jit(solution)/shard_map/ppermute | solution.py:472
  12.8 4.3 %collective-permute-start.3 = (bf16[144,512]{1,0:T(8,128)(2,1)S(1)}, bf16[144,512]{1,0:T(8,128)(2,1)S(1)}, u32[]{:S(2)}, u32[]{:S(2)}) collective-permute-start(bf16[144,512]{1,0:T(8,128)(2,1)S(1)} %collective-permute-done.2.refs_2_), channel_id=1, source_target_pairs={{0,2},{4,6},{8,10},{12,14},{16,18},{20,22},{24,26},{28,30},{2,0},{... | collective-permute-start | bytes 442376 | tf_op jit(solution)/shard_map/ppermute | solution.py:472
  13.7 1.0 %copy-start = (bf16[3,256,256]{2,1,0:T(8,128)(2,1)S(1)}, bf16[3,256,256]{2,1,0:T(8,128)(2,1)}, u32[]{:S(2)}) copy-start(bf16[3,256,256]{2,1,0:T(8,128)(2,1)} %constant.4.clone.refs_2_.refs_1_.refs_3_) | copy-start | bytes 1179652
  16.3 0.9 %copy-start.1 = (bf16[256,256]{1,0:T(8,128)(2,1)S(1)}, bf16[256,256]{1,0:T(8,128)(2,1)}, u32[]{:S(2)}) copy-start(bf16[256,256]{1,0:T(8,128)(2,1)} %constant.5.clone.refs_3_.refs_2_) | copy-start | bytes 393220
  19.4 1.7 %collective-permute-start.7 = (f32[8,128]{1,0:T(8,128)S(1)}, f32[8,128]{1,0:T(8,128)S(1)}, u32[]{:S(2)}, u32[]{:S(2)}) collective-permute-start(f32[8,128]{1,0:T(8,128)S(1)} %get-tuple-element.31.refs_3_), channel_id=1, source_target_pairs={{0,2},{4,6},{8,10},{12,14},{16,18},{20,22},{24,26},{28,30},{2,0},{... | collective-permute-start | bytes 12296 | tf_op jit(solution)/shard_map/ppermute | solution.py:472
  19.5 3.1 %collective-permute-start.8 = (f32[8,128]{1,0:T(8,128)S(1)}, f32[8,128]{1,0:T(8,128)S(1)}, u32[]{:S(2)}, u32[]{:S(2)}) collective-permute-start(f32[8,128]{1,0:T(8,128)S(1)} %get-tuple-element.31.refs_3_), channel_id=1, source_target_pairs={{0,3},{1,2},{4,7},{5,6},{8,11},{9,10},{12,15},{13,14},{16,19},{17,... | collective-permute-start | bytes 12296 | tf_op jit(solution)/shard_map/ppermute | solution.py:544
  23.6 3.1 %collective-permute-start.10 = (f32[8,128]{1,0:T(8,128)S(1)}, f32[8,128]{1,0:T(8,128)S(1)}, u32[]{:S(2)}, u32[]{:S(2)}) collective-permute-start(f32[8,128]{1,0:T(8,128)S(1)} %iteration.2.refs_3_), channel_id=1, source_target_pairs={{0,3},{1,2},{4,7},{5,6},{8,11},{9,10},{12,15},{13,14},{16,19},{17,... | collective-permute-start | bytes 12296 | tf_op jit(solution)/shard_map/ppermute | solution.py:544
  25.2 1.5 %collective-permute-start.9 = (f32[8,128]{1,0:T(8,128)S(1)}, f32[8,128]{1,0:T(8,128)S(1)}, u32[]{:S(2)}, u32[]{:S(2)}) collective-permute-start(f32[8,128]{1,0:T(8,128)S(1)} %iteration.2.refs_3_), channel_id=1, source_target_pairs={{0,2},{4,6},{8,10},{12,14},{16,18},{20,22},{24,26},{28,30},{2,0},{... | collective-permute-start | bytes 12296 | tf_op jit(solution)/shard_map/ppermute | solution.py:472
  27.5 3.1 %collective-permute-start.12 = (f32[8,128]{1,0:T(8,128)S(1)}, f32[8,128]{1,0:T(8,128)S(1)}, u32[]{:S(2)}, u32[]{:S(2)}) collective-permute-start(f32[8,128]{1,0:T(8,128)S(1)} %iteration.3.refs_0_), channel_id=1, source_target_pairs={{0,3},{1,2},{4,7},{5,6},{8,11},{9,10},{12,15},{13,14},{16,19},{17,... | collective-permute-start | bytes 12296 | tf_op jit(solution)/shard_map/ppermute | solution.py:544
  29.1 1.9 %collective-permute-start.11 = (f32[8,128]{1,0:T(8,128)S(1)}, f32[8,128]{1,0:T(8,128)S(1)}, u32[]{:S(2)}, u32[]{:S(2)}) collective-permute-start(f32[8,128]{1,0:T(8,128)S(1)} %iteration.3.refs_0_), channel_id=1, source_target_pairs={{0,2},{4,6},{8,10},{12,14},{16,18},{20,22},{24,26},{28,30},{2,0},{... | collective-permute-start | bytes 12296 | tf_op jit(solution)/shard_map/ppermute | solution.py:472
  30.6 1.2 %collective-permute-start.13 = (f32[8,128]{1,0:T(8,128)S(1)}, f32[8,128]{1,0:T(8,128)S(1)}, u32[]{:S(2)}, u32[]{:S(2)}) collective-permute-start(f32[8,128]{1,0:T(8,128)S(1)} %collective-permute-done.12.refs_2_), channel_id=1, source_target_pairs={{0,2},{4,6},{8,10},{12,14},{16,18},{20,22},{24,26},{28,30},{2,0},{... | collective-permute-start | bytes 12296 | tf_op jit(solution)/shard_map/ppermute | solution.py:472

commit v5 on v4

--- a/solution.py
+++ b/solution.py
@@ -14,9 +14,9 @@
 HALO = 3
 WINDOW = 8
 EXTRA = 16
+PARTS = 8
 FIRST_GROUP = 4
 GROUP = 10
-DEPTH = 1
 
 step_size = 0.5
 stiffness = 0.2
@@ -75,6 +75,19 @@
     return wide[:, :PATCH] + wide[:, PATCH:]
 
 
+def side_by_side(left_high, left_low, rights):
+    left = jnp.concatenate([left_high, left_low, left_high], axis=1)
+    results = []
+    for at in range(0, len(rights), 2):
+        columns = []
+        for right in rights[at : at + 2]:
+            high, low = split(right)
+            columns.append(jnp.concatenate([high, high, low], axis=0))
+        wide = dot(left, jnp.concatenate(columns, axis=1))
+        results += [wide[:, k * PATCH : (k + 1) * PATCH] for k in range(len(columns))]
+    return results
+
+
 def lanes(shape):
     return lax.broadcasted_iota(jnp.int32, shape, len(shape) - 1)
 
@@ -89,14 +102,16 @@
 
 def pack_kernel(shift_ref, mask_ref, image_ref, out_ref, shift, mask, sems):
     copies = [
-        pltpu.make_async_copy(image_ref.at[0], out_ref.at[:PATCH], sems.at[0]),
-        pltpu.make_async_copy(shift_ref, shift, sems.at[1]),
-        pltpu.make_async_copy(mask_ref, mask, sems.at[2]),
+        pltpu.make_async_copy(shift_ref, shift, sems.at[0]),
+        pltpu.make_async_copy(mask_ref, mask, sems.at[1]),
     ]
+    for part in range(PARTS):
+        rows = pl.ds(part * (PATCH // PARTS), PATCH // PARTS)
+        copies.append(pltpu.make_async_copy(image_ref.at[0, rows], out_ref.at[rows], sems.at[2 + part]))
     for copy in copies:
         copy.start()
+    copies[0].wait()
     copies[1].wait()
-    copies[2].wait()
     row = lax.broadcasted_iota(jnp.int32, (EXTRA, PATCH), 0)
     for col in range(shift_ref.shape[-1]):
         values = jnp.zeros((EXTRA, PATCH), f32)
@@ -110,32 +125,38 @@
                 values = jnp.where(row == 3 * dim + at, part, values)
             values = jnp.where(row == 6 + dim, allowed, values)
         out_ref[PATCH:, col * PATCH : (col + 1) * PATCH] = values.astype(bf16)
-    copies[0].wait()
+    for copy in copies[2:]:
+        copy.wait()
 
 
 def forward_patches(patches, basis, down, mean_row):
     count = len(patches)
     rows = fold(dot(jnp.concatenate(patches, axis=0), basis))
     lane = lanes((1, PATCH))
-    sign = alternating((WINDOW, PATCH), 0)
+    first_row = lax.broadcasted_iota(jnp.int32, (WINDOW, PATCH), 0) == 0
     sigma = jnp.where(lane > HALF, 1.0, -1.0) * jnp.where(lane % HALF == 0, 0.0, 1.0)
-    centred, nyquist_rows, pairs = [], [], []
+    pairs = []
     for k in range(count):
         row = rows[k * PATCH : (k + 1) * PATCH]
         part = jnp.sum(row.reshape(PATCH // WINDOW, WINDOW, PATCH), axis=0)
         whole = jnp.sum(part, axis=0, keepdims=True)
         row = row - (whole[:, :1] * (1.0 / (PATCH * PATCH))) * mean_row
-        nyquist_rows.append(jnp.sum(part * sign, axis=0, keepdims=True))
         pair = jnp.concatenate(split(row), axis=1)
-        centred.append(row)
         pairs.append(jnp.concatenate([pair, pair], axis=0))
     both = [fold(dot(down, pair)) for pair in pairs]
     result = []
-    for row, nyquist_row, wide in zip(centred, nyquist_rows, both):
+    for wide in both:
         first, second = wide[:PATCH], wide[PATCH:]
         real = first + sigma * pltpu.roll(second, HALF, 1)
         imag = second - sigma * pltpu.roll(first, HALF, 1)
-        result.append((real, imag, jnp.sum(row * row, axis=0, keepdims=True), nyquist_row))
+        squares = (real * real + imag * imag).reshape(PATCH // WINDOW, WINDOW, PATCH)
+        at = HALF // WINDOW
+        energy = jnp.where(first_row, 0.0, squares[at])
+        for k in range(PATCH // WINDOW):
+            if k != at:
+                energy = energy + squares[k]
+        energy = jnp.sum(energy, axis=0, keepdims=True)
+        result.append((real, imag, energy, real[HALF : HALF + 1], imag[HALF : HALF + 1]))
     return result
 
 
@@ -170,55 +191,50 @@
     starts = [pl.multiple_of((half * cols + col) * PATCH, PATCH) for col in range(cols)]
     patches = [block[:PATCH, pl.ds(starts[col], PATCH)] for block, slot, col in places]
     results = forward_patches(patches, basis, down_ref[...], mean_row)
-    for (block, slot, col), (real, imag, energy_row, nyquist_row) in zip(places, results):
+    corner = (lax.broadcasted_iota(jnp.int32, (WINDOW, PATCH), 0) == 0) & (lanes((WINDOW, PATCH)) == HALF)
+    for (block, slot, col), (real, imag, energy_row, nyquist_real, nyquist_imag) in zip(places, results):
         real_ref[slot, col] = real
         imag_ref[slot, col] = imag
+        band = slice(HALF, HALF + WINDOW)
+        real_ref[slot, col, band, :] = jnp.where(corner, 0.0, real[band])
+        imag_ref[slot, col, band, :] = jnp.where(corner, 0.0, imag[band])
         row_ref[col, 0, pl.ds(slot, 1), :] = energy_row
-        row_ref[col, 1, pl.ds(slot, 1), :] = nyquist_row
+        row_ref[col, 1, pl.ds(slot, 1), :] = nyquist_real
+        row_ref[col, 11, pl.ds(slot, 1), :] = nyquist_imag
         small = block[PATCH:, pl.ds(starts[col], PATCH)].astype(f32)
         for dim in range(2):
             shift = small[3 * dim : 3 * dim + 1] + small[3 * dim + 1 : 3 * dim + 2] + small[3 * dim + 2 : 3 * dim + 3]
             row_ref[col, 2 + dim, pl.ds(slot, 1), :] = shift
             row_ref[col, 4 + dim, pl.ds(slot, 1), :] = small[6 + dim : 7 + dim]
     low_lane = lanes((1, PATCH)) <= HALF
-    products = []
-
-    def finish(k):
-        wide = fold(dot(up_ref[...], products[k]))
-        base_ref[k % cols, pairs[k // cols]] = jnp.concatenate(split(wide[:PATCH] + wide[PATCH:]), axis=1)
-
-    for pair in pairs:
-        for col in range(cols):
+    tasks = [(pair, col) for pair in pairs for col in range(cols)]
+    for at in range(0, len(tasks), 2):
+        products = []
+        for pair, col in tasks[at : at + 2]:
             sr, si = real_ref[pair, col], imag_ref[pair, col]
             nr, ni = real_ref[pair + 1, col], imag_ref[pair + 1, col]
             same = sr * nr + si * ni
             cross = si * nr - sr * ni
-            top = jnp.concatenate(split(jnp.where(low_lane, same, cross)), axis=1)
-            bottom = jnp.concatenate(split(jnp.where(low_lane, cross, -same)), axis=1)
-            products.append(jnp.concatenate([top, bottom], axis=0))
-            if len(products) > DEPTH:
-                finish(len(products) - 1 - DEPTH)
-    for k in range(max(len(products) - DEPTH, 0), len(products)):
-        finish(k)
+            products.append(
+                jnp.concatenate([jnp.where(low_lane, same, cross), jnp.where(low_lane, cross, -same)], axis=0)
+            )
+        for (pair, col), base in zip(tasks[at : at + 2], side_by_side(up_ref[:PATCH], up_ref[PATCH:], products)):
+            base_ref[col, pair] = jnp.concatenate(split(base), axis=1)
 
 
 def energies(row_ref, col):
     lane = lanes((WINDOW, PATCH))
-    weight = jnp.where(lane % HALF == 0, 1.0, 2.0)
+    weight = jnp.where(lane == 0, 1.0, jnp.where(lane < HALF, 2.0, 0.0))
     at_nyquist = jnp.where(lane == HALF, 1.0, 0.0)
     area = float(PATCH * PATCH)
 
     def spread(values):
         return jnp.broadcast_to(jnp.sum(values, axis=1, keepdims=True), (WINDOW, PATCH))
 
-    energy, nyquist = row_ref[col, 0], row_ref[col, 1]
-    corner = spread(nyquist * at_nyquist)
-    corner_energy = corner * corner / area
-    row_energy = spread(weight * (1.0 - at_nyquist) * nyquist * nyquist) / area
-    col_energy = jnp.maximum(spread(energy * at_nyquist) / PATCH - corner_energy, 0.0)
-    whole = spread(weight * energy) / PATCH
-    bulk = jnp.maximum(whole - row_energy - col_energy - corner_energy, 0.0)
-    return bulk, row_energy, col_energy, corner_energy, corner
+    energy, real, imag = row_ref[col, 0], row_ref[col, 1], row_ref[col, 11]
+    corner = spread(real * at_nyquist)
+    row_energy = spread(weight * (real * real + imag * imag)) / area
+    return spread(weight * energy) / area, row_energy, spread(energy * at_nyquist) / area, corner * corner / area, corner
 
 
 def sine_cosine(z):
@@ -331,7 +347,7 @@
         gamma_x = cos_x * next_section(cos_x)
         gamma = cos_both * next_section(cos_both)
         corner = nyquist * next_section(nyquist) * (1.0 / (PATCH * PATCH))
-        ripple.append((gamma - gamma_y * gamma_x) * corner * scale)
+        ripple.append(gamma * corner * scale)
         rows.append(shift_row(dy - next_section(dy), gamma_y, lane))
         cosine, sine = cos_sin_turns((dx - next_section(dx)) * frequency)
         turn_cos.append(jnp.where(nyquist_lane, gamma_x, cosine) * scale)
@@ -479,7 +495,7 @@
         scratch_shapes=[
             pltpu.SMEM(displacement.shape, f32),
             pltpu.SMEM(fold_mask.shape, jnp.int32),
-            pltpu.SemaphoreType.DMA((3,)),
+            pltpu.SemaphoreType.DMA((2 + PARTS,)),
         ],
         compiler_params=limit(4),
         cost_estimate=pl.CostEstimate(flops=0, bytes_accessed=8000000, transcendentals=0),
@@ -504,7 +520,7 @@
     state_shapes = [
         jax.ShapeDtypeStruct((WINDOW, cols, PATCH, PATCH), f32),
         jax.ShapeDtypeStruct((WINDOW, cols, PATCH, PATCH), f32),
-        jax.ShapeDtypeStruct((cols, 11, WINDOW, PATCH), f32),
+        jax.ShapeDtypeStruct((cols, 12, WINDOW, PATCH), f32),
         jax.ShapeDtypeStruct((cols, WINDOW - 1, PATCH, 2 * PATCH), bf16),
     ]
     message_shape = jax.ShapeDtypeStruct((WINDOW, PATCH), f32)

time: 32.7 us -> 32.8 us (level)
  the two profiles are of different devices: /device:TPU:21 before, /device:TPU:15 now
where the time goes in v5:
time: 32.8 us; the launch traced here: 32.6 us
  starting transfers between devices  12.4 us (38%)
  waiting for transfers between devices  10.4 us (32%)
  Pallas kernels  7.99 us (24%)
  local copies, waits for them, and re-layouts  1.1 us (3%)
  between operations  0.75 us (2%)
    ppermute x3, starting transfers between devices, per_device(): blocks[source, 0] = lax.ppermute(payload, 'sec', perm)  8.77 us
    ppermute x3, waiting for transfers between devices, diagonal(): return lax.ppermute(x, ('sec', 'row'), pairs)  6.76 us
    pallas_call x4, Pallas kernels, per_device(): pl.pallas_call(stage_kernel, out_shape=state_shapes + [message_shape] * l...  4.62 us
    ppermute x3, waiting for transfers between devices, per_device(): blocks[source, 0] = lax.ppermute(payload, 'sec', perm)  2.26 us
    ppermute x8, starting transfers between devices, between_cores(): return lax.ppermute(x, 'sec', cores)  1.89 us
    pallas_call x2, Pallas kernels, per_device(): pl.pallas_call(lambda *refs, step=step: iteration_kernel(cols, step, WIND...  1.78 us
    ppermute x3, starting transfers between devices, diagonal(): return lax.ppermute(x, ('sec', 'row'), pairs)  1.72 us
    ppermute x8, waiting for transfers between devices, between_cores(): return lax.ppermute(x, 'sec', cores)  1.36 us
  transfers between devices with their start and end apart: 14, of which 6 were waited for; matrix products, arithmetic and copies ran while one was open for 0% of the time, Pallas kernels for 7%

profile of v5, /device:TPU:15, one launch (start us, length us, event | category | flops | bytes accessed | tf_op | source)
XLA Modules:
  0.0 32.6 jit_solution(3815007506837196698)
XLA Ops:
  0.6 0.9 %pack.1.refs_0_ = bf16[144,512]{1,0:T(8,128)(2,1)S(1)} custom-call(f32[2,1,1,4]{3,2,1,0:T(1,128)} %shift_ref.1, s32[2,1,1,4]{3,2,1,0:T(1,128)} %mask_ref.1, bf16[1,128,512]{2,1,0:T(8,128)(2,1)} %image_ref.1), custom_call_target="tpu_custom_call" | custom-call | bytes 8000000 | tf_op jit(solution)/shard_map/pack/pallas_call | solution.py:490
  1.6 0.3 collective-permute-start.4
  1.9 4.1 %collective-permute-start = (bf16[144,512]{1,0:T(8,128)(2,1)S(1)}, bf16[144,512]{1,0:T(8,128)(2,1)S(1)}, u32[]{:S(2)}, u32[]{:S(2)}) collective-permute-start(bf16[144,512]{1,0:T(8,128)(2,1)S(1)} %pack.1.refs_0_), channel_id=1, source_target_pairs={{4,8},{6,10},{12,16},{14,18},{20,24},{22,26},{8,4},{10,6},{16,12},... | collective-permute-start | bytes 442376 | tf_op jit(solution)/shard_map/ppermute | solution.py:506
  6.0 4.3 %collective-permute-start.2 = (bf16[144,512]{1,0:T(8,128)(2,1)S(1)}, bf16[144,512]{1,0:T(8,128)(2,1)S(1)}, u32[]{:S(2)}, u32[]{:S(2)}) collective-permute-start(bf16[144,512]{1,0:T(8,128)(2,1)S(1)} %pack.1.refs_0_), channel_id=1, source_target_pairs={{2,8},{6,12},{10,16},{14,20},{18,24},{22,28},{8,2},{12,6},{16,10},... | collective-permute-start | bytes 442376 | tf_op jit(solution)/shard_map/ppermute | solution.py:506
  10.3 0.1 collective-permute-start.6
  10.4 0.0 collective-permute-done.4.refs_0_
  10.4 0.6 %collective-permute-start.5 = (bf16[144,512]{1,0:T(8,128)(2,1)S(1)}, bf16[144,512]{1,0:T(8,128)(2,1)S(1)}, u32[]{:S(2)}, u32[]{:S(2)}) collective-permute-start(bf16[144,512]{1,0:T(8,128)(2,1)S(1)} %collective-permute-done.4.refs_0_), channel_id=1, source_target_pairs={{0,2},{4,6},{8,10},{12,14},{16,18},{20,22},{24,26},{28,30},{2,0},{... | collective-permute-start | bytes 442376 | tf_op jit(solution)/shard_map/ppermute | solution.py:488
  11.1 0.0 collective-permute-done.refs_1_
  11.1 0.0 collective-permute-start.1
  11.1 2.3 %collective-permute-done.2.refs_2_ = bf16[144,512]{1,0:T(8,128)(2,1)S(1)} collective-permute-done((bf16[144,512]{1,0:T(8,128)(2,1)S(1)}, bf16[144,512]{1,0:T(8,128)(2,1)S(1)}, u32[]{:S(2)}, u32[]{:S(2)}) %collective-permute-start.2) | collective-permute-done | bytes 147488 | tf_op jit(solution)/shard_map/ppermute | solution.py:506
  13.3 0.4 %collective-permute-start.3 = (bf16[144,512]{1,0:T(8,128)(2,1)S(1)}, bf16[144,512]{1,0:T(8,128)(2,1)S(1)}, u32[]{:S(2)}, u32[]{:S(2)}) collective-permute-start(bf16[144,512]{1,0:T(8,128)(2,1)S(1)} %collective-permute-done.2.refs_2_), channel_id=1, source_target_pairs={{0,2},{4,6},{8,10},{12,14},{16,18},{20,22},{24,26},{28,30},{2,0},{... | collective-permute-start | bytes 442376 | tf_op jit(solution)/shard_map/ppermute | solution.py:488
  13.7 0.0 collective-permute-done.6.refs_1_
  13.7 0.0 copy-start
  13.7 1.0 %copy-done = bf16[3,256,256]{2,1,0:T(8,128)(2,1)S(1)} copy-done((bf16[3,256,256]{2,1,0:T(8,128)(2,1)S(1)}, bf16[3,256,256]{2,1,0:T(8,128)(2,1)}, u32[]{:S(2)}) %copy-start) | copy-done | bytes 393240
  14.7 1.0 %spectra.4 = (f32[8,2,128,128]{3,2,1,0:T(8,128)S(1)}, f32[8,2,128,128]{3,2,1,0:T(8,128)S(1)}, f32[2,12,8,128]{3,2,1,0:T(8,128)S(1)}, bf16[2,7,128,256]{3,2,1,0:T(8,128)(2,1)S(1)}) custom-call(bf16[144,512]{1,0:T(8,128)(2,1)S(1)} %pack.1.refs_0_, bf16[144,512]{1,0:T(8,128)(2,1)S(1)} %collective-permute-done.6.refs_1_, bf16[3,256,256]{2,1,0:T(8,128)(2,1)S(1)} %copy-done), custom_call_target="tpu_custom_call" | custom-call | flops 500000000 | bytes 1000000 | tf_op jit(solution)/shard_map/spectra/pallas_call | solution.py:545
  15.7 0.6 %spectra.5 = (f32[8,2,128,128]{3,2,1,0:T(8,128)S(1)}, f32[8,2,128,128]{3,2,1,0:T(8,128)S(1)}, f32[2,12,8,128]{3,2,1,0:T(8,128)S(1)}, bf16[2,7,128,256]{3,2,1,0:T(8,128)(2,1)S(1)}) custom-call(bf16[144,512]{1,0:T(8,128)(2,1)S(1)} %collective-permute-done.4.refs_0_, ...), custom_call_target="tpu_custom_call", output_to_operand_aliasing={{0}: (2, {}), {1}: (3, {}), {2}: (4, {}), {3}: (5, {})} | custom-call | flops 500000000 | bytes 1000000 | tf_op jit(solution)/shard_map/spectra/pallas_call | solution.py:545
  16.3 0.0 collective-permute-done.5.refs_0_
  16.3 0.0 copy-start.1
  16.3 0.8 %spectra.6 = (f32[8,2,128,128]{3,2,1,0:T(8,128)S(1)}, f32[8,2,128,128]{3,2,1,0:T(8,128)S(1)}, f32[2,12,8,128]{3,2,1,0:T(8,128)S(1)}, bf16[2,7,128,256]{3,2,1,0:T(8,128)(2,1)S(1)}) custom-call(bf16[144,512]{1,0:T(8,128)(2,1)S(1)} %collective-permute-done.5.refs_0_, ...), custom_call_target="tpu_custom_call", output_to_operand_aliasing={{0}: (4, {}), {1}: (5, {}), {2}: (6, {}), {3}: (7, {})} | custom-call | flops 500000000 | bytes 1000000 | tf_op jit(solution)/shard_map/spectra/pallas_call | solution.py:545
  17.1 0.0 collective-permute-done.1.refs_0_
  17.1 0.0 collective-permute-done.3.refs_1_
  17.1 0.1 copy-done.1
  17.2 2.3 %spectra.7 = (f32[8,2,128,128]{3,2,1,0:T(8,128)S(1)}, f32[8,2,128,128]{3,2,1,0:T(8,128)S(1)}, f32[2,12,8,128]{3,2,1,0:T(8,128)S(1)}, bf16[2,7,128,256]{3,2,1,0:T(8,128)(2,1)S(1)}, f32[8,128]{1,0:T(8,128)S(1)}) custom-call(bf16[144,512]{1,0:T(8,128)(2,1)S(1)} %collective-permute-done.1.refs_0_, ...), custom_call_target="tpu_custom_call", output_to_operand_aliasing={{0}: (4, {}), {1}: (5, {}), {2}: (6, {}), {3}: (7, {})} | custom-call | flops 500000000 | bytes 1000000 | tf_op jit(solution)/shard_map/spectra/pallas_call | solution.py:545
  19.5 0.2 collective-permute-start.7
  19.7 0.5 %collective-permute-start.8 = (f32[8,128]{1,0:T(8,128)S(1)}, f32[8,128]{1,0:T(8,128)S(1)}, u32[]{:S(2)}, u32[]{:S(2)}) collective-permute-start(f32[8,128]{1,0:T(8,128)S(1)} %get-tuple-element.31.refs_3_), channel_id=1, source_target_pairs={{0,3},{1,2},{4,7},{5,6},{8,11},{9,10},{12,15},{13,14},{16,19},{17,... | collective-permute-start | bytes 12296 | tf_op jit(solution)/shard_map/ppermute | solution.py:560
  20.2 0.5 %collective-permute-done.7.refs_4_ = f32[8,128]{1,0:T(8,128)S(1)} collective-permute-done((f32[8,128]{1,0:T(8,128)S(1)}, f32[8,128]{1,0:T(8,128)S(1)}, u32[]{:S(2)}, u32[]{:S(2)}) %collective-permute-start.7) | collective-permute-done | bytes 4128 | tf_op jit(solution)/shard_map/ppermute | solution.py:488
  20.7 2.0 %collective-permute-done.8.refs_5_ = f32[8,128]{1,0:T(8,128)S(1)} collective-permute-done((f32[8,128]{1,0:T(8,128)S(1)}, f32[8,128]{1,0:T(8,128)S(1)}, u32[]{:S(2)}, u32[]{:S(2)}) %collective-permute-start.8) | collective-permute-done | bytes 4128 | tf_op jit(solution)/shard_map/ppermute | solution.py:560
  22.7 1.0 %iteration.2.refs_3_ = f32[8,128]{1,0:T(8,128)S(1)} custom-call(bf16[2,7,128,256]{3,2,1,0:T(8,128)(2,1)S(1)} %get-tuple-element.29.refs_0_, f32[2,12,8,128]{3,2,1,0:T(8,128)S(1)} %get-tuple-element.30.refs_1_, bf16[256,256]{1,0:T(8,128)(2,1)S(1)} %copy-done.1, f32[8,128]{1,0:T(8,128)S(1)} %get-tuple-element.31.refs_3_, ...), custom_call_target="tpu_custom_call" | custom-call | tf_op jit(solution)/shard_map/iteration/pallas_call | solution.py:565
  23.7 0.6 %collective-permute-start.10 = (f32[8,128]{1,0:T(8,128)S(1)}, f32[8,128]{1,0:T(8,128)S(1)}, u32[]{:S(2)}, u32[]{:S(2)}) collective-permute-start(f32[8,128]{1,0:T(8,128)S(1)} %iteration.2.refs_3_), channel_id=1, source_target_pairs={{0,3},{1,2},{4,7},{5,6},{8,11},{9,10},{12,15},{13,14},{16,19},{17,... | collective-permute-start | bytes 12296 | tf_op jit(solution)/shard_map/ppermute | solution.py:560
  24.3 0.1 collective-permute-start.9
  24.4 2.4 %collective-permute-done.10.refs_5_ = f32[8,128]{1,0:T(8,128)S(1)} collective-permute-done((f32[8,128]{1,0:T(8,128)S(1)}, f32[8,128]{1,0:T(8,128)S(1)}, u32[]{:S(2)}, u32[]{:S(2)}) %collective-permute-start.10) | collective-permute-done | bytes 4128 | tf_op jit(solution)/shard_map/ppermute | solution.py:560
  26.8 0.0 collective-permute-done.9.refs_4_
  26.8 0.8 %iteration.3.refs_0_ = f32[8,128]{1,0:T(8,128)S(1)} custom-call(bf16[2,7,128,256]{3,2,1,0:T(8,128)(2,1)S(1)} %get-tuple-element.29.refs_0_, f32[2,12,8,128]{3,2,1,0:T(8,128)S(1)} %get-tuple-element.30.refs_1_, bf16[256,256]{1,0:T(8,128)(2,1)S(1)} %copy-done.1, f32[8,128]{1,0:T(8,128)S(1)} %iteration.2.refs_3_, f32[8,128]{1,0:T(8,128)S(1)} %collective-permute-done.9.refs_4_, ...), custom_call_target="tpu_custom_call" | custom-call | tf_op jit(solution)/shard_map/iteration/pallas_call | solution.py:565
  27.6 0.6 %collective-permute-start.12 = (f32[8,128]{1,0:T(8,128)S(1)}, f32[8,128]{1,0:T(8,128)S(1)}, u32[]{:S(2)}, u32[]{:S(2)}) collective-permute-start(f32[8,128]{1,0:T(8,128)S(1)} %iteration.3.refs_0_), channel_id=1, source_target_pairs={{0,3},{1,2},{4,7},{5,6},{8,11},{9,10},{12,15},{13,14},{16,19},{17,... | collective-permute-start | bytes 12296 | tf_op jit(solution)/shard_map/ppermute | solution.py:560
  28.2 0.1 collective-permute-start.11
  28.3 2.4 %collective-permute-done.12.refs_2_ = f32[8,128]{1,0:T(8,128)S(1)} collective-permute-done((f32[8,128]{1,0:T(8,128)S(1)}, f32[8,128]{1,0:T(8,128)S(1)}, u32[]{:S(2)}, u32[]{:S(2)}) %collective-permute-start.12) | collective-permute-done | bytes 4128 | tf_op jit(solution)/shard_map/ppermute | solution.py:560
  30.7 0.4 %collective-permute-start.13 = (f32[8,128]{1,0:T(8,128)S(1)}, f32[8,128]{1,0:T(8,128)S(1)}, u32[]{:S(2)}, u32[]{:S(2)}) collective-permute-start(f32[8,128]{1,0:T(8,128)S(1)} %collective-permute-done.12.refs_2_), channel_id=1, source_target_pairs={{0,2},{4,6},{8,10},{12,14},{16,18},{20,22},{24,26},{28,30},{2,0},{... | collective-permute-start | bytes 12296 | tf_op jit(solution)/shard_map/ppermute | solution.py:488
  31.1 0.0 collective-permute-done.11.refs_1_
  31.1 0.8 %collective-permute-done.13.refs_3_ = f32[8,128]{1,0:T(8,128)S(1)} collective-permute-done((f32[8,128]{1,0:T(8,128)S(1)}, f32[8,128]{1,0:T(8,128)S(1)}, u32[]{:S(2)}, u32[]{:S(2)}) %collective-permute-start.13) | collective-permute-done | bytes 4128 | tf_op jit(solution)/shard_map/ppermute | solution.py:488
  31.9 0.7 %final.1 = (f32[2,1,1,4]{3,2,1,0:T(1,128)}, f32[2,1,1,4]{3,2,1,0:T(1,128)}) custom-call(f32[8,128]{1,0:T(8,128)S(1)} %iteration.3.refs_0_, f32[8,128]{1,0:T(8,128)S(1)} %collective-permute-done.11.refs_1_, f32[8,128]{1,0:T(8,128)S(1)} %collective-permute-done.12.refs_2_, f32[8,128]{1,0:T(8,128)S(1)} %collective-permute-done.13.refs_3_), custom_call_target="tpu_custom_call" | custom-call | tf_op jit(solution)/shard_map/final/pallas_call | solution.py:580
Async XLA Ops:
  1.6 8.9 %collective-permute-start.4 = (bf16[144,512]{1,0:T(8,128)(2,1)S(1)}, bf16[144,512]{1,0:T(8,128)(2,1)S(1)}, u32[]{:S(2)}, u32[]{:S(2)}) collective-permute-start(bf16[144,512]{1,0:T(8,128)(2,1)S(1)} %pack.1.refs_0_), channel_id=1, source_target_pairs={{0,4},{2,6},{8,12},{10,14},{16,20},{18,22},{24,28},{26,30},{4,0},{... | collective-permute-start | bytes 442376 | tf_op jit(solution)/shard_map/ppermute | solution.py:506
  1.9 9.2 %collective-permute-start = (bf16[144,512]{1,0:T(8,128)(2,1)S(1)}, bf16[144,512]{1,0:T(8,128)(2,1)S(1)}, u32[]{:S(2)}, u32[]{:S(2)}) collective-permute-start(bf16[144,512]{1,0:T(8,128)(2,1)S(1)} %pack.1.refs_0_), channel_id=1, source_target_pairs={{4,8},{6,10},{12,16},{14,18},{20,24},{22,26},{8,4},{10,6},{16,12},... | collective-permute-start | bytes 442376 | tf_op jit(solution)/shard_map/ppermute | solution.py:506
  6.0 7.3 %collective-permute-start.2 = (bf16[144,512]{1,0:T(8,128)(2,1)S(1)}, bf16[144,512]{1,0:T(8,128)(2,1)S(1)}, u32[]{:S(2)}, u32[]{:S(2)}) collective-permute-start(bf16[144,512]{1,0:T(8,128)(2,1)S(1)} %pack.1.refs_0_), channel_id=1, source_target_pairs={{2,8},{6,12},{10,16},{14,20},{18,24},{22,28},{8,2},{12,6},{16,10},... | collective-permute-start | bytes 442376 | tf_op jit(solution)/shard_map/ppermute | solution.py:506
  10.3 3.4 %collective-permute-start.6 = (bf16[144,512]{1,0:T(8,128)(2,1)S(1)}, bf16[144,512]{1,0:T(8,128)(2,1)S(1)}, u32[]{:S(2)}, u32[]{:S(2)}) collective-permute-start(bf16[144,512]{1,0:T(8,128)(2,1)S(1)} %pack.1.refs_0_), channel_id=1, source_target_pairs={{0,2},{4,6},{8,10},{12,14},{16,18},{20,22},{24,26},{28,30},{2,0},{... | collective-permute-start | bytes 442376 | tf_op jit(solution)/shard_map/ppermute | solution.py:488
  10.4 5.9 %collective-permute-start.5 = (bf16[144,512]{1,0:T(8,128)(2,1)S(1)}, bf16[144,512]{1,0:T(8,128)(2,1)S(1)}, u32[]{:S(2)}, u32[]{:S(2)}) collective-permute-start(bf16[144,512]{1,0:T(8,128)(2,1)S(1)} %collective-permute-done.4.refs_0_), channel_id=1, source_target_pairs={{0,2},{4,6},{8,10},{12,14},{16,18},{20,22},{24,26},{28,30},{2,0},{... | collective-permute-start | bytes 442376 | tf_op jit(solution)/shard_map/ppermute | solution.py:488
  11.1 6.1 %collective-permute-start.1 = (bf16[144,512]{1,0:T(8,128)(2,1)S(1)}, bf16[144,512]{1,0:T(8,128)(2,1)S(1)}, u32[]{:S(2)}, u32[]{:S(2)}) collective-permute-start(bf16[144,512]{1,0:T(8,128)(2,1)S(1)} %collective-permute-done.refs_1_), channel_id=1, source_target_pairs={{0,2},{4,6},{8,10},{12,14},{16,18},{20,22},{24,26},{28,30},{2,0},{... | collective-permute-start | bytes 442376 | tf_op jit(solution)/shard_map/ppermute | solution.py:488
  13.3 3.8 %collective-permute-start.3 = (bf16[144,512]{1,0:T(8,128)(2,1)S(1)}, bf16[144,512]{1,0:T(8,128)(2,1)S(1)}, u32[]{:S(2)}, u32[]{:S(2)}) collective-permute-start(bf16[144,512]{1,0:T(8,128)(2,1)S(1)} %collective-permute-done.2.refs_2_), channel_id=1, source_target_pairs={{0,2},{4,6},{8,10},{12,14},{16,18},{20,22},{24,26},{28,30},{2,0},{... | collective-permute-start | bytes 442376 | tf_op jit(solution)/shard_map/ppermute | solution.py:488
  13.7 1.0 %copy-start = (bf16[3,256,256]{2,1,0:T(8,128)(2,1)S(1)}, bf16[3,256,256]{2,1,0:T(8,128)(2,1)}, u32[]{:S(2)}) copy-start(bf16[3,256,256]{2,1,0:T(8,128)(2,1)} %constant.4.clone.refs_2_.refs_1_.refs_3_) | copy-start | bytes 1179652
  16.3 0.9 %copy-start.1 = (bf16[256,256]{1,0:T(8,128)(2,1)S(1)}, bf16[256,256]{1,0:T(8,128)(2,1)}, u32[]{:S(2)}) copy-start(bf16[256,256]{1,0:T(8,128)(2,1)} %constant.5.clone.refs_3_.refs_2_) | copy-start | bytes 393220
  19.5 1.2 %collective-permute-start.7 = (f32[8,128]{1,0:T(8,128)S(1)}, f32[8,128]{1,0:T(8,128)S(1)}, u32[]{:S(2)}, u32[]{:S(2)}) collective-permute-start(f32[8,128]{1,0:T(8,128)S(1)} %get-tuple-element.31.refs_3_), channel_id=1, source_target_pairs={{0,2},{4,6},{8,10},{12,14},{16,18},{20,22},{24,26},{28,30},{2,0},{... | collective-permute-start | bytes 12296 | tf_op jit(solution)/shard_map/ppermute | solution.py:488
  19.7 3.0 %collective-permute-start.8 = (f32[8,128]{1,0:T(8,128)S(1)}, f32[8,128]{1,0:T(8,128)S(1)}, u32[]{:S(2)}, u32[]{:S(2)}) collective-permute-start(f32[8,128]{1,0:T(8,128)S(1)} %get-tuple-element.31.refs_3_), channel_id=1, source_target_pairs={{0,3},{1,2},{4,7},{5,6},{8,11},{9,10},{12,15},{13,14},{16,19},{17,... | collective-permute-start | bytes 12296 | tf_op jit(solution)/shard_map/ppermute | solution.py:560
  23.7 3.1 %collective-permute-start.10 = (f32[8,128]{1,0:T(8,128)S(1)}, f32[8,128]{1,0:T(8,128)S(1)}, u32[]{:S(2)}, u32[]{:S(2)}) collective-permute-start(f32[8,128]{1,0:T(8,128)S(1)} %iteration.2.refs_3_), channel_id=1, source_target_pairs={{0,3},{1,2},{4,7},{5,6},{8,11},{9,10},{12,15},{13,14},{16,19},{17,... | collective-permute-start | bytes 12296 | tf_op jit(solution)/shard_map/ppermute | solution.py:560
  24.3 2.5 %collective-permute-start.9 = (f32[8,128]{1,0:T(8,128)S(1)}, f32[8,128]{1,0:T(8,128)S(1)}, u32[]{:S(2)}, u32[]{:S(2)}) collective-permute-start(f32[8,128]{1,0:T(8,128)S(1)} %iteration.2.refs_3_), channel_id=1, source_target_pairs={{0,2},{4,6},{8,10},{12,14},{16,18},{20,22},{24,26},{28,30},{2,0},{... | collective-permute-start | bytes 12296 | tf_op jit(solution)/shard_map/ppermute | solution.py:488
  27.6 3.1 %collective-permute-start.12 = (f32[8,128]{1,0:T(8,128)S(1)}, f32[8,128]{1,0:T(8,128)S(1)}, u32[]{:S(2)}, u32[]{:S(2)}) collective-permute-start(f32[8,128]{1,0:T(8,128)S(1)} %iteration.3.refs_0_), channel_id=1, source_target_pairs={{0,3},{1,2},{4,7},{5,6},{8,11},{9,10},{12,15},{13,14},{16,19},{17,... | collective-permute-start | bytes 12296 | tf_op jit(solution)/shard_map/ppermute | solution.py:560
  28.2 2.9 %collective-permute-start.11 = (f32[8,128]{1,0:T(8,128)S(1)}, f32[8,128]{1,0:T(8,128)S(1)}, u32[]{:S(2)}, u32[]{:S(2)}) collective-permute-start(f32[8,128]{1,0:T(8,128)S(1)} %iteration.3.refs_0_), channel_id=1, source_target_pairs={{0,2},{4,6},{8,10},{12,14},{16,18},{20,22},{24,26},{28,30},{2,0},{... | collective-permute-start | bytes 12296 | tf_op jit(solution)/shard_map/ppermute | solution.py:488
  30.7 1.2 %collective-permute-start.13 = (f32[8,128]{1,0:T(8,128)S(1)}, f32[8,128]{1,0:T(8,128)S(1)}, u32[]{:S(2)}, u32[]{:S(2)}) collective-permute-start(f32[8,128]{1,0:T(8,128)S(1)} %collective-permute-done.12.refs_2_), channel_id=1, source_target_pairs={{0,2},{4,6},{8,10},{12,14},{16,18},{20,22},{24,26},{28,30},{2,0},{... | collective-permute-start | bytes 12296 | tf_op jit(solution)/shard_map/ppermute | solution.py:488
